TPU v7x, 128 devices: a whole 4x4x4 slice. The times are simulated.
128 devices in a mesh: tile: 16 (over x, y), phi: 8 (over z, core).
Axes of the slice: x: 4, y: 4, z: 4, core: 2. Of those that a mesh axis runs over, the one named last changes fastest.
Arguments:
- blocks: bfloat16 [4096, 5, 64, 256], P(('tile', 'phi')), may hold values from -6 to 6
- levels: int32 [4096], P(('tile', 'phi')), may hold values from 0 to 3
- block_dest: int32 [4096], P(('tile', 'phi')), may hold values from 0 to 15, as said below
- block_phi: int32 [4096], P(('tile', 'phi')), may hold values from 0 to 3, as said below
- block_group: int32 [4096], P(('tile', 'phi')), may hold values from 0 to 7, as said below
Outputs:
- spectra: float32 [5, 128, 256, 2048], P(None, 'tile', 'phi')
Inputs may be any that keep to these rules, and one draw needn't show every extreme that they name: `block_dest`: at most 4 of one device's blocks name one tile, and some device sends exactly 4 to some tile; for each tile and each phi segment, the blocks of that segment that name the tile are exactly 32. Among the blocks of one phi segment that name one tile, the pairs (block_phi, block_group) take each of the 32 values once. `block_group`: see block_phi.
All inputs are finite; a program needn't handle non-finite values.
Results may differ from a plain program's by a relative error of at most 0.003.
Values may be sent and summed in bfloat16 or wider, within the bound.
A program may use at most 192 MiB of HBM per device.

v0:
```python
import math

import jax
import jax.numpy as jnp
from jax import lax
from jax.sharding import PartitionSpec as P

FIELDS = 5
NPHI = 2048
BPHI = 64
COLS = 256
CG_DEV = 8


def dft_basis(length):
    column = jnp.arange(length, dtype=jnp.int32)
    half = length // 2
    mode = jnp.where(column <= half, column, column - half)
    phase = column[:, None] * mode[None, :] % length
    angle = phase.astype(jnp.float32) * jnp.float32(2.0 * math.pi / length)
    values = jnp.where((column <= half)[None, :], jnp.cos(angle), jnp.sin(angle))
    return (values * jnp.float32(1.0 / math.sqrt(length))).astype(jnp.bfloat16)


def local(blocks, levels, block_dest, block_phi, block_group):
    tile_count = lax.axis_size("tile")
    plane_count = lax.axis_size("phi")
    slot_count = blocks.shape[0]
    per_plane = NPHI // BPHI // plane_count
    capacity = 2 * slot_count // tile_count
    sliver = COLS // plane_count
    weight = (1.0 / jnp.left_shift(1, levels).astype(jnp.float32)).astype(jnp.bfloat16)
    weighted = blocks * weight[:, None, None, None]
    onehot_dest = (block_dest[:, None] == jnp.arange(tile_count, dtype=jnp.int32)[None, :]).astype(
        jnp.int32
    )
    slot_rank = jnp.sum((jnp.cumsum(onehot_dest, axis=0) - 1) * onehot_dest, axis=1)
    send_slot = block_dest * capacity + slot_rank
    outbox = (
        jnp.zeros((tile_count * capacity,) + blocks.shape[1:], jnp.bfloat16)
        .at[send_slot]
        .set(weighted)
    )
    basis_table = dft_basis(NPHI).reshape(plane_count, per_plane, BPHI, NPHI)
    phi_out = jnp.full((tile_count * capacity,), -1, jnp.int32).at[send_slot].set(block_phi)
    group_out = jnp.full((tile_count * capacity,), -1, jnp.int32).at[send_slot].set(block_group)
    arrived, arrived_phi, arrived_group = (
        lax.all_to_all(outbox, "tile", split_axis=0, concat_axis=0, tiled=True),
        lax.all_to_all(phi_out, "tile", split_axis=0, concat_axis=0, tiled=True),
        lax.all_to_all(group_out, "tile", split_axis=0, concat_axis=0, tiled=True),
    )
    recv_slot = jnp.where(arrived_phi >= 0, arrived_phi * CG_DEV + arrived_group, slot_count)
    arranged = (
        jnp.zeros((slot_count,) + blocks.shape[1:], jnp.bfloat16)
        .at[recv_slot]
        .set(arrived, mode="drop")
    )
    arranged = arranged.reshape(per_plane, CG_DEV, FIELDS, BPHI, plane_count, sliver)
    arranged = jnp.transpose(arranged, (4, 2, 0, 1, 3, 5)).reshape(
        plane_count, FIELDS, per_plane, CG_DEV, BPHI * sliver
    )
    pieces = lax.all_to_all(arranged, "phi", split_axis=0, concat_axis=0, tiled=True)
    field_count = pieces.shape[1]
    shaped = pieces.reshape(plane_count, field_count, per_plane, CG_DEV, BPHI, sliver)
    return jnp.einsum("pnagbc,pabk->ngck", shaped, basis_table, preferred_element_type=jnp.float32)


def solution(mesh):
    in_specs = (
        P(("tile", "phi"), None, None, None),
        P(("tile", "phi")),
        P(("tile", "phi")),
        P(("tile", "phi")),
        P(("tile", "phi")),
    )
    out_specs = P(None, "tile", "phi", None)
    return jax.shard_map(local, mesh=mesh, in_specs=in_specs, out_specs=out_specs, check_vma=False)
```

profile of v0, /device:TPU:97, one launch (start us, length us, event | category | flops | bytes accessed | tf_op | source)
XLA Modules:
  0.0 482.6 jit_solution(17838243653629182748)
XLA Ops:
  0.0 0.7 fusion.15
  0.7 0.1 reduce_window_sum.11
  0.8 0.8 select_reduce_fusion
  1.6 0.7 compare_select_fusion.2
  2.3 0.8 scatter_custom_fusion
  3.1 0.7 all_to_all.18
  3.8 6.8 %all-to-all-start = ((s32[16,4,1]{1,2,0:T(1,128)}), s32[16,4,1]{1,2,0:T(1,128)S(1)}, u32[]{:S(2)}, u32[]{:S(2)}) async-start(s32[16,4,1]{1,2,0:T(1,128)} %bitcast), calls=%async_computation | async-start | bytes 16384 | tf_op jit(solution)/shard_map/all_to_all | solution.py:49
  10.5 0.7 divide_convert_fusion
  11.2 0.8 scatter_custom_fusion.1
  12.0 0.7 all_to_all.20
  12.7 4.2 all-to-all-done
  16.9 3.4 all-to-all-start.1
  20.3 5.2 %broadcast_multiply_fusion = bf16[32,5,64,256]{3,2,1,0:T(8,128)(2,1)} fusion(bf16[32,5,64,256]{3,2,1,0:T(8,128)(2,1)} %param.5, bf16[32]{0:T(256)(128)(2,1)S(1)} %divide_convert_fusion), kind=kLoop, calls=%fused_computation.25 | loop fusion | flops 2621440 | bytes 10485824 | tf_op jit(solution)/shard_map/mul | solution.py:33
  25.5 5.4 %broadcast_in_dim.36 = bf16[64,5,64,256]{3,2,1,0:T(8,128)(2,1)} broadcast(bf16[]{:T(256)} %constant.16.clone.1), dimensions={} | broadcast | bytes 10485762 | tf_op jit(solution)/shard_map/broadcast_in_dim | solution.py:40
  31.0 12.4 %scatter_fusion = bf16[64,5,64,256]{3,2,1,0:T(8,128)(2,1)} fusion(bf16[64,5,64,256]{3,2,1,0:T(8,128)(2,1)} %broadcast_in_dim.36, s32[32]{0:T(128)S(1)} %compare_select_fusion.2, bf16[32,5,64,256]{3,2,1,0:T(8,128)(2,1)} %broadcast_multiply_fusion), kind=kCustom, calls=%fused_computation.2 | custom fusion | bytes 15728768 | tf_op jit(solution)/shard_map/scatter | solution.py:42
  43.4 0.0 all-to-all-done.1
  43.4 6.6 %all-to-all-start.2 = ((bf16[64,5,64,256]{3,2,1,0:T(8,128)(2,1)}), bf16[64,5,64,256]{3,2,1,0:T(8,128)(2,1)}, u32[]{:S(2)}, u32[]{:S(2)}) async-start(bf16[64,5,64,256]{3,2,1,0:T(8,128)(2,1)} %scatter_fusion), calls=%async_computation.2 | async-start | bytes 20971520 | tf_op jit(solution)/shard_map/all_to_all | solution.py:48
  50.1 0.1 select_n.52
  50.2 165.9 %all-to-all-done.2 = bf16[64,5,64,256]{3,2,1,0:T(8,128)(2,1)} async-done(((bf16[64,5,64,256]{3,2,1,0:T(8,128)(2,1)}), bf16[64,5,64,256]{3,2,1,0:T(8,128)(2,1)}, u32[]{:S(2)}, u32[]{:S(2)}) %all-to-all-start.2) | async-done | bytes 10485792 | tf_op jit(solution)/shard_map/all_to_all | solution.py:48
  216.1 3.0 broadcast_in_dim.32
  219.1 22.9 %scatter_fusion.1 = bf16[32,5,64,256]{3,2,1,0:T(8,128)(2,1)} fusion(bf16[32,5,64,256]{3,2,1,0:T(8,128)(2,1)} %broadcast_in_dim.32, s32[64]{0:T(128)S(1)} %fusion.17, bf16[64,5,64,256]{3,2,1,0:T(8,128)(2,1)} %all-to-all-done.2), kind=kCustom, calls=%fused_computation.3 | custom fusion | bytes 31457536 | tf_op jit(solution)/shard_map/scatter | solution.py:56
  242.0 10.2 %copy.14 = bf16[32,5,64,256]{2,3,1,0:T(8,128)(2,1)} copy(bf16[32,5,64,256]{3,2,1,0:T(8,128)(2,1)} %scatter_fusion.1) | data formatting | bytes 10485760 | tf_op jit(solution)/shard_map/scatter | solution.py:56
  252.2 19.5 %copy.15 = bf16[8,5,4,8,64,32]{5,4,3,2,1,0:T(8,128)(2,1)} copy(bf16[8,5,4,8,64,32]{4,5,0,1,3,2:T(8,128)(2,1)} %bitcast.21) | data formatting | bytes 10485760 | tf_op jit(solution)/shard_map/transpose | solution.py:59
  271.7 27.9 %reshape.99 = bf16[8,5,4,8,2048]{4,3,2,1,0:T(8,128)(2,1)} reshape(bf16[8,5,4,8,64,32]{5,4,3,2,1,0:T(8,128)(2,1)} %copy.15) | data formatting | bytes 10485760 | tf_op jit(solution)/shard_map/reshape | solution.py:59
  299.6 9.8 %all-to-all-start.3 = ((bf16[8,5,4,8,2048]{4,3,2,1,0:T(8,128)(2,1)}), bf16[8,5,4,8,2048]{4,3,2,1,0:T(8,128)(2,1)}, u32[]{:S(2)}, u32[]{:S(2)}) async-start(bf16[8,5,4,8,2048]{4,3,2,1,0:T(8,128)(2,1)} %reshape.99), calls=%async_computation.3 | async-start | bytes 10485760 | tf_op jit(solution)/shard_map/all_to_all | solution.py:62
  309.4 58.4 %all-to-all-done.3 = bf16[8,5,4,8,2048]{4,3,2,1,0:T(8,128)(2,1)} async-done(((bf16[8,5,4,8,2048]{4,3,2,1,0:T(8,128)(2,1)}), bf16[8,5,4,8,2048]{4,3,2,1,0:T(8,128)(2,1)}, u32[]{:S(2)}, u32[]{:S(2)}) %all-to-all-start.3) | async-done | bytes 5242912 | tf_op jit(solution)/shard_map/all_to_all | solution.py:62
  367.8 24.2 %reshape.100 = bf16[8,5,4,8,64,32]{5,4,3,2,1,0:T(8,128)(2,1)} reshape(bf16[8,5,4,8,2048]{4,3,2,1,0:T(8,128)(2,1)} %all-to-all-done.3) | data formatting | bytes 10485760 | tf_op jit(solution)/shard_map/reshape | solution.py:64
  392.0 80.9 %fusion = f32[5,8,32,2048,1,1]{3,2,4,0,1,5:T(8,128)} fusion(bf16[8,5,4,8,64,32]{5,4,3,2,1,0:T(8,128)(2,1)} %reshape.100, s32[2048]{0:T(1024)S(1)} %add_select_fusion.1, s32[8,4,64]{2,1,0:T(4,128)S(1)} %multiply_add_fusion, pred[2048]{0:T(1024)(128)(4,1)S(1)} %iota_compare_fusion.1), kind=kOutput, calls=%fused_computation.9 | convolution fusion | flops 10808721408 | bytes 15747072 | tf_op jit(solution)/shard_map/pnagbc,pabk->ngck/dot_general | solution.py:65
  472.9 9.7 %copy.25 = f32[5,8,32,2048,1,1]{3,2,1,0,4,5:T(8,128)} copy(f32[5,8,32,2048,1,1]{3,2,4,0,1,5:T(8,128)} %fusion) | data formatting | bytes 20971520 | tf_op jit(solution)/shard_map/pnagbc,pabk->ngck/dot_general | solution.py:65
  (5 shorter events, 0.1 us)
Async XLA Ops:
  3.8 13.1 %all-to-all-start = ((s32[16,4,1]{1,2,0:T(1,128)}), s32[16,4,1]{1,2,0:T(1,128)S(1)}, u32[]{:S(2)}, u32[]{:S(2)}) async-start(s32[16,4,1]{1,2,0:T(1,128)} %bitcast), calls=%async_computation | async-start | bytes 16384 | tf_op jit(solution)/shard_map/all_to_all | solution.py:49
  16.9 26.5 %all-to-all-start.1 = ((s32[16,4,1]{1,2,0:T(1,128)}), s32[16,4,1]{1,2,0:T(1,128)S(1)}, u32[]{:S(2)}, u32[]{:S(2)}) async-start(s32[16,4,1]{1,2,0:T(1,128)} %bitcast.1), calls=%async_computation.1 | async-start | bytes 16384 | tf_op jit(solution)/shard_map/all_to_all | solution.py:50
  43.4 172.7 %all-to-all-start.2 = ((bf16[64,5,64,256]{3,2,1,0:T(8,128)(2,1)}), bf16[64,5,64,256]{3,2,1,0:T(8,128)(2,1)}, u32[]{:S(2)}, u32[]{:S(2)}) async-start(bf16[64,5,64,256]{3,2,1,0:T(8,128)(2,1)} %scatter_fusion), calls=%async_computation.2 | async-start | bytes 20971520 | tf_op jit(solution)/shard_map/all_to_all | solution.py:48
  299.6 68.3 %all-to-all-start.3 = ((bf16[8,5,4,8,2048]{4,3,2,1,0:T(8,128)(2,1)}), bf16[8,5,4,8,2048]{4,3,2,1,0:T(8,128)(2,1)}, u32[]{:S(2)}, u32[]{:S(2)}) async-start(bf16[8,5,4,8,2048]{4,3,2,1,0:T(8,128)(2,1)} %reshape.99), calls=%async_computation.3 | async-start | bytes 10485760 | tf_op jit(solution)/shard_map/all_to_all | solution.py:62
where the time goes:
time: 491 us; the launch traced here: 483 us
  waiting for transfers between devices  228 us (46%)
  local copies, waits for them, and re-layouts  138 us (28%)
  matrix products  80.9 us (16%)
  starting transfers between devices  26.7 us (5%)
  other arithmetic  8.21 us (2%)
    all_to_all x1, waiting for transfers between devices, local(): lax.all_to_all(outbox, 'tile', split_axis=0, concat_axis=0, tiled=True)  166 us
    dot_general x1, matrix products, local(): jnp.einsum('pnagbc,pabk->ngck', shaped, basis_table, preferred_element_ty...  80.9 us
    all_to_all x1, waiting for transfers between devices, local(): lax.all_to_all(arranged, 'phi', split_axis=0, concat_axis=0, tiled=True)  58.4 us
    scatter x2, local copies, waits for them, and re-layouts, local(): arranged = jnp.zeros((slot_count,) + blocks.shape[1:], jnp.bfloat16).at[r...  33.1 us
    reshape x1, local copies, waits for them, and re-layouts, local(): jnp.transpose(arranged, (4, 2, 0, 1, 3, 5))  27.9 us
    reshape x1, local copies, waits for them, and re-layouts, local(): pieces.reshape(plane_count, field_count, per_plane, CG_DEV, BPHI, sliver)  24.2 us
    transpose x1, local copies, waits for them, and re-layouts, local(): jnp.transpose(arranged, (4, 2, 0, 1, 3, 5))  19.5 us
    scatter x1, local copies, waits for them, and re-layouts, local(): outbox = jnp.zeros((tile_count * capacity,) + blocks.shape[1:], jnp.bfloa...  12.4 us
  transfers between devices with their start and end apart: 4, of which 3 were waited for; matrix products, arithmetic and copies ran while one was open for 5% of the time, Pallas kernels for 0%

commit v1 on v0

v1 whole, which is shorter than its diff:
```python
import math

import jax
import jax.numpy as jnp
from jax import lax
from jax.sharding import PartitionSpec as P

FIELDS = 5
NPHI = 2048
BPHI = 64
COLS = 256
CG_DEV = 8


def dft_basis(length):
    half = length // 2
    column = jnp.arange(length, dtype=jnp.int32)
    mode = jnp.where(column <= half, column, column - half)
    scale = jnp.float32(2.0 * math.pi / length)
    hi = jnp.arange(length // BPHI, dtype=jnp.int32) * BPHI
    lo = jnp.arange(BPHI, dtype=jnp.int32)
    angle_hi = (hi[:, None] * mode[None, :] % length).astype(jnp.float32) * scale
    angle_lo = (lo[:, None] * mode[None, :] % length).astype(jnp.float32) * scale
    ch, sh = jnp.cos(angle_hi)[:, None, :], jnp.sin(angle_hi)[:, None, :]
    cl, sl = jnp.cos(angle_lo)[None, :, :], jnp.sin(angle_lo)[None, :, :]
    is_cos = (column <= half)[None, None, :]
    values = jnp.where(is_cos, ch * cl - sh * sl, sh * cl + ch * sl)
    values = values * jnp.float32(1.0 / math.sqrt(length))
    return values.reshape(length, length).astype(jnp.bfloat16)


def local(blocks, levels, block_dest, block_phi, block_group):
    tile_count = lax.axis_size("tile")
    plane_count = lax.axis_size("phi")
    slot_count = blocks.shape[0]
    fields = blocks.shape[1]
    per_plane = NPHI // BPHI // plane_count
    capacity = 2 * slot_count // tile_count
    sliver = COLS // plane_count
    weight = (1.0 / jnp.left_shift(1, levels).astype(jnp.float32)).astype(jnp.bfloat16)

    onehot_dest = (block_dest[:, None] == jnp.arange(tile_count, dtype=jnp.int32)[None, :]).astype(
        jnp.int32
    )
    slot_rank = jnp.sum((jnp.cumsum(onehot_dest, axis=0) - 1) * onehot_dest, axis=1)
    send_slot = block_dest * capacity + slot_rank
    slot_ids = jnp.arange(tile_count * capacity, dtype=jnp.int32)
    match = send_slot[None, :] == slot_ids[:, None]
    filled = jnp.any(match, axis=1)
    source = jnp.argmax(match, axis=1).astype(jnp.int32)
    slot_weight = jnp.where(filled, weight[source], jnp.zeros((), jnp.bfloat16))
    outbox = blocks[source] * slot_weight[:, None, None, None]
    code = jnp.where(filled, block_phi[source] * CG_DEV + block_group[source], -1)

    arrived = lax.all_to_all(outbox, "tile", split_axis=0, concat_axis=0, tiled=True)
    arrived_code = lax.all_to_all(code, "tile", split_axis=0, concat_axis=0, tiled=True)

    want = jnp.arange(slot_count, dtype=jnp.int32)
    pick = jnp.argmax(arrived_code[None, :] == want[:, None], axis=1).astype(jnp.int32)
    arranged = arrived[pick].reshape(per_plane, CG_DEV, fields, BPHI, plane_count, sliver)
    outgoing = jnp.transpose(arranged, (4, 0, 3, 2, 1, 5)).reshape(
        plane_count, per_plane * BPHI, fields, CG_DEV * sliver
    )
    pieces = lax.all_to_all(outgoing, "phi", split_axis=0, concat_axis=0, tiled=True)
    pieces = pieces.reshape(NPHI, fields, CG_DEV * sliver)
    basis = dft_basis(NPHI)
    spectra = lax.dot_general(
        pieces, basis, (((0,), (0,)), ((), ())), preferred_element_type=jnp.float32
    )
    return spectra.reshape(fields, CG_DEV, sliver, NPHI)


def solution(mesh):
    in_specs = (
        P(("tile", "phi"), None, None, None),
        P(("tile", "phi")),
        P(("tile", "phi")),
        P(("tile", "phi")),
        P(("tile", "phi")),
    )
    out_specs = P(None, "tile", "phi", None)
    return jax.shard_map(local, mesh=mesh, in_specs=in_specs, out_specs=out_specs, check_vma=False)
```

time: 491 us -> 375 us (0.76)
  matrix products: 80.9 us -> 17.3 us
  local copies, waits for them, and re-layouts: 138 us -> 76.9 us
  other arithmetic: 8.21 us -> 25.2 us
  starting transfers between devices: 26.7 us -> 21.1 us
    dot_general x1, matrix products: 80.9 us -> 17.3 us  [local(): lax.dot_general(pieces, basis, (((0,), (0,)), ((), ())), preferred_elemen...]
    scatter x5 -> x0, local copies, waits for them, and re-layouts: 47.1 us -> none  [the longest x2 33.1 us: local(): arranged = jnp.zeros((slot_count,) + blocks.shape[1:], jnp.bfloat16).at[r...]
    reshape x2 -> x1, local copies, waits for them, and re-layouts: 52 us -> 15.7 us  [local(): jnp.transpose(arranged, (4, 0, 3, 2, 1, 5))]
    gather x0 -> x6, local copies, waits for them, and re-layouts: none -> 29.5 us  [the longest x2 17.4 us: local(): arrived[pick].reshape(per_plane, CG_DEV, fields, BPHI, plane_count, sliver)]
    all_to_all x3 -> x2, waiting for transfers between devices: 62.6 us -> 48.3 us  [the longest x1 48.3 us: local(): lax.all_to_all(outgoing, 'phi', split_axis=0, concat_axis=0, tiled=True)]
    all_to_all x1, waiting for transfers between devices: 166 us -> 180 us  [local(): lax.all_to_all(outbox, 'tile', split_axis=0, concat_axis=0, tiled=True)]
    broadcast_in_dim x2 -> x0, local copies, waits for them, and re-layouts: 8.45 us -> none  [the longest x1 5.42 us: local(): jnp.zeros((tile_count * capacity,) + blocks.shape[1:], jnp.bfloat16)]
    convert_element_type x0 -> x1, other arithmetic: none -> 7 us  [dft_basis(): return values.reshape(length, length).astype(jnp.bfloat16)]
  transfers between devices with their start and end apart: 4 -> 3, of which waited for: 3 -> 2; matrix products, arithmetic and copies ran while one was open for 5% -> 9% of each run, Pallas kernels for 0% -> 0%
where the time goes in v1:
time: 375 us; the launch traced here: 369 us
  waiting for transfers between devices  228 us (61%)
  local copies, waits for them, and re-layouts  76.9 us (21%)
  other arithmetic  25.2 us (7%)
  starting transfers between devices  21.1 us (6%)
  matrix products  17.3 us (5%)
    all_to_all x1, waiting for transfers between devices, local(): lax.all_to_all(outbox, 'tile', split_axis=0, concat_axis=0, tiled=True)  180 us
    all_to_all x1, waiting for transfers between devices, local(): lax.all_to_all(outgoing, 'phi', split_axis=0, concat_axis=0, tiled=True)  48.3 us
    gather x2, local copies, waits for them, and re-layouts, local(): arrived[pick].reshape(per_plane, CG_DEV, fields, BPHI, plane_count, sliver)  17.4 us
    dot_general x1, matrix products, local(): lax.dot_general(pieces, basis, (((0,), (0,)), ((), ())), preferred_elemen...  17.3 us
    reshape x1, local copies, waits for them, and re-layouts, local(): jnp.transpose(arranged, (4, 0, 3, 2, 1, 5))  15.7 us
    transpose x1, local copies, waits for them, and re-layouts, local(): jnp.transpose(arranged, (4, 0, 3, 2, 1, 5))  14.7 us
    mul x1, other arithmetic, local(): outbox = blocks[source] * slot_weight[:, None, None, None]  9.96 us
    gather x1, local copies, waits for them, and re-layouts, local(): outbox = blocks[source] * slot_weight[:, None, None, None]  9.1 us
  transfers between devices with their start and end apart: 3, of which 2 were waited for; matrix products, arithmetic and copies ran while one was open for 9% of the time, Pallas kernels for 0%

profile of v1, /device:TPU:97, one launch (start us, length us, event | category | flops | bytes accessed | tf_op | source)
XLA Modules:
  0.0 368.6 jit_solution(3955325548200454984)
XLA Ops:
  0.0 0.7 fusion.14
  0.7 0.1 reduce_window_sum.11
  0.8 0.8 select_reduce_fusion
  1.6 0.7 multiply_add_fusion
  2.3 0.6 iota_reduce_fusion.1
  2.9 0.1 fusion.13
  3.0 0.8 gather_fusion.2
  3.8 1.4 gather_fusion.3
  5.2 0.7 select_n.89
  5.9 6.8 %all-to-all-start.1 = ((s32[16,4,1]{1,2,0:T(1,128)}), s32[16,4,1]{1,2,0:T(1,128)S(1)}, u32[]{:S(2)}, u32[]{:S(2)}) async-start(s32[16,4,1]{1,2,0:T(1,128)} %bitcast), calls=%async_computation.1 | async-start | bytes 16384 | tf_op jit(solution)/shard_map/all_to_all | solution.py:56
  12.7 0.7 divide_convert_fusion
  13.4 0.8 gather_fusion.1
  14.1 9.1 %gather_fusion = bf16[64,5,64,256]{3,2,1,0:T(8,128)(2,1)} fusion(bf16[32,5,64,256]{3,2,1,0:T(8,128)(2,1)} %param.5, s32[1024]{0:T(1024)S(1)} %pad_clamp_fusion.1), kind=kCustom, calls=%fused_computation | custom fusion | bytes 20971776 | tf_op jit(solution)/shard_map/gather | solution.py:52
  23.2 10.0 %broadcast_multiply_fusion = bf16[64,5,64,256]{3,2,1,0:T(8,128)(2,1)} fusion(bf16[64,5,64,256]{3,2,1,0:T(8,128)(2,1)} %gather_fusion, bf16[64]{0:T(256)(128)(2,1)S(1)} %broadcast_select_fusion), kind=kLoop, calls=%fused_computation.6 | loop fusion | flops 5242880 | bytes 20971648 | tf_op jit(solution)/shard_map/mul | solution.py:52
  33.2 6.7 %all-to-all-start = ((bf16[64,5,64,256]{3,2,1,0:T(8,128)(2,1)}), bf16[64,5,64,256]{3,2,1,0:T(8,128)(2,1)}, u32[]{:S(2)}, u32[]{:S(2)}) async-start(bf16[64,5,64,256]{3,2,1,0:T(8,128)(2,1)} %broadcast_multiply_fusion), calls=%async_computation | async-start | bytes 20971520 | tf_op jit(solution)/shard_map/all_to_all | solution.py:55
  39.9 0.6 broadcast.317
  40.5 0.7 reduce.41
  41.2 0.1 eq.55
  41.3 0.7 iota_reduce_fusion
  42.0 179.8 %all-to-all-done = bf16[64,5,64,256]{3,2,1,0:T(8,128)(2,1)} async-done(((bf16[64,5,64,256]{3,2,1,0:T(8,128)(2,1)}), bf16[64,5,64,256]{3,2,1,0:T(8,128)(2,1)}, u32[]{:S(2)}, u32[]{:S(2)}) %all-to-all-start) | async-done | bytes 10485792 | tf_op jit(solution)/shard_map/all_to_all | solution.py:55
  221.8 7.2 %gather_fusion.4 = bf16[32,5,64,256]{3,2,1,0:T(8,128)(2,1)} fusion(bf16[64,5,64,256]{3,2,1,0:T(8,128)(2,1)} %all-to-all-done, s32[1024]{0:T(1024)S(1)} %pad_clamp_fusion), kind=kCustom, calls=%fused_computation.4 | custom fusion | bytes 10485888 | tf_op jit(solution)/shard_map/gather | solution.py:60
  229.0 10.2 %copy.17 = bf16[32,5,64,256]{2,3,1,0:T(8,128)(2,1)} copy(bf16[32,5,64,256]{3,2,1,0:T(8,128)(2,1)} %gather_fusion.4) | data formatting | bytes 10485760 | tf_op jit(solution)/shard_map/gather | solution.py:60
  239.2 14.7 %copy.18 = bf16[8,4,64,5,8,32]{2,1,5,4,3,0:T(4,128)(2,1)} copy(bf16[8,4,64,5,8,32]{2,5,0,3,4,1:T(8,128)(2,1)} %bitcast.18) | data formatting | bytes 10485760 | tf_op jit(solution)/shard_map/transpose | solution.py:61
  253.8 15.7 %reshape.241 = bf16[8,256,5,256]{1,3,2,0:T(8,128)(2,1)} reshape(bf16[8,4,64,5,8,32]{2,1,5,4,3,0:T(4,128)(2,1)} %copy.18) | data formatting | bytes 10485760 | tf_op jit(solution)/shard_map/reshape | solution.py:61
  269.6 7.6 %all-to-all-start.2 = ((bf16[8,256,5,256]{1,3,2,0:T(8,128)(2,1)}), bf16[8,256,5,256]{1,3,2,0:T(8,128)(2,1)}, u32[]{:S(2)}, u32[]{:S(2)}) async-start(bf16[8,256,5,256]{1,3,2,0:T(8,128)(2,1)} %reshape.241), calls=%async_computation.2 | async-start | bytes 10485760 | tf_op jit(solution)/shard_map/all_to_all | solution.py:64
  277.2 1.1 fusion.12
  278.3 2.0 fusion.10
  280.4 7.0 %multiply_convert_fusion = bf16[32,64,2048]{2,1,0:T(8,128)(2,1)} fusion(f32[64,2048]{1,0:T(8,128)S(1)} %get-tuple-element.12, f32[32,2048]{1,0:T(8,128)S(1)} %get-tuple-element.10, f32[64,2048]{1,0:T(8,128)S(1)} %get-tuple-element.11, f32[32,2048]{1,0:T(8,128)S(1)} %get-tuple-element.9, pred[2048]{0:T(1024)(128)(4,1)S(1)} %iota_compare_fusion.3), kind=kLoop, calls=%fused_computation.5 | loop fusion | flops 37748736 | bytes 9963520 | tf_op jit(solution)/shard_map/convert_element_type | solution.py:29
  287.4 48.3 %all-to-all-done.2 = bf16[8,256,5,256]{1,3,2,0:T(8,128)(2,1)} async-done(((bf16[8,256,5,256]{1,3,2,0:T(8,128)(2,1)}), bf16[8,256,5,256]{1,3,2,0:T(8,128)(2,1)}, u32[]{:S(2)}, u32[]{:S(2)}) %all-to-all-start.2) | async-done | bytes 5242912 | tf_op jit(solution)/shard_map/all_to_all | solution.py:64
  335.6 7.8 %copy.19 = bf16[8,256,5,256]{3,1,0,2:T(8,128)(2,1)} copy(bf16[8,256,5,256]{1,3,2,0:T(8,128)(2,1)} %all-to-all-done.2) | data formatting | bytes 10485760 | tf_op jit(solution)/shard_map/all_to_all | solution.py:64
  343.4 7.9 %copy.20 = bf16[5,256,2048]{2,1,0:T(8,128)(2,1)} copy(bf16[5,256,2048]{1,2,0:T(8,128)(2,1)} %bitcast.19) | data formatting | bytes 10485760 | tf_op jit(solution)/shard_map/dot_general | solution.py:67
  351.3 17.3 %fusion.15 = f32[5,8,32,2048]{3,2,1,0:T(8,128)} fusion(bf16[5,8,32,2048]{3,2,1,0:T(8,128)(2,1)} %bitcast.21, bf16[2048,2048,1,1]{1,0,3,2:T(8,128)(2,1)} %bitcast.20), kind=kOutput, calls=%fused_computation.47 | convolution fusion | flops 10737418240 | bytes 24117248 | tf_op jit(solution)/shard_map/dot_general | solution.py:67
  (14 shorter events, 0.1 us)
Async XLA Ops:
  0.0 3.0 copy-start
  5.9 27.3 %all-to-all-start.1 = ((s32[16,4,1]{1,2,0:T(1,128)}), s32[16,4,1]{1,2,0:T(1,128)S(1)}, u32[]{:S(2)}, u32[]{:S(2)}) async-start(s32[16,4,1]{1,2,0:T(1,128)} %bitcast), calls=%async_computation.1 | async-start | bytes 16384 | tf_op jit(solution)/shard_map/all_to_all | solution.py:56
  33.2 188.5 %all-to-all-start = ((bf16[64,5,64,256]{3,2,1,0:T(8,128)(2,1)}), bf16[64,5,64,256]{3,2,1,0:T(8,128)(2,1)}, u32[]{:S(2)}, u32[]{:S(2)}) async-start(bf16[64,5,64,256]{3,2,1,0:T(8,128)(2,1)} %broadcast_multiply_fusion), calls=%async_computation | async-start | bytes 20971520 | tf_op jit(solution)/shard_map/all_to_all | solution.py:55
  269.6 66.1 %all-to-all-start.2 = ((bf16[8,256,5,256]{1,3,2,0:T(8,128)(2,1)}), bf16[8,256,5,256]{1,3,2,0:T(8,128)(2,1)}, u32[]{:S(2)}, u32[]{:S(2)}) async-start(bf16[8,256,5,256]{1,3,2,0:T(8,128)(2,1)} %reshape.241), calls=%async_computation.2 | async-start | bytes 10485760 | tf_op jit(solution)/shard_map/all_to_all | solution.py:64
  351.3 17.3 %copy-start.1 = (s32[32]{0:T(128)S(1)}, s32[32]{0:T(128)}, u32[]{:S(2)}) copy-start(s32[32]{0:T(128)} %param.8) | copy-start | bytes 388

commit v2 on v1

--- a/solution.py
+++ b/solution.py
@@ -1,8 +1,11 @@
+import functools
 import math
 
 import jax
 import jax.numpy as jnp
 from jax import lax
+from jax.experimental import pallas as pl
+from jax.experimental.pallas import tpu as pltpu
 from jax.sharding import PartitionSpec as P
 
 FIELDS = 5
@@ -29,6 +32,54 @@
     return values.reshape(length, length).astype(jnp.bfloat16)
 
 
+def exchange_kernel(tile_count, capacity, src_ref, dst_ref, send_sem, recv_sem, own_sem):
+    me = lax.axis_index("tile")
+    plane = lax.axis_index("phi")
+    mesh_ids = pl.DeviceIdType.MESH
+    barrier = pltpu.get_barrier_semaphore()
+    for step in range(1, tile_count):
+        peer = lax.rem(me + step, tile_count)
+        pl.semaphore_signal(barrier, inc=1, device_id=(peer, plane), device_id_type=mesh_ids)
+    pl.semaphore_wait(barrier, tile_count - 1)
+    own = pltpu.make_async_copy(
+        src_ref.at[pl.ds(me * capacity, capacity)],
+        dst_ref.at[pl.ds(me * capacity, capacity)],
+        own_sem,
+    )
+    own.start()
+    copies = []
+    for step in range(1, tile_count):
+        peer = lax.rem(me + step, tile_count)
+        copy = pltpu.make_async_remote_copy(
+            src_ref=src_ref.at[pl.ds(peer * capacity, capacity)],
+            dst_ref=dst_ref.at[pl.ds(me * capacity, capacity)],
+            send_sem=send_sem.at[step],
+            recv_sem=recv_sem.at[step],
+            device_id=(peer, plane),
+            device_id_type=mesh_ids,
+        )
+        copy.start()
+        copies.append(copy)
+    for copy in copies:
+        copy.wait()
+    own.wait()
+
+
+def tile_exchange(outbox, tile_count, capacity):
+    return pl.pallas_call(
+        functools.partial(exchange_kernel, tile_count, capacity),
+        out_shape=jax.ShapeDtypeStruct(outbox.shape, outbox.dtype),
+        in_specs=[pl.BlockSpec(memory_space=pl.ANY)],
+        out_specs=pl.BlockSpec(memory_space=pl.ANY),
+        scratch_shapes=[
+            pltpu.SemaphoreType.DMA((tile_count,)),
+            pltpu.SemaphoreType.DMA((tile_count,)),
+            pltpu.SemaphoreType.DMA,
+        ],
+        compiler_params=pltpu.CompilerParams(collective_id=0, has_side_effects=True),
+    )(outbox)
+
+
 def local(blocks, levels, block_dest, block_phi, block_group):
     tile_count = lax.axis_size("tile")
     plane_count = lax.axis_size("phi")
@@ -37,8 +88,6 @@
     per_plane = NPHI // BPHI // plane_count
     capacity = 2 * slot_count // tile_count
     sliver = COLS // plane_count
-    weight = (1.0 / jnp.left_shift(1, levels).astype(jnp.float32)).astype(jnp.bfloat16)
-
     onehot_dest = (block_dest[:, None] == jnp.arange(tile_count, dtype=jnp.int32)[None, :]).astype(
         jnp.int32
     )
@@ -48,16 +97,20 @@
     match = send_slot[None, :] == slot_ids[:, None]
     filled = jnp.any(match, axis=1)
     source = jnp.argmax(match, axis=1).astype(jnp.int32)
-    slot_weight = jnp.where(filled, weight[source], jnp.zeros((), jnp.bfloat16))
-    outbox = blocks[source] * slot_weight[:, None, None, None]
-    code = jnp.where(filled, block_phi[source] * CG_DEV + block_group[source], -1)
+    outbox = blocks[source]
+    place = block_phi[source] * CG_DEV + block_group[source]
+    code = jnp.where(filled, levels[source] * slot_count + place, -1)
 
-    arrived = lax.all_to_all(outbox, "tile", split_axis=0, concat_axis=0, tiled=True)
+    arrived = tile_exchange(outbox, tile_count, capacity)
     arrived_code = lax.all_to_all(code, "tile", split_axis=0, concat_axis=0, tiled=True)
 
     want = jnp.arange(slot_count, dtype=jnp.int32)
-    pick = jnp.argmax(arrived_code[None, :] == want[:, None], axis=1).astype(jnp.int32)
-    arranged = arrived[pick].reshape(per_plane, CG_DEV, fields, BPHI, plane_count, sliver)
+    hit = (arrived_code[None, :] % slot_count == want[:, None]) & (arrived_code[None, :] >= 0)
+    pick = jnp.argmax(hit, axis=1).astype(jnp.int32)
+    level_of = arrived_code[pick] // slot_count
+    weight = (1.0 / jnp.left_shift(1, level_of).astype(jnp.float32)).astype(jnp.bfloat16)
+    arranged = arrived[pick] * weight[:, None, None, None]
+    arranged = arranged.reshape(per_plane, CG_DEV, fields, BPHI, plane_count, sliver)
     outgoing = jnp.transpose(arranged, (4, 0, 3, 2, 1, 5)).reshape(
         plane_count, per_plane * BPHI, fields, CG_DEV * sliver
     )

time: 375 us -> 410 us (1.093)
  the two profiles are of different devices: /device:TPU:97 before, /device:TPU:28 now
where the time goes in v2:
time: 410 us; the launch traced here: 409 us
  Pallas kernels  236 us (58%)
  local copies, waits for them, and re-layouts  71.5 us (17%)
  waiting for transfers between devices  50.8 us (12%)
  other arithmetic  20.2 us (5%)
  matrix products  17.3 us (4%)
  starting transfers between devices  12.8 us (3%)
    pallas_call x1, Pallas kernels, tile_exchange(): pl.pallas_call(functools.partial(exchange_kernel, tile_count, capacity),...  236 us
    all_to_all x1, waiting for transfers between devices, local(): lax.all_to_all(outgoing, 'phi', split_axis=0, concat_axis=0, tiled=True)  50.8 us
    gather x2, local copies, waits for them, and re-layouts, local(): arranged = arrived[pick] * weight[:, None, None, None]  17.4 us
    dot_general x1, matrix products, local(): lax.dot_general(pieces, basis, (((0,), (0,)), ((), ())), preferred_elemen...  17.3 us
    reshape x1, local copies, waits for them, and re-layouts, local(): jnp.transpose(arranged, (4, 0, 3, 2, 1, 5))  15.7 us
    gather x1, local copies, waits for them, and re-layouts, local(): outbox = blocks[source]  9 us
  transfers between devices with their start and end apart: 2, of which 1 were waited for; matrix products, arithmetic and copies ran while one was open for 5% of the time, Pallas kernels for 58%

profile of v2, /device:TPU:28, one launch (start us, length us, event | category | flops | bytes accessed | tf_op | source)
XLA Modules:
  0.0 408.7 jit_solution(2299132485027257262)
XLA Ops:
  0.0 0.7 fusion.14
  0.7 0.1 reduce_window_sum.11
  0.8 0.8 select_reduce_fusion
  1.6 0.7 multiply_add_fusion
  2.3 0.6 iota_reduce_fusion.1
  2.9 0.1 fusion.13
  3.0 0.8 gather_fusion.1
  3.8 1.4 gather_fusion.2
  5.2 1.4 gather_fusion.3
  6.7 0.7 select_n.101
  7.4 7.1 %all-to-all-start = ((s32[16,4,1]{1,2,0:T(1,128)}), s32[16,4,1]{1,2,0:T(1,128)S(1)}, u32[]{:S(2)}, u32[]{:S(2)}) async-start(s32[16,4,1]{1,2,0:T(1,128)} %bitcast), calls=%async_computation | async-start | bytes 16384 | tf_op jit(solution)/shard_map/all_to_all | solution.py:105
  14.5 9.0 %gather_fusion = bf16[64,5,64,256]{3,2,1,0:T(8,128)(2,1)} fusion(bf16[32,5,64,256]{3,2,1,0:T(8,128)(2,1)} %param.5, s32[1024]{0:T(1024)S(1)} %pad_clamp_fusion.1), kind=kCustom, calls=%fused_computation | custom fusion | bytes 20971776 | tf_op jit(solution)/shard_map/gather | solution.py:100
  23.5 235.9 %shard_map.55 = bf16[64,5,64,256]{3,2,1,0:T(8,128)(2,1)} custom-call(bf16[64,5,64,256]{3,2,1,0:T(8,128)(2,1)} %gather_fusion), custom_call_target="tpu_custom_call" | custom-call | tf_op jit(solution)/shard_map/pallas_call | solution.py:69
  259.4 0.5 broadcast.412
  259.9 0.7 reduce.41
  260.6 0.1 all_to_all.10
  260.7 0.6 iota_reduce_fusion
  261.4 0.7 gather_fusion.5
  262.1 0.1 gather.29
  262.2 7.2 %gather_fusion.4 = bf16[32,5,64,256]{3,2,1,0:T(8,128)(2,1)} fusion(bf16[64,5,64,256]{3,2,1,0:T(8,128)(2,1)} %shard_map.55, s32[1024]{0:T(1024)S(1)} %pad_clamp_fusion), kind=kCustom, calls=%fused_computation.4 | custom fusion | bytes 10485888 | tf_op jit(solution)/shard_map/gather | solution.py:112
  269.4 10.2 %copy.18 = bf16[32,5,64,256]{2,3,1,0:T(8,128)(2,1)} copy(bf16[32,5,64,256]{3,2,1,0:T(8,128)(2,1)} %gather_fusion.4) | data formatting | bytes 10485760 | tf_op jit(solution)/shard_map/gather | solution.py:112
  279.6 5.7 %multiply_bitcast_fusion = bf16[8,4,64,5,8,32]{2,5,0,3,4,1:T(8,128)(2,1)S(1)} fusion(bf16[4,8,5,64,8,32]{3,5,4,2,1,0:T(8,128)(2,1)} %bitcast.18, bf16[4,8]{1,0:T(4,128)(2,1)S(1)} %fusion.20), kind=kLoop, calls=%fused_computation.7 | loop fusion | flops 2621440 | bytes 10485824 | tf_op jit(solution)/shard_map/transpose | solution.py:114
  285.2 8.0 %copy.19 = bf16[8,4,64,5,8,32]{2,1,5,4,3,0:T(4,128)(2,1)} copy(bf16[8,4,64,5,8,32]{2,5,0,3,4,1:T(8,128)(2,1)S(1)} %multiply_bitcast_fusion) | data formatting | bytes 10485760 | tf_op jit(solution)/shard_map/transpose | solution.py:114
  293.3 15.7 %reshape.305 = bf16[8,256,5,256]{1,3,2,0:T(8,128)(2,1)} reshape(bf16[8,4,64,5,8,32]{2,1,5,4,3,0:T(4,128)(2,1)} %copy.19) | data formatting | bytes 10485760 | tf_op jit(solution)/shard_map/reshape | solution.py:114
  309.0 5.7 %all-to-all-start.1 = ((bf16[8,256,5,256]{1,3,2,0:T(8,128)(2,1)}), bf16[8,256,5,256]{1,3,2,0:T(8,128)(2,1)}, u32[]{:S(2)}, u32[]{:S(2)}) async-start(bf16[8,256,5,256]{1,3,2,0:T(8,128)(2,1)} %reshape.305), calls=%async_computation.1 | async-start | bytes 10485760 | tf_op jit(solution)/shard_map/all_to_all | solution.py:117
  314.7 1.1 fusion.12
  315.8 2.0 fusion.10
  317.9 7.0 %multiply_convert_fusion = bf16[32,64,2048]{2,1,0:T(8,128)(2,1)} fusion(f32[64,2048]{1,0:T(8,128)S(1)} %get-tuple-element.12, f32[32,2048]{1,0:T(8,128)S(1)} %get-tuple-element.10, f32[64,2048]{1,0:T(8,128)S(1)} %get-tuple-element.11, f32[32,2048]{1,0:T(8,128)S(1)} %get-tuple-element.9, pred[2048]{0:T(1024)(128)(4,1)S(1)} %iota_compare_fusion.3), kind=kLoop, calls=%fused_computation.6 | loop fusion | flops 37748736 | bytes 9963520 | tf_op jit(solution)/shard_map/convert_element_type | solution.py:32
  324.9 50.8 %all-to-all-done.1 = bf16[8,256,5,256]{1,3,2,0:T(8,128)(2,1)} async-done(((bf16[8,256,5,256]{1,3,2,0:T(8,128)(2,1)}), bf16[8,256,5,256]{1,3,2,0:T(8,128)(2,1)}, u32[]{:S(2)}, u32[]{:S(2)}) %all-to-all-start.1) | async-done | bytes 5242912 | tf_op jit(solution)/shard_map/all_to_all | solution.py:117
  375.7 7.8 %copy.20 = bf16[8,256,5,256]{3,1,0,2:T(8,128)(2,1)} copy(bf16[8,256,5,256]{1,3,2,0:T(8,128)(2,1)} %all-to-all-done.1) | data formatting | bytes 10485760 | tf_op jit(solution)/shard_map/all_to_all | solution.py:117
  383.5 7.9 %copy.21 = bf16[5,256,2048]{2,1,0:T(8,128)(2,1)} copy(bf16[5,256,2048]{1,2,0:T(8,128)(2,1)} %bitcast.19) | data formatting | bytes 10485760 | tf_op jit(solution)/shard_map/dot_general | solution.py:120
  391.4 17.3 %fusion.23 = f32[5,8,32,2048]{3,2,1,0:T(8,128)} fusion(bf16[5,8,32,2048]{3,2,1,0:T(8,128)(2,1)} %bitcast.21, bf16[2048,2048,1,1]{1,0,3,2:T(8,128)(2,1)} %bitcast.20), kind=kOutput, calls=%fused_computation.63 | convolution fusion | flops 10737418240 | bytes 24117248 | tf_op jit(solution)/shard_map/dot_general | solution.py:120
  (16 shorter events, 0.1 us)
Async XLA Ops:
  0.0 3.0 copy-start
  7.4 252.1 %all-to-all-start = ((s32[16,4,1]{1,2,0:T(1,128)}), s32[16,4,1]{1,2,0:T(1,128)S(1)}, u32[]{:S(2)}, u32[]{:S(2)}) async-start(s32[16,4,1]{1,2,0:T(1,128)} %bitcast), calls=%async_computation | async-start | bytes 16384 | tf_op jit(solution)/shard_map/all_to_all | solution.py:105
  309.0 66.7 %all-to-all-start.1 = ((bf16[8,256,5,256]{1,3,2,0:T(8,128)(2,1)}), bf16[8,256,5,256]{1,3,2,0:T(8,128)(2,1)}, u32[]{:S(2)}, u32[]{:S(2)}) async-start(bf16[8,256,5,256]{1,3,2,0:T(8,128)(2,1)} %reshape.305), calls=%async_computation.1 | async-start | bytes 10485760 | tf_op jit(solution)/shard_map/all_to_all | solution.py:117
  391.4 17.3 %copy-start.1 = (s32[32]{0:T(128)S(1)}, s32[32]{0:T(128)}, u32[]{:S(2)}) copy-start(s32[32]{0:T(128)} %param.6) | copy-start | bytes 388

commit v3 on v1

--- a/solution.py
+++ b/solution.py
@@ -48,21 +48,37 @@
     match = send_slot[None, :] == slot_ids[:, None]
     filled = jnp.any(match, axis=1)
     source = jnp.argmax(match, axis=1).astype(jnp.int32)
-    slot_weight = jnp.where(filled, weight[source], jnp.zeros((), jnp.bfloat16))
-    outbox = blocks[source] * slot_weight[:, None, None, None]
-    code = jnp.where(filled, block_phi[source] * CG_DEV + block_group[source], -1)
+    place = block_phi[source] * CG_DEV + block_group[source]
+    code = jnp.where(filled, levels[source] * slot_count + place, -1)
+    device_count = tile_count * plane_count
 
-    arrived = lax.all_to_all(outbox, "tile", split_axis=0, concat_axis=0, tiled=True)
-    arrived_code = lax.all_to_all(code, "tile", split_axis=0, concat_axis=0, tiled=True)
+    outbox = blocks[source].reshape(tile_count, capacity, fields, BPHI, plane_count, sliver)
+    outbox = jnp.transpose(outbox, (0, 4, 1, 2, 3, 5)).reshape(
+        device_count, capacity, fields, BPHI, sliver
+    )
+    code_out = jnp.broadcast_to(
+        code.reshape(tile_count, 1, capacity), (tile_count, plane_count, capacity)
+    ).reshape(device_count, capacity)
+    arrived = lax.all_to_all(outbox, ("tile", "phi"), split_axis=0, concat_axis=0, tiled=True)
+    arrived_code = lax.all_to_all(code_out, ("tile", "phi"), split_axis=0, concat_axis=0, tiled=True)
 
+    by_segment = jnp.transpose(
+        arrived_code.reshape(tile_count, plane_count, capacity), (1, 0, 2)
+    ).reshape(plane_count, tile_count * capacity)
     want = jnp.arange(slot_count, dtype=jnp.int32)
-    pick = jnp.argmax(arrived_code[None, :] == want[:, None], axis=1).astype(jnp.int32)
-    arranged = arrived[pick].reshape(per_plane, CG_DEV, fields, BPHI, plane_count, sliver)
-    outgoing = jnp.transpose(arranged, (4, 0, 3, 2, 1, 5)).reshape(
-        plane_count, per_plane * BPHI, fields, CG_DEV * sliver
+    hit = (by_segment[:, None, :] % slot_count == want[None, :, None]) & (
+        by_segment[:, None, :] >= 0
     )
-    pieces = lax.all_to_all(outgoing, "phi", split_axis=0, concat_axis=0, tiled=True)
-    pieces = pieces.reshape(NPHI, fields, CG_DEV * sliver)
+    pick = jnp.argmax(hit, axis=2).astype(jnp.int32)
+    origin = pick // capacity
+    segment = jnp.arange(plane_count, dtype=jnp.int32)[:, None]
+    flat = (origin * plane_count + segment) * capacity + pick % capacity
+    level_of = jnp.take_along_axis(by_segment, pick, axis=1) // slot_count
+    weight = (1.0 / jnp.left_shift(1, level_of).astype(jnp.float32)).astype(jnp.bfloat16)
+    gathered = arrived.reshape(device_count * capacity, fields, BPHI, sliver)[flat.reshape(-1)]
+    gathered = gathered * weight.reshape(-1)[:, None, None, None]
+    gathered = gathered.reshape(plane_count, per_plane, CG_DEV, fields, BPHI, sliver)
+    pieces = jnp.transpose(gathered, (0, 1, 4, 3, 2, 5)).reshape(NPHI, fields, CG_DEV * sliver)
     basis = dft_basis(NPHI)
     spectra = lax.dot_general(
         pieces, basis, (((0,), (0,)), ((), ())), preferred_element_type=jnp.float32

time: 375 us -> 344 us (0.917)
  waiting for transfers between devices: 228 us -> 124 us
  local copies, waits for them, and re-layouts: 76.9 us -> 159 us
  other arithmetic: 25.2 us -> 20.4 us
    all_to_all x3 -> x2, waiting for transfers between devices: 228 us -> 124 us  [the longest x1 124 us: local(): lax.all_to_all(outbox, ('tile', 'phi'), split_axis=0, concat_axis=0, tile...]
    unnamed x4 -> x6, local copies, waits for them, and re-layouts: 0.01 us -> 62.3 us
    gather x6 -> x9, local copies, waits for them, and re-layouts: 29.5 us -> 51 us  [the longest x2 28.3 us: local(): blocks[source]]
    transpose x1 -> x3, local copies, waits for them, and re-layouts: 14.7 us -> 27.5 us  [the longest x1 19.3 us: local(): jnp.transpose(outbox, (0, 4, 1, 2, 3, 5))]
    mul x1 -> x0, other arithmetic: 9.96 us -> none  [local(): outbox = blocks[source] * slot_weight[:, None, None, None]]
    all_to_all x2 -> x0, local copies, waits for them, and re-layouts: 8.34 us -> none  [the longest x1 7.76 us: local(): lax.all_to_all(outgoing, 'phi', split_axis=0, concat_axis=0, tiled=True)]
    dot_general x1 -> x0, local copies, waits for them, and re-layouts: 7.89 us -> none  [local(): lax.dot_general(pieces, basis, (((0,), (0,)), ((), ())), preferred_elemen...]
    transpose x0 -> x1, other arithmetic: none -> 6.1 us  [local(): jnp.transpose(gathered, (0, 1, 4, 3, 2, 5))]
  transfers between devices with their start and end apart: 3 -> 2, of which waited for: 2 -> 1; matrix products, arithmetic and copies ran while one was open for 9% -> 27% of each run, Pallas kernels for 0% -> 0%
where the time goes in v3:
time: 344 us; the launch traced here: 341 us
  local copies, waits for them, and re-layouts  159 us (46%)
  waiting for transfers between devices  124 us (36%)
  other arithmetic  20.4 us (6%)
  starting transfers between devices  20.3 us (6%)
  matrix products  17.3 us (5%)
    all_to_all x1, waiting for transfers between devices, local(): lax.all_to_all(outbox, ('tile', 'phi'), split_axis=0, concat_axis=0, tile...  124 us
    unnamed x6, local copies, waits for them, and re-layouts  62.3 us
    gather x2, local copies, waits for them, and re-layouts, local(): blocks[source]  28.3 us
    transpose x1, local copies, waits for them, and re-layouts, local(): jnp.transpose(outbox, (0, 4, 1, 2, 3, 5))  19.3 us
    dot_general x1, matrix products, local(): lax.dot_general(pieces, basis, (((0,), (0,)), ((), ())), preferred_elemen...  17.3 us
    reshape x1, local copies, waits for them, and re-layouts, local(): jnp.transpose(gathered, (0, 1, 4, 3, 2, 5))  17.1 us
    gather x1, local copies, waits for them, and re-layouts, local(): arrived.reshape(device_count * capacity, fields, BPHI, sliver)  16.9 us
    all_to_all x1, starting transfers between devices, local(): lax.all_to_all(outbox, ('tile', 'phi'), split_axis=0, concat_axis=0, tile...  10.2 us
  transfers between devices with their start and end apart: 2, of which 1 were waited for; matrix products, arithmetic and copies ran while one was open for 27% of the time, Pallas kernels for 0%

profile of v3, /device:TPU:97, one launch (start us, length us, event | category | flops | bytes accessed | tf_op | source)
XLA Modules:
  0.0 340.7 jit_solution(5290003267412906432)
XLA Ops:
  0.0 0.7 fusion.20
  0.8 0.8 select_reduce_fusion
  1.6 0.7 multiply_add_fusion
  2.3 0.6 iota_reduce_fusion.1
  2.9 0.1 fusion.19
  3.0 0.8 gather_fusion.3
  3.8 1.4 gather_fusion.2
  5.2 1.4 gather_fusion.1
  6.7 0.1 select_n.128
  6.8 0.6 broadcast_in_dim.19.clone
  7.4 10.2 %all-to-all-start.1 = ((s32[128,1,4]{2,1,0:T(1,128)}), s32[128,1,4]{2,1,0:T(1,128)S(1)}, u32[]{:S(2)}, u32[]{:S(2)}) async-start(s32[128,1,4]{2,1,0:T(1,128)} %bitcast.4), calls=%async_computation.1 | async-start | bytes 131072 | tf_op jit(solution)/shard_map/all_to_all | solution.py:63
  17.6 9.0 %gather_fusion = bf16[64,5,64,256]{3,2,1,0:T(8,128)(2,1)} fusion(bf16[32,5,64,256]{3,2,1,0:T(8,128)(2,1)} %param.5, s32[1024]{0:T(1024)S(1)} %pad_clamp_fusion.1), kind=kCustom, calls=%fused_computation | custom fusion | bytes 20971776 | tf_op jit(solution)/shard_map/gather | solution.py:55
  26.6 19.3 %copy.33 = bf16[64,5,64,256]{2,3,1,0:T(8,128)(2,1)} copy(bf16[64,5,64,256]{3,2,1,0:T(8,128)(2,1)} %gather_fusion) | data formatting | bytes 20971520 | tf_op jit(solution)/shard_map/gather | solution.py:55
  45.9 19.3 %copy.34 = bf16[16,8,4,5,64,32]{4,5,3,2,1,0:T(8,128)(2,1)} copy(bf16[16,8,4,5,64,32]{4,5,1,3,2,0:T(8,128)(2,1)} %bitcast.38) | data formatting | bytes 20971520 | tf_op jit(solution)/shard_map/transpose | solution.py:56
  65.3 30.7 %reshape.410 = bf16[128,2,20480]{2,1,0:T(2,128)(2,1)} reshape(bf16[128,4,5,32,64]{4,3,2,1,0:T(8,128)(2,1)} %bitcast.39) | data formatting | bytes 20971520
  96.0 10.2 %all-to-all-start = ((bf16[128,2,20480]{2,1,0:T(2,128)(2,1)}), bf16[128,2,20480]{2,1,0:T(2,128)(2,1)}, u32[]{:S(2)}, u32[]{:S(2)}) async-start(bf16[128,2,20480]{2,1,0:T(2,128)(2,1)} %reshape.410), calls=%async_computation | async-start | bytes 20971520 | tf_op jit(solution)/shard_map/all_to_all | solution.py:62
  106.2 1.1 fusion.12
  107.3 2.0 fusion.10
  109.4 7.1 %multiply_convert_fusion = bf16[32,64,2048]{2,1,0:T(8,128)(2,1)} fusion(f32[64,2048]{1,0:T(8,128)S(1)} %get-tuple-element.12, f32[32,2048]{1,0:T(8,128)S(1)} %get-tuple-element.10, f32[64,2048]{1,0:T(8,128)S(1)} %get-tuple-element.11, f32[32,2048]{1,0:T(8,128)S(1)} %get-tuple-element.9, pred[2048]{0:T(1024)(128)(4,1)S(1)} %iota_compare_fusion.3), kind=kLoop, calls=%fused_computation.6 | loop fusion | flops 37748736 | bytes 9963520 | tf_op jit(solution)/shard_map/convert_element_type | solution.py:29
  116.4 0.2 copy.38
  116.8 1.0 iota_reduce_fusion
  117.7 0.1 reshape.394
  117.8 2.0 gather_fusion.5
  119.9 0.1 reshape.351
  120.0 0.1 select_n.135
  120.2 123.5 %all-to-all-done = bf16[128,2,20480]{2,1,0:T(2,128)(2,1)} async-done(((bf16[128,2,20480]{2,1,0:T(2,128)(2,1)}), bf16[128,2,20480]{2,1,0:T(2,128)(2,1)}, u32[]{:S(2)}, u32[]{:S(2)}) %all-to-all-start) | async-done | bytes 10485792 | tf_op jit(solution)/shard_map/all_to_all | solution.py:62
  243.7 31.5 %reshape.411 = bf16[128,4,5,32,64]{4,3,2,1,0:T(8,128)(2,1)} reshape(bf16[128,2,20480]{2,1,0:T(2,128)(2,1)} %all-to-all-done) | data formatting | bytes 20971520
  275.2 16.9 %gather_fusion.4 = bf16[256,5,64,32]{2,3,1,0:T(8,128)(2,1)} fusion(bf16[512,5,64,32]{2,3,1,0:T(8,128)(2,1)} %bitcast.37, s32[1024]{0:T(1024)S(1)} %pad_clamp_fusion), kind=kCustom, calls=%fused_computation.4 | custom fusion | bytes 10486784 | tf_op jit(solution)/shard_map/gather | solution.py:78
  292.1 6.1 %multiply_bitcast_fusion = bf16[8,4,64,5,8,32]{2,5,3,4,1,0:T(8,128)(2,1)S(1)} fusion(bf16[8,4,8,5,64,32]{4,5,3,2,1,0:T(8,128)(2,1)} %bitcast.36, bf16[8,4,8]{2,1,0:T(4,128)(2,1)S(1)} %fusion.21), kind=kLoop, calls=%fused_computation.7 | loop fusion | flops 2621440 | bytes 10486272 | tf_op jit(solution)/shard_map/transpose | solution.py:81
  298.2 8.0 %copy.41 = bf16[8,4,64,5,8,32]{2,1,0,5,4,3:T(4,128)(2,1)} copy(bf16[8,4,64,5,8,32]{2,5,3,4,1,0:T(8,128)(2,1)S(1)} %multiply_bitcast_fusion) | data formatting | bytes 10485760 | tf_op jit(solution)/shard_map/transpose | solution.py:81
  306.2 17.1 %reshape.353 = bf16[2048,5,256]{0,2,1:T(8,128)(2,1)} reshape(bf16[8,4,64,5,8,32]{2,1,0,5,4,3:T(4,128)(2,1)} %copy.41) | data formatting | bytes 10485760 | tf_op jit(solution)/shard_map/reshape | solution.py:81
  323.3 17.3 %fusion.31 = f32[5,8,32,2048]{3,2,1,0:T(8,128)} fusion(bf16[5,8,32,2048]{3,2,1,0:T(8,128)(2,1)} %bitcast.41, bf16[2048,2048,1,1]{1,0,3,2:T(8,128)(2,1)} %bitcast.40), kind=kOutput, calls=%fused_computation.80 | convolution fusion | flops 10737418240 | bytes 24117248 | tf_op jit(solution)/shard_map/dot_general | solution.py:83
  (22 shorter events, 0.4 us)
Async XLA Ops:
  0.0 3.0 copy-start
  7.4 88.6 %all-to-all-start.1 = ((s32[128,1,4]{2,1,0:T(1,128)}), s32[128,1,4]{2,1,0:T(1,128)S(1)}, u32[]{:S(2)}, u32[]{:S(2)}) async-start(s32[128,1,4]{2,1,0:T(1,128)} %bitcast.4), calls=%async_computation.1 | async-start | bytes 131072 | tf_op jit(solution)/shard_map/all_to_all | solution.py:63
  96.0 147.7 %all-to-all-start = ((bf16[128,2,20480]{2,1,0:T(2,128)(2,1)}), bf16[128,2,20480]{2,1,0:T(2,128)(2,1)}, u32[]{:S(2)}, u32[]{:S(2)}) async-start(bf16[128,2,20480]{2,1,0:T(2,128)(2,1)} %reshape.410), calls=%async_computation | async-start | bytes 20971520 | tf_op jit(solution)/shard_map/all_to_all | solution.py:62
  323.3 17.3 %copy-start.1 = (s32[32]{0:T(128)S(1)}, s32[32]{0:T(128)}, u32[]{:S(2)}) copy-start(s32[32]{0:T(128)} %param.9) | copy-start | bytes 388

commit v4 on v3

--- a/solution.py
+++ b/solution.py
@@ -1,8 +1,11 @@
+import functools
 import math
 
 import jax
 import jax.numpy as jnp
 from jax import lax
+from jax.experimental import pallas as pl
+from jax.experimental.pallas import tpu as pltpu
 from jax.sharding import PartitionSpec as P
 
 FIELDS = 5
@@ -29,6 +32,105 @@
     return values.reshape(length, length).astype(jnp.bfloat16)
 
 
+def pack_kernel(source_ref, scale_ref, first_ref, second_ref, out_ref):
+    tile = pl.program_id(0)
+    pair = pl.program_id(1)
+    slot = (tile * pl.num_programs(1) + pair) * 2
+    first_scale = scale_ref[slot]
+    second_scale = scale_ref[slot + 1]
+    fields, planes, sliver = out_ref.shape[3], out_ref.shape[1], out_ref.shape[4]
+    for field in range(fields):
+        both = jnp.concatenate(
+            [
+                first_ref[0, field].astype(jnp.float32) * first_scale,
+                second_ref[0, field].astype(jnp.float32) * second_scale,
+            ],
+            axis=0,
+        )
+        flipped = both.T.reshape(planes, sliver, both.shape[0])
+        out_ref[0, :, 0, field] = flipped.astype(out_ref.dtype)
+
+
+def pack_outbox(blocks, source, scale, tile_count, capacity, plane_count):
+    slot_count, fields, bphi, cols = blocks.shape
+    pairs = capacity // 2
+    sliver = cols // plane_count
+
+    def block_map(half):
+        return lambda t, q, src_ref: (src_ref[(t * pairs + q) * 2 + half], 0, 0, 0)
+
+    return pl.pallas_call(
+        pack_kernel,
+        out_shape=jax.ShapeDtypeStruct(
+            (tile_count, plane_count, pairs, fields, sliver, 2 * bphi), blocks.dtype
+        ),
+        grid_spec=pltpu.PrefetchScalarGridSpec(
+            num_scalar_prefetch=1,
+            grid=(tile_count, pairs),
+            in_specs=[
+                pl.BlockSpec(memory_space=pltpu.SMEM),
+                pl.BlockSpec((1, fields, bphi, cols), block_map(0)),
+                pl.BlockSpec((1, fields, bphi, cols), block_map(1)),
+            ],
+            out_specs=pl.BlockSpec(
+                (1, plane_count, 1, fields, sliver, 2 * bphi),
+                lambda t, q, src_ref: (t, 0, q, 0, 0, 0),
+            ),
+        ),
+    )(source, scale, blocks, blocks)
+
+
+def unpack_kernel(groups, row_ref, half_ref, *refs):
+    out_ref = refs[-1]
+    segment = pl.program_id(0)
+    quad = pl.program_id(1)
+    lanes = out_ref.shape[-1]
+    shape = out_ref.shape[:1] + out_ref.shape[2:]
+    lane = lax.broadcasted_iota(jnp.int32, shape, 2)
+    for group in range(groups):
+        parts = []
+        for side in range(2):
+            index = ((segment * 2 * pl.num_programs(1) + quad * 2 + side) * groups) + group
+            piece = refs[group * 2 + side][0].astype(jnp.float32)
+            turned = pltpu.roll(piece, lanes // 2, 2)
+            keep = half_ref[index] == side
+            parts.append(jnp.where(keep, piece, turned))
+        merged = jnp.where(lane < lanes // 2, parts[0], parts[1])
+        out_ref[:, group] = merged.astype(out_ref.dtype)
+
+
+def unpack_lhs(landed, row, half, plane_count, per_plane, groups):
+    _, fields, sliver, lanes = landed.shape
+    quads = per_plane // 2
+
+    def piece_map(side, group):
+        def index_map(s, q, row_ref, half_ref):
+            return (row_ref[((s * per_plane + q * 2 + side) * groups) + group], 0, 0, 0)
+
+        return index_map
+
+    in_specs = [
+        pl.BlockSpec((1, fields, sliver, lanes), piece_map(side, group))
+        for group in range(groups)
+        for side in range(2)
+    ]
+    return pl.pallas_call(
+        functools.partial(unpack_kernel, groups),
+        out_shape=jax.ShapeDtypeStruct(
+            (fields, groups, sliver, plane_count * per_plane * lanes // 2), landed.dtype
+        ),
+        grid_spec=pltpu.PrefetchScalarGridSpec(
+            num_scalar_prefetch=2,
+            grid=(plane_count, quads),
+            in_specs=in_specs,
+            out_specs=pl.BlockSpec(
+                (fields, groups, sliver, lanes),
+                lambda s, q, row_ref, half_ref: (0, 0, 0, s * quads + q),
+            ),
+        ),
+    )(row, half, *([landed] * (2 * groups)))
+
+
 def local(blocks, levels, block_dest, block_phi, block_group):
     tile_count = lax.axis_size("tile")
     plane_count = lax.axis_size("phi")
@@ -37,7 +139,6 @@
     per_plane = NPHI // BPHI // plane_count
     capacity = 2 * slot_count // tile_count
     sliver = COLS // plane_count
-    weight = (1.0 / jnp.left_shift(1, levels).astype(jnp.float32)).astype(jnp.bfloat16)
 
     onehot_dest = (block_dest[:, None] == jnp.arange(tile_count, dtype=jnp.int32)[None, :]).astype(
         jnp.int32
@@ -49,13 +150,13 @@
     filled = jnp.any(match, axis=1)
     source = jnp.argmax(match, axis=1).astype(jnp.int32)
     place = block_phi[source] * CG_DEV + block_group[source]
-    code = jnp.where(filled, levels[source] * slot_count + place, -1)
+    code = jnp.where(filled, place, -1)
+    scale = 1.0 / jnp.left_shift(1, levels[source]).astype(jnp.float32)
     device_count = tile_count * plane_count
+    pairs = capacity // 2
 
-    outbox = blocks[source].reshape(tile_count, capacity, fields, BPHI, plane_count, sliver)
-    outbox = jnp.transpose(outbox, (0, 4, 1, 2, 3, 5)).reshape(
-        device_count, capacity, fields, BPHI, sliver
-    )
+    outbox = pack_outbox(blocks, source, scale, tile_count, capacity, plane_count)
+    outbox = outbox.reshape(device_count, pairs * fields * sliver, 2 * BPHI)
     code_out = jnp.broadcast_to(
         code.reshape(tile_count, 1, capacity), (tile_count, plane_count, capacity)
     ).reshape(device_count, capacity)
@@ -66,22 +167,17 @@
         arrived_code.reshape(tile_count, plane_count, capacity), (1, 0, 2)
     ).reshape(plane_count, tile_count * capacity)
     want = jnp.arange(slot_count, dtype=jnp.int32)
-    hit = (by_segment[:, None, :] % slot_count == want[None, :, None]) & (
-        by_segment[:, None, :] >= 0
-    )
+    hit = by_segment[:, None, :] == want[None, :, None]
     pick = jnp.argmax(hit, axis=2).astype(jnp.int32)
     origin = pick // capacity
     segment = jnp.arange(plane_count, dtype=jnp.int32)[:, None]
-    flat = (origin * plane_count + segment) * capacity + pick % capacity
-    level_of = jnp.take_along_axis(by_segment, pick, axis=1) // slot_count
-    weight = (1.0 / jnp.left_shift(1, level_of).astype(jnp.float32)).astype(jnp.bfloat16)
-    gathered = arrived.reshape(device_count * capacity, fields, BPHI, sliver)[flat.reshape(-1)]
-    gathered = gathered * weight.reshape(-1)[:, None, None, None]
-    gathered = gathered.reshape(plane_count, per_plane, CG_DEV, fields, BPHI, sliver)
-    pieces = jnp.transpose(gathered, (0, 1, 4, 3, 2, 5)).reshape(NPHI, fields, CG_DEV * sliver)
+    row = ((origin * plane_count + segment) * pairs + (pick % capacity) // 2).reshape(-1)
+    half = (pick % 2).reshape(-1)
+    landed = arrived.reshape(device_count * pairs, fields, sliver, 2 * BPHI)
+    lhs = unpack_lhs(landed, row, half, plane_count, per_plane, CG_DEV)
     basis = dft_basis(NPHI)
-    spectra = lax.dot_general(
-        pieces, basis, (((0,), (0,)), ((), ())), preferred_element_type=jnp.float32
+    spectra = jnp.dot(
+        lhs.reshape(fields * CG_DEV * sliver, NPHI), basis, preferred_element_type=jnp.float32
     )
     return spectra.reshape(fields, CG_DEV, sliver, NPHI)
 

time: 344 us -> 223 us (0.65)
  local copies, waits for them, and re-layouts: 159 us -> 5.9 us
  Pallas kernels: 0 us -> 37.9 us
  waiting for transfers between devices: 124 us -> 114 us
  other arithmetic: 20.4 us -> 25.7 us
    unnamed x6, local copies, waits for them, and re-layouts: 62.3 us -> 0.01 us
    gather x7 -> x1, local copies, waits for them, and re-layouts: 48.8 us -> 1.43 us  [local(): scale = 1.0 / jnp.left_shift(1, levels[source]).astype(jnp.float32)]
    pallas_call x0 -> x2, Pallas kernels: none -> 37.9 us  [the longest x1 22.7 us: pack_outbox(): pl.pallas_call(pack_kernel, out_shape=jax.ShapeDtypeStruct((tile_count, p...]
    transpose x2 -> x0, local copies, waits for them, and re-layouts: 27.3 us -> none  [the longest x1 19.3 us: local(): jnp.transpose(outbox, (0, 4, 1, 2, 3, 5))]
    reshape x2, local copies, waits for them, and re-layouts: 17.2 us -> 1.31 us  [the longest x1 0.65 us: local(): half = (pick % 2).reshape(-1)]
    all_to_all x1, waiting for transfers between devices: 124 us -> 114 us  [local(): lax.all_to_all(outbox, ('tile', 'phi'), split_axis=0, concat_axis=0, tile...]
    sub x0 -> x1, other arithmetic: none -> 7.04 us  [dft_basis(): values = jnp.where(is_cos, ch * cl - sh * sl, sh * cl + ch * sl)]
    transpose x1 -> x0, other arithmetic: 6.1 us -> none  [local(): jnp.transpose(gathered, (0, 1, 4, 3, 2, 5))]
  transfers between devices with their start and end apart: 2 -> 2, of which waited for: 1 -> 1; matrix products, arithmetic and copies ran while one was open for 27% -> 12% of each run, Pallas kernels for 0% -> 10%
where the time goes in v4:
time: 223 us; the launch traced here: 221 us
  waiting for transfers between devices  114 us (51%)
  Pallas kernels  37.9 us (17%)
  other arithmetic  25.7 us (12%)
  starting transfers between devices  20.7 us (9%)
  matrix products  17.4 us (8%)
  local copies, waits for them, and re-layouts  5.9 us (3%)
    all_to_all x1, waiting for transfers between devices, local(): lax.all_to_all(outbox, ('tile', 'phi'), split_axis=0, concat_axis=0, tile...  114 us
    pallas_call x1, Pallas kernels, pack_outbox(): pl.pallas_call(pack_kernel, out_shape=jax.ShapeDtypeStruct((tile_count, p...  22.7 us
    dot_general x1, matrix products, local(): jnp.dot(lhs.reshape(fields * CG_DEV * sliver, NPHI), basis, preferred_ele...  17.4 us
    pallas_call x1, Pallas kernels, unpack_lhs(): pl.pallas_call(functools.partial(unpack_kernel, groups), out_shape=jax.Sh...  15.2 us
    convert_element_type x1, other arithmetic, dft_basis(): return values.reshape(length, length).astype(jnp.bfloat16)  10.9 us
    all_to_all x1, starting transfers between devices, local(): lax.all_to_all(outbox, ('tile', 'phi'), split_axis=0, concat_axis=0, tile...  10.5 us
    all_to_all x1, starting transfers between devices, local(): lax.all_to_all(code_out, ('tile', 'phi'), split_axis=0, concat_axis=0, ti...  10.2 us
    sub x1, other arithmetic, dft_basis(): values = jnp.where(is_cos, ch * cl - sh * sl, sh * cl + ch * sl)  7.04 us
  transfers between devices with their start and end apart: 2, of which 1 were waited for; matrix products, arithmetic and copies ran while one was open for 12% of the time, Pallas kernels for 10%

profile of v4, /device:TPU:97, one launch (start us, length us, event | category | flops | bytes accessed | tf_op | source)
XLA Modules:
  0.0 221.4 jit_solution(6683506009121462766)
XLA Ops:
  0.0 0.0 copy-start
  0.0 0.7 fusion.18
  0.7 0.1 reduce_window_sum.11
  0.8 0.8 select_reduce_fusion
  1.6 0.7 multiply_add_fusion.1
  2.3 0.1 fusion.17
  2.4 0.6 iota_reduce_fusion.1
  3.0 0.0 copy-done
  3.0 0.8 gather_fusion.1
  3.8 1.4 gather_fusion
  5.2 0.1 select_n.86
  5.3 0.6 broadcast_in_dim.15.clone
  6.0 10.2 %all-to-all-start = ((s32[128,1,4]{2,1,0:T(1,128)}), s32[128,1,4]{2,1,0:T(1,128)S(1)}, u32[]{:S(2)}, u32[]{:S(2)}) async-start(s32[128,1,4]{2,1,0:T(1,128)} %bitcast), calls=%async_computation | async-start | bytes 131072 | tf_op jit(solution)/shard_map/all_to_all | solution.py:164
  16.1 1.4 gather_fusion.2
  17.6 0.5 convert_divide_fusion.scale_ref
  18.1 0.0 copy-done.2
  18.1 22.7 %shard_map.55 = bf16[16,8,2,5,32,128]{5,4,3,2,1,0:T(8,128)(2,1)} custom-call(s32[64]{0:T(128)} %copy-done.2, f32[64]{0:T(128)} %convert_divide_fusion.scale_ref, bf16[32,5,64,256]{3,2,1,0:T(8,128)(2,1)} %second_ref.1, bf16[32,5,64,256]{3,2,1,0:T(8,128)(2,1)} %second_ref.1), custom_call_target="tpu_custom_call" | custom-call | tf_op jit(solution)/shard_map/pallas_call | solution.py:62
  40.8 0.0 all-to-all-done
  40.8 10.5 %all-to-all-start.1 = ((bf16[128,320,128]{2,1,0:T(8,128)(2,1)}), bf16[128,320,128]{2,1,0:T(8,128)(2,1)}, u32[]{:S(2)}, u32[]{:S(2)}) async-start(bf16[128,320,128]{2,1,0:T(8,128)(2,1)} %bitcast.22), calls=%async_computation.1 | async-start | bytes 20971520 | tf_op jit(solution)/shard_map/all_to_all | solution.py:163
  51.4 1.1 fusion.16
  52.5 2.0 fusion.14
  54.5 7.0 %multiply_subtract_fusion = (f32[32,64,2048]{2,1,0:T(8,128)S(1)}, f32[32,64,2048]{2,1,0:T(8,128)}) fusion(f32[64,2048]{1,0:T(8,128)S(1)} %get-tuple-element.14, f32[32,2048]{1,0:T(8,128)S(1)} %get-tuple-element.12, f32[64,2048]{1,0:T(8,128)S(1)} %get-tuple-element.13, f32[32,2048]{1,0:T(8,128)S(1)} %get-tuple-element.11), kind=kLoop, calls=%fused_computation.7 | loop fusion | flops 25165824 | bytes 35127296 | tf_op jit(solution)/shard_map/sub | solution.py:30
  61.6 10.9 %fusion.1 = bf16[2048,2048]{1,0:T(8,128)(2,1)} fusion(f32[32,64,2048]{2,1,0:T(8,128)} %get-tuple-element.10, f32[32,64,2048]{2,1,0:T(8,128)S(1)} %get-tuple-element.9, pred[2048]{0:T(1024)(128)(4,1)S(1)} %iota_compare_fusion.3), kind=kLoop, calls=%fused_computation.5 | loop fusion | flops 12582912 | bytes 41945088 | tf_op jit(solution)/shard_map/convert_element_type | solution.py:32
  72.5 0.2 copy.21
  72.7 0.1 copy.22
  72.7 1.0 iota_reduce_fusion
  73.7 0.7 reshape.208.half_ref
  74.4 0.7 reshape.207.row_ref
  75.0 113.8 %all-to-all-done.1 = bf16[128,320,128]{2,1,0:T(8,128)(2,1)} async-done(((bf16[128,320,128]{2,1,0:T(8,128)(2,1)}), bf16[128,320,128]{2,1,0:T(8,128)(2,1)}, u32[]{:S(2)}, u32[]{:S(2)}) %all-to-all-start.1) | async-done | bytes 10485792 | tf_op jit(solution)/shard_map/all_to_all | solution.py:163
  188.8 15.2 %shard_map.56 = bf16[5,8,32,2048]{3,2,1,0:T(8,128)(2,1)} custom-call(s32[256]{0:T(256)} %reshape.207.row_ref, s32[256]{0:T(256)} %reshape.208.half_ref, bf16[256,5,32,128]{3,2,1,0:T(8,128)(2,1)} %bitcast.6.refs_0_.refs_1_.refs_2_.refs_3_.refs_4_.refs_5_.refs_6_.refs_7_.refs_8_.refs_9_.refs_10_.refs_11_.refs_12_.refs_13_.refs_14_.refs_15_, ...), custom_call_target="tpu_custom_call" | custom-call | tf_op jit(solution)/shard_map/pallas_call | solution.py:117
  204.0 17.4 %fusion.2 = f32[5,8,32,2048]{3,2,1,0:T(8,128)} fusion(bf16[5,8,32,2048]{3,2,1,0:T(8,128)(2,1)} %shard_map.56, bf16[2048,2048]{1,0:T(8,128)(2,1)} %fusion.1), kind=kOutput, calls=%fused_computation.8 | convolution fusion | flops 10737418240 | bytes 24117248 | tf_op jit(solution)/shard_map/dot_general | solution.py:179
  221.4 0.0 copy-done.1
  (9 shorter events, 0.1 us)
Async XLA Ops:
  0.0 3.0 %copy-start = (s32[32]{0:T(128)S(1)}, s32[32]{0:T(128)}, u32[]{:S(2)}) copy-start(s32[32]{0:T(128)} %param.9) | copy-start | bytes 388
  3.0 15.1 %copy-start.2 = (s32[64]{0:T(128)}, s32[64]{0:T(128)S(1)}, u32[]{:S(2)}) copy-start(s32[64]{0:T(128)S(1)} %get-tuple-element.7.source_ref) | copy-start | bytes 772
  6.0 34.8 %all-to-all-start = ((s32[128,1,4]{2,1,0:T(1,128)}), s32[128,1,4]{2,1,0:T(1,128)S(1)}, u32[]{:S(2)}, u32[]{:S(2)}) async-start(s32[128,1,4]{2,1,0:T(1,128)} %bitcast), calls=%async_computation | async-start | bytes 131072 | tf_op jit(solution)/shard_map/all_to_all | solution.py:164
  40.8 148.0 %all-to-all-start.1 = ((bf16[128,320,128]{2,1,0:T(8,128)(2,1)}), bf16[128,320,128]{2,1,0:T(8,128)(2,1)}, u32[]{:S(2)}, u32[]{:S(2)}) async-start(bf16[128,320,128]{2,1,0:T(8,128)(2,1)} %bitcast.22), calls=%async_computation.1 | async-start | bytes 20971520 | tf_op jit(solution)/shard_map/all_to_all | solution.py:163
  188.8 32.6 %copy-start.1 = (s32[32]{0:T(128)S(1)}, s32[32]{0:T(128)}, u32[]{:S(2)}) copy-start(s32[32]{0:T(128)} %param.9) | copy-start | bytes 388

commit v5 on v4

--- a/solution.py
+++ b/solution.py
@@ -36,14 +36,14 @@
     tile = pl.program_id(0)
     pair = pl.program_id(1)
     slot = (tile * pl.num_programs(1) + pair) * 2
-    first_scale = scale_ref[slot]
-    second_scale = scale_ref[slot + 1]
+    first_scale = scale_ref[slot].astype(first_ref.dtype)
+    second_scale = scale_ref[slot + 1].astype(first_ref.dtype)
     fields, planes, sliver = out_ref.shape[3], out_ref.shape[1], out_ref.shape[4]
     for field in range(fields):
         both = jnp.concatenate(
             [
-                first_ref[0, field].astype(jnp.float32) * first_scale,
-                second_ref[0, field].astype(jnp.float32) * second_scale,
+                first_ref[0, field] * first_scale,
+                second_ref[0, field] * second_scale,
             ],
             axis=0,
         )
@@ -91,7 +91,7 @@
         parts = []
         for side in range(2):
             index = ((segment * 2 * pl.num_programs(1) + quad * 2 + side) * groups) + group
-            piece = refs[group * 2 + side][0].astype(jnp.float32)
+            piece = refs[group * 2 + side][0]
             turned = pltpu.roll(piece, lanes // 2, 2)
             keep = half_ref[index] == side
             parts.append(jnp.where(keep, piece, turned))

time: 223 us -> 222 us (level)
  no operation moved by 1% of the time
where the time goes in v5:
time: 222 us; the launch traced here: 220 us
  waiting for transfers between devices  114 us (51%)
  Pallas kernels  36.6 us (16%)
  other arithmetic  25.7 us (12%)
  starting transfers between devices  20.6 us (9%)
  matrix products  17.4 us (8%)
  local copies, waits for them, and re-layouts  5.9 us (3%)
    all_to_all x1, waiting for transfers between devices, local(): lax.all_to_all(outbox, ('tile', 'phi'), split_axis=0, concat_axis=0, tile...  114 us
    pallas_call x1, Pallas kernels, pack_outbox(): pl.pallas_call(pack_kernel, out_shape=jax.ShapeDtypeStruct((tile_count, p...  22.3 us
    dot_general x1, matrix products, local(): jnp.dot(lhs.reshape(fields * CG_DEV * sliver, NPHI), basis, preferred_ele...  17.4 us
    pallas_call x1, Pallas kernels, unpack_lhs(): pl.pallas_call(functools.partial(unpack_kernel, groups), out_shape=jax.Sh...  14.3 us
    convert_element_type x1, other arithmetic, dft_basis(): return values.reshape(length, length).astype(jnp.bfloat16)  10.9 us
    all_to_all x1, starting transfers between devices, local(): lax.all_to_all(outbox, ('tile', 'phi'), split_axis=0, concat_axis=0, tile...  10.4 us
    all_to_all x1, starting transfers between devices, local(): lax.all_to_all(code_out, ('tile', 'phi'), split_axis=0, concat_axis=0, ti...  10.2 us
    sub x1, other arithmetic, dft_basis(): values = jnp.where(is_cos, ch * cl - sh * sl, sh * cl + ch * sl)  7.04 us
  transfers between devices with their start and end apart: 2, of which 1 were waited for; matrix products, arithmetic and copies ran while one was open for 12% of the time, Pallas kernels for 10%

profile of v5, /device:TPU:97, one launch (start us, length us, event | category | flops | bytes accessed | tf_op | source)
XLA Modules:
  0.0 220.0 jit_solution(2703869897883646525)
XLA Ops:
  0.0 0.0 copy-start
  0.0 0.7 fusion.18
  0.7 0.1 reduce_window_sum.11
  0.8 0.8 select_reduce_fusion
  1.6 0.7 multiply_add_fusion.1
  2.3 0.1 fusion.17
  2.4 0.6 iota_reduce_fusion.1
  3.0 0.0 copy-done
  3.0 0.8 gather_fusion.1
  3.8 1.4 gather_fusion
  5.2 0.1 select_n.86
  5.3 0.6 broadcast_in_dim.15.clone
  6.0 10.2 %all-to-all-start = ((s32[128,1,4]{2,1,0:T(1,128)}), s32[128,1,4]{2,1,0:T(1,128)S(1)}, u32[]{:S(2)}, u32[]{:S(2)}) async-start(s32[128,1,4]{2,1,0:T(1,128)} %bitcast), calls=%async_computation | async-start | bytes 131072 | tf_op jit(solution)/shard_map/all_to_all | solution.py:164
  16.1 1.4 gather_fusion.2
  17.6 0.5 convert_divide_fusion.scale_ref
  18.1 0.0 copy-done.2
  18.1 22.3 %shard_map.55 = bf16[16,8,2,5,32,128]{5,4,3,2,1,0:T(8,128)(2,1)} custom-call(s32[64]{0:T(128)} %copy-done.2, f32[64]{0:T(128)} %convert_divide_fusion.scale_ref, bf16[32,5,64,256]{3,2,1,0:T(8,128)(2,1)} %second_ref.1, bf16[32,5,64,256]{3,2,1,0:T(8,128)(2,1)} %second_ref.1), custom_call_target="tpu_custom_call" | custom-call | tf_op jit(solution)/shard_map/pallas_call | solution.py:62
  40.4 0.0 all-to-all-done
  40.4 10.4 %all-to-all-start.1 = ((bf16[128,320,128]{2,1,0:T(8,128)(2,1)}), bf16[128,320,128]{2,1,0:T(8,128)(2,1)}, u32[]{:S(2)}, u32[]{:S(2)}) async-start(bf16[128,320,128]{2,1,0:T(8,128)(2,1)} %bitcast.22), calls=%async_computation.1 | async-start | bytes 20971520 | tf_op jit(solution)/shard_map/all_to_all | solution.py:163
  50.8 1.1 fusion.16
  51.9 2.0 fusion.14
  54.0 7.0 %multiply_subtract_fusion = (f32[32,64,2048]{2,1,0:T(8,128)S(1)}, f32[32,64,2048]{2,1,0:T(8,128)}) fusion(f32[64,2048]{1,0:T(8,128)S(1)} %get-tuple-element.14, f32[32,2048]{1,0:T(8,128)S(1)} %get-tuple-element.12, f32[64,2048]{1,0:T(8,128)S(1)} %get-tuple-element.13, f32[32,2048]{1,0:T(8,128)S(1)} %get-tuple-element.11), kind=kLoop, calls=%fused_computation.7 | loop fusion | flops 25165824 | bytes 35127296 | tf_op jit(solution)/shard_map/sub | solution.py:30
  61.0 10.9 %fusion.1 = bf16[2048,2048]{1,0:T(8,128)(2,1)} fusion(f32[32,64,2048]{2,1,0:T(8,128)} %get-tuple-element.10, f32[32,64,2048]{2,1,0:T(8,128)S(1)} %get-tuple-element.9, pred[2048]{0:T(1024)(128)(4,1)S(1)} %iota_compare_fusion.3), kind=kLoop, calls=%fused_computation.5 | loop fusion | flops 12582912 | bytes 41945088 | tf_op jit(solution)/shard_map/convert_element_type | solution.py:32
  72.0 0.2 copy.21
  72.1 0.1 copy.22
  72.2 1.0 iota_reduce_fusion
  73.2 0.7 reshape.208.half_ref
  73.8 0.7 reshape.207.row_ref
  74.5 113.8 %all-to-all-done.1 = bf16[128,320,128]{2,1,0:T(8,128)(2,1)} async-done(((bf16[128,320,128]{2,1,0:T(8,128)(2,1)}), bf16[128,320,128]{2,1,0:T(8,128)(2,1)}, u32[]{:S(2)}, u32[]{:S(2)}) %all-to-all-start.1) | async-done | bytes 10485792 | tf_op jit(solution)/shard_map/all_to_all | solution.py:163
  188.3 14.3 %shard_map.56 = bf16[5,8,32,2048]{3,2,1,0:T(8,128)(2,1)} custom-call(s32[256]{0:T(256)} %reshape.207.row_ref, s32[256]{0:T(256)} %reshape.208.half_ref, bf16[256,5,32,128]{3,2,1,0:T(8,128)(2,1)} %bitcast.6.refs_0_.refs_1_.refs_2_.refs_3_.refs_4_.refs_5_.refs_6_.refs_7_.refs_8_.refs_9_.refs_10_.refs_11_.refs_12_.refs_13_.refs_14_.refs_15_, ...), custom_call_target="tpu_custom_call" | custom-call | tf_op jit(solution)/shard_map/pallas_call | solution.py:117
  202.7 17.4 %fusion.2 = f32[5,8,32,2048]{3,2,1,0:T(8,128)} fusion(bf16[5,8,32,2048]{3,2,1,0:T(8,128)(2,1)} %shard_map.56, bf16[2048,2048]{1,0:T(8,128)(2,1)} %fusion.1), kind=kOutput, calls=%fused_computation.8 | convolution fusion | flops 10737418240 | bytes 24117248 | tf_op jit(solution)/shard_map/dot_general | solution.py:179
  220.0 0.0 copy-done.1
  (9 shorter events, 0.1 us)
Async XLA Ops:
  0.0 3.0 %copy-start = (s32[32]{0:T(128)S(1)}, s32[32]{0:T(128)}, u32[]{:S(2)}) copy-start(s32[32]{0:T(128)} %param.9) | copy-start | bytes 388
  3.0 15.1 %copy-start.2 = (s32[64]{0:T(128)}, s32[64]{0:T(128)S(1)}, u32[]{:S(2)}) copy-start(s32[64]{0:T(128)S(1)} %get-tuple-element.7.source_ref) | copy-start | bytes 772
  6.0 34.4 %all-to-all-start = ((s32[128,1,4]{2,1,0:T(1,128)}), s32[128,1,4]{2,1,0:T(1,128)S(1)}, u32[]{:S(2)}, u32[]{:S(2)}) async-start(s32[128,1,4]{2,1,0:T(1,128)} %bitcast), calls=%async_computation | async-start | bytes 131072 | tf_op jit(solution)/shard_map/all_to_all | solution.py:164
  40.4 147.9 %all-to-all-start.1 = ((bf16[128,320,128]{2,1,0:T(8,128)(2,1)}), bf16[128,320,128]{2,1,0:T(8,128)(2,1)}, u32[]{:S(2)}, u32[]{:S(2)}) async-start(bf16[128,320,128]{2,1,0:T(8,128)(2,1)} %bitcast.22), calls=%async_computation.1 | async-start | bytes 20971520 | tf_op jit(solution)/shard_map/all_to_all | solution.py:163
  188.3 31.7 %copy-start.1 = (s32[32]{0:T(128)S(1)}, s32[32]{0:T(128)}, u32[]{:S(2)}) copy-start(s32[32]{0:T(128)} %param.9) | copy-start | bytes 388

commit v6 on v5

--- a/solution.py
+++ b/solution.py
@@ -32,23 +32,25 @@
     return values.reshape(length, length).astype(jnp.bfloat16)
 
 
-def pack_kernel(source_ref, scale_ref, first_ref, second_ref, out_ref):
+def pack_kernel(source_ref, scale_ref, *refs):
+    out_ref = refs[-1]
+    slots = len(refs) - 1
     tile = pl.program_id(0)
-    pair = pl.program_id(1)
-    slot = (tile * pl.num_programs(1) + pair) * 2
-    first_scale = scale_ref[slot].astype(first_ref.dtype)
-    second_scale = scale_ref[slot + 1].astype(first_ref.dtype)
     fields, planes, sliver = out_ref.shape[3], out_ref.shape[1], out_ref.shape[4]
-    for field in range(fields):
-        both = jnp.concatenate(
-            [
-                first_ref[0, field] * first_scale,
-                second_ref[0, field] * second_scale,
-            ],
-            axis=0,
-        )
-        flipped = both.T.reshape(planes, sliver, both.shape[0])
-        out_ref[0, :, 0, field] = flipped.astype(out_ref.dtype)
+    for pair in range(slots // 2):
+        first = tile * slots + 2 * pair
+        first_scale = scale_ref[first].astype(out_ref.dtype)
+        second_scale = scale_ref[first + 1].astype(out_ref.dtype)
+        for field in range(fields):
+            both = jnp.concatenate(
+                [
+                    refs[2 * pair][0, field] * first_scale,
+                    refs[2 * pair + 1][0, field] * second_scale,
+                ],
+                axis=0,
+            )
+            flipped = both.T.reshape(planes, sliver, both.shape[0])
+            out_ref[0, :, pair, field] = flipped.astype(out_ref.dtype)
 
 
 def pack_outbox(blocks, source, scale, tile_count, capacity, plane_count):
@@ -56,8 +58,8 @@
     pairs = capacity // 2
     sliver = cols // plane_count
 
-    def block_map(half):
-        return lambda t, q, src_ref: (src_ref[(t * pairs + q) * 2 + half], 0, 0, 0)
+    def block_map(slot):
+        return lambda t, src_ref: (src_ref[t * capacity + slot], 0, 0, 0)
 
     return pl.pallas_call(
         pack_kernel,
@@ -66,69 +68,64 @@
         ),
         grid_spec=pltpu.PrefetchScalarGridSpec(
             num_scalar_prefetch=1,
-            grid=(tile_count, pairs),
-            in_specs=[
-                pl.BlockSpec(memory_space=pltpu.SMEM),
-                pl.BlockSpec((1, fields, bphi, cols), block_map(0)),
-                pl.BlockSpec((1, fields, bphi, cols), block_map(1)),
-            ],
+            grid=(tile_count,),
+            in_specs=[pl.BlockSpec(memory_space=pltpu.SMEM)]
+            + [pl.BlockSpec((1, fields, bphi, cols), block_map(slot)) for slot in range(capacity)],
             out_specs=pl.BlockSpec(
-                (1, plane_count, 1, fields, sliver, 2 * bphi),
-                lambda t, q, src_ref: (t, 0, q, 0, 0, 0),
+                (1, plane_count, pairs, fields, sliver, 2 * bphi),
+                lambda t, src_ref: (t, 0, 0, 0, 0, 0),
             ),
         ),
-    )(source, scale, blocks, blocks)
+    )(source, scale, *([blocks] * capacity))
 
 
-def unpack_kernel(groups, row_ref, half_ref, *refs):
+def unpack_kernel(groups, per_plane, row_ref, half_ref, *refs):
     out_ref = refs[-1]
     segment = pl.program_id(0)
-    quad = pl.program_id(1)
-    lanes = out_ref.shape[-1]
-    shape = out_ref.shape[:1] + out_ref.shape[2:]
+    lanes = refs[0].shape[-1]
+    shape = refs[0].shape[1:]
     lane = lax.broadcasted_iota(jnp.int32, shape, 2)
     for group in range(groups):
-        parts = []
-        for side in range(2):
-            index = ((segment * 2 * pl.num_programs(1) + quad * 2 + side) * groups) + group
-            piece = refs[group * 2 + side][0]
-            turned = pltpu.roll(piece, lanes // 2, 2)
-            keep = half_ref[index] == side
-            parts.append(jnp.where(keep, piece, turned))
-        merged = jnp.where(lane < lanes // 2, parts[0], parts[1])
-        out_ref[:, group] = merged.astype(out_ref.dtype)
+        for quad in range(per_plane // 2):
+            parts = []
+            for side in range(2):
+                position = quad * 2 + side
+                index = (segment * per_plane + position) * groups + group
+                piece = refs[position * groups + group][0]
+                turned = pltpu.roll(piece, lanes // 2, 2)
+                keep = half_ref[index] == side
+                parts.append(jnp.where(keep, piece, turned))
+            merged = jnp.where(lane < lanes // 2, parts[0], parts[1])
+            out_ref[:, group, :, quad * lanes : (quad + 1) * lanes] = merged.astype(out_ref.dtype)
 
 
 def unpack_lhs(landed, row, half, plane_count, per_plane, groups):
     _, fields, sliver, lanes = landed.shape
-    quads = per_plane // 2
 
-    def piece_map(side, group):
-        def index_map(s, q, row_ref, half_ref):
-            return (row_ref[((s * per_plane + q * 2 + side) * groups) + group], 0, 0, 0)
+    def piece_map(position, group):
+        def index_map(s, row_ref, half_ref):
+            return (row_ref[(s * per_plane + position) * groups + group], 0, 0, 0)
 
         return index_map
 
     in_specs = [
-        pl.BlockSpec((1, fields, sliver, lanes), piece_map(side, group))
+        pl.BlockSpec((1, fields, sliver, lanes), piece_map(position, group))
+        for position in range(per_plane)
         for group in range(groups)
-        for side in range(2)
     ]
+    width = per_plane * lanes // 2
     return pl.pallas_call(
-        functools.partial(unpack_kernel, groups),
-        out_shape=jax.ShapeDtypeStruct(
-            (fields, groups, sliver, plane_count * per_plane * lanes // 2), landed.dtype
-        ),
+        functools.partial(unpack_kernel, groups, per_plane),
+        out_shape=jax.ShapeDtypeStruct((fields, groups, sliver, plane_count * width), landed.dtype),
         grid_spec=pltpu.PrefetchScalarGridSpec(
             num_scalar_prefetch=2,
-            grid=(plane_count, quads),
+            grid=(plane_count,),
             in_specs=in_specs,
             out_specs=pl.BlockSpec(
-                (fields, groups, sliver, lanes),
-                lambda s, q, row_ref, half_ref: (0, 0, 0, s * quads + q),
+                (fields, groups, sliver, width), lambda s, row_ref, half_ref: (0, 0, 0, s)
             ),
         ),
-    )(row, half, *([landed] * (2 * groups)))
+    )(row, half, *([landed] * (per_plane * groups)))
 
 
 def local(blocks, levels, block_dest, block_phi, block_group):

time: 222 us -> 212 us (0.955)
  Pallas kernels: 36.6 us -> 27.6 us
    pallas_call x1, Pallas kernels: 22.3 us -> 15.4 us  [pack_outbox(): pl.pallas_call(pack_kernel, out_shape=jax.ShapeDtypeStruct((tile_count, p...]
  transfers between devices with their start and end apart: 2 -> 2, of which waited for: 1 -> 1; matrix products, arithmetic and copies ran while one was open for 12% -> 12% of each run, Pallas kernels for 10% -> 7%
where the time goes in v6:
time: 212 us; the launch traced here: 211 us
  waiting for transfers between devices  114 us (54%)
  Pallas kernels  27.6 us (13%)
  other arithmetic  25.7 us (12%)
  starting transfers between devices  20.3 us (10%)
  matrix products  17.4 us (8%)
  local copies, waits for them, and re-layouts  5.9 us (3%)
    all_to_all x1, waiting for transfers between devices, local(): lax.all_to_all(outbox, ('tile', 'phi'), split_axis=0, concat_axis=0, tile...  114 us
    dot_general x1, matrix products, local(): jnp.dot(lhs.reshape(fields * CG_DEV * sliver, NPHI), basis, preferred_ele...  17.4 us
    pallas_call x1, Pallas kernels, pack_outbox(): pl.pallas_call(pack_kernel, out_shape=jax.ShapeDtypeStruct((tile_count, p...  15.4 us
    pallas_call x1, Pallas kernels, unpack_lhs(): pl.pallas_call(functools.partial(unpack_kernel, groups, per_plane), out_s...  12.2 us
    convert_element_type x1, other arithmetic, dft_basis(): return values.reshape(length, length).astype(jnp.bfloat16)  10.9 us
    all_to_all x1, starting transfers between devices, local(): lax.all_to_all(code_out, ('tile', 'phi'), split_axis=0, concat_axis=0, ti...  10.2 us
    all_to_all x1, starting transfers between devices, local(): lax.all_to_all(outbox, ('tile', 'phi'), split_axis=0, concat_axis=0, tile...  10.1 us
    sub x1, other arithmetic, dft_basis(): values = jnp.where(is_cos, ch * cl - sh * sl, sh * cl + ch * sl)  7.04 us
  transfers between devices with their start and end apart: 2, of which 1 were waited for; matrix products, arithmetic and copies ran while one was open for 12% of the time, Pallas kernels for 7%

profile of v6, /device:TPU:97, one launch (start us, length us, event | category | flops | bytes accessed | tf_op | source)
XLA Modules:
  0.0 210.7 jit_solution(8748845383837959689)
XLA Ops:
  0.0 0.0 copy-start
  0.0 0.7 fusion.18
  0.7 0.1 reduce_window_sum.11
  0.8 0.8 select_reduce_fusion
  1.6 0.7 multiply_add_fusion.1
  2.3 0.1 fusion.17
  2.4 0.6 iota_reduce_fusion.1
  3.0 0.0 copy-done
  3.0 0.8 gather_fusion.1
  3.8 1.4 gather_fusion
  5.2 0.1 select_n.86
  5.3 0.6 broadcast_in_dim.15.clone
  6.0 10.2 %all-to-all-start = ((s32[128,1,4]{2,1,0:T(1,128)}), s32[128,1,4]{2,1,0:T(1,128)S(1)}, u32[]{:S(2)}, u32[]{:S(2)}) async-start(s32[128,1,4]{2,1,0:T(1,128)} %bitcast), calls=%async_computation | async-start | bytes 131072 | tf_op jit(solution)/shard_map/all_to_all | solution.py:161
  16.1 1.4 gather_fusion.2
  17.6 0.5 convert_divide_fusion.scale_ref
  18.1 0.0 copy-done.2
  18.1 15.4 %shard_map.55 = bf16[16,8,2,5,32,128]{5,4,3,2,1,0:T(8,128)(2,1)} custom-call(s32[64]{0:T(128)} %copy-done.2, f32[64]{0:T(128)} %convert_divide_fusion.scale_ref, bf16[32,5,64,256]{3,2,1,0:T(8,128)(2,1)} %refs_3_.1, bf16[32,5,64,256]{3,2,1,0:T(8,128)(2,1)} %refs_3_.1, bf16[32,5,64,256]{3,2,1,0:T(8,128)(2,1)} %refs_3_.1, bf16[32,5,64,256]{3,2,1,0:T(8,128)(2,1)} %refs_3_.1), custom_call_target="tpu_custom_call" | custom-call | tf_op jit(solution)/shard_map/pallas_call | solution.py:64
  33.5 0.0 all-to-all-done
  33.5 10.1 %all-to-all-start.1 = ((bf16[128,320,128]{2,1,0:T(8,128)(2,1)}), bf16[128,320,128]{2,1,0:T(8,128)(2,1)}, u32[]{:S(2)}, u32[]{:S(2)}) async-start(bf16[128,320,128]{2,1,0:T(8,128)(2,1)} %bitcast.22), calls=%async_computation.1 | async-start | bytes 20971520 | tf_op jit(solution)/shard_map/all_to_all | solution.py:160
  43.7 1.1 fusion.16
  44.8 2.0 fusion.14
  46.8 7.0 %multiply_subtract_fusion = (f32[32,64,2048]{2,1,0:T(8,128)S(1)}, f32[32,64,2048]{2,1,0:T(8,128)}) fusion(f32[64,2048]{1,0:T(8,128)S(1)} %get-tuple-element.14, f32[32,2048]{1,0:T(8,128)S(1)} %get-tuple-element.12, f32[64,2048]{1,0:T(8,128)S(1)} %get-tuple-element.13, f32[32,2048]{1,0:T(8,128)S(1)} %get-tuple-element.11), kind=kLoop, calls=%fused_computation.7 | loop fusion | flops 25165824 | bytes 35127296 | tf_op jit(solution)/shard_map/sub | solution.py:30
  53.9 10.9 %fusion.1 = bf16[2048,2048]{1,0:T(8,128)(2,1)} fusion(f32[32,64,2048]{2,1,0:T(8,128)} %get-tuple-element.10, f32[32,64,2048]{2,1,0:T(8,128)S(1)} %get-tuple-element.9, pred[2048]{0:T(1024)(128)(4,1)S(1)} %iota_compare_fusion.3), kind=kLoop, calls=%fused_computation.5 | loop fusion | flops 12582912 | bytes 41945088 | tf_op jit(solution)/shard_map/convert_element_type | solution.py:32
  64.8 0.2 copy.21
  65.0 0.1 copy.22
  65.1 1.0 iota_reduce_fusion
  66.0 0.7 reshape.208.half_ref
  66.7 0.7 reshape.207.row_ref
  67.4 113.8 %all-to-all-done.1 = bf16[128,320,128]{2,1,0:T(8,128)(2,1)} async-done(((bf16[128,320,128]{2,1,0:T(8,128)(2,1)}), bf16[128,320,128]{2,1,0:T(8,128)(2,1)}, u32[]{:S(2)}, u32[]{:S(2)}) %all-to-all-start.1) | async-done | bytes 10485792 | tf_op jit(solution)/shard_map/all_to_all | solution.py:160
  181.2 12.2 %shard_map.56 = bf16[5,8,32,2048]{3,2,1,0:T(8,128)(2,1)} custom-call(s32[256]{0:T(256)} %reshape.207.row_ref, s32[256]{0:T(256)} %reshape.208.half_ref, ...), custom_call_target="tpu_custom_call" | custom-call | tf_op jit(solution)/shard_map/pallas_call | solution.py:117
  193.3 17.4 %fusion.2 = f32[5,8,32,2048]{3,2,1,0:T(8,128)} fusion(bf16[5,8,32,2048]{3,2,1,0:T(8,128)(2,1)} %shard_map.56, bf16[2048,2048]{1,0:T(8,128)(2,1)} %fusion.1), kind=kOutput, calls=%fused_computation.8 | convolution fusion | flops 10737418240 | bytes 24117248 | tf_op jit(solution)/shard_map/dot_general | solution.py:176
  210.7 0.0 copy-done.1
  (9 shorter events, 0.1 us)
Async XLA Ops:
  0.0 3.0 %copy-start = (s32[32]{0:T(128)S(1)}, s32[32]{0:T(128)}, u32[]{:S(2)}) copy-start(s32[32]{0:T(128)} %param.9) | copy-start | bytes 388
  3.0 15.1 %copy-start.2 = (s32[64]{0:T(128)}, s32[64]{0:T(128)S(1)}, u32[]{:S(2)}) copy-start(s32[64]{0:T(128)S(1)} %get-tuple-element.7.source_ref) | copy-start | bytes 772
  6.0 27.5 %all-to-all-start = ((s32[128,1,4]{2,1,0:T(1,128)}), s32[128,1,4]{2,1,0:T(1,128)S(1)}, u32[]{:S(2)}, u32[]{:S(2)}) async-start(s32[128,1,4]{2,1,0:T(1,128)} %bitcast), calls=%async_computation | async-start | bytes 131072 | tf_op jit(solution)/shard_map/all_to_all | solution.py:161
  33.5 147.7 %all-to-all-start.1 = ((bf16[128,320,128]{2,1,0:T(8,128)(2,1)}), bf16[128,320,128]{2,1,0:T(8,128)(2,1)}, u32[]{:S(2)}, u32[]{:S(2)}) async-start(bf16[128,320,128]{2,1,0:T(8,128)(2,1)} %bitcast.22), calls=%async_computation.1 | async-start | bytes 20971520 | tf_op jit(solution)/shard_map/all_to_all | solution.py:160
  181.2 29.5 %copy-start.1 = (s32[32]{0:T(128)S(1)}, s32[32]{0:T(128)}, u32[]{:S(2)}) copy-start(s32[32]{0:T(128)} %param.9) | copy-start | bytes 388

commit v7 on v6

--- a/solution.py
+++ b/solution.py
@@ -34,23 +34,24 @@
 
 def pack_kernel(source_ref, scale_ref, *refs):
     out_ref = refs[-1]
-    slots = len(refs) - 1
-    tile = pl.program_id(0)
-    fields, planes, sliver = out_ref.shape[3], out_ref.shape[1], out_ref.shape[4]
-    for pair in range(slots // 2):
-        first = tile * slots + 2 * pair
-        first_scale = scale_ref[first].astype(out_ref.dtype)
-        second_scale = scale_ref[first + 1].astype(out_ref.dtype)
-        for field in range(fields):
-            both = jnp.concatenate(
-                [
-                    refs[2 * pair][0, field] * first_scale,
-                    refs[2 * pair + 1][0, field] * second_scale,
-                ],
-                axis=0,
-            )
-            flipped = both.T.reshape(planes, sliver, both.shape[0])
-            out_ref[0, :, pair, field] = flipped.astype(out_ref.dtype)
+    per_step, planes, pairs, fields, sliver = out_ref.shape[:5]
+    step = pl.program_id(0)
+    for local_tile in range(per_step):
+        for pair in range(pairs):
+            slot = (local_tile * pairs + pair) * 2
+            first = step * (len(refs) - 1) + slot
+            first_scale = scale_ref[first].astype(out_ref.dtype)
+            second_scale = scale_ref[first + 1].astype(out_ref.dtype)
+            for field in range(fields):
+                both = jnp.concatenate(
+                    [
+                        refs[slot][0, field] * first_scale,
+                        refs[slot + 1][0, field] * second_scale,
+                    ],
+                    axis=0,
+                )
+                flipped = both.T.reshape(planes, sliver, both.shape[0])
+                out_ref[local_tile, :, pair, field] = flipped.astype(out_ref.dtype)
 
 
 def pack_outbox(blocks, source, scale, tile_count, capacity, plane_count):
@@ -58,8 +59,11 @@
     pairs = capacity // 2
     sliver = cols // plane_count
 
+    per_step = 2
+    per_call = per_step * capacity
+
     def block_map(slot):
-        return lambda t, src_ref: (src_ref[t * capacity + slot], 0, 0, 0)
+        return lambda t, src_ref: (src_ref[t * per_call + slot], 0, 0, 0)
 
     return pl.pallas_call(
         pack_kernel,
@@ -68,64 +72,72 @@
         ),
         grid_spec=pltpu.PrefetchScalarGridSpec(
             num_scalar_prefetch=1,
-            grid=(tile_count,),
+            grid=(tile_count // per_step,),
             in_specs=[pl.BlockSpec(memory_space=pltpu.SMEM)]
-            + [pl.BlockSpec((1, fields, bphi, cols), block_map(slot)) for slot in range(capacity)],
+            + [pl.BlockSpec((1, fields, bphi, cols), block_map(slot)) for slot in range(per_call)],
             out_specs=pl.BlockSpec(
-                (1, plane_count, pairs, fields, sliver, 2 * bphi),
+                (per_step, plane_count, pairs, fields, sliver, 2 * bphi),
                 lambda t, src_ref: (t, 0, 0, 0, 0, 0),
             ),
         ),
-    )(source, scale, *([blocks] * capacity))
-
-
-def unpack_kernel(groups, per_plane, row_ref, half_ref, *refs):
+    )(source, scale, *([blocks] * per_call))
+
+
+def unpack_kernel(groups, per_plane, per_step, row_ref, half_ref, *refs):
     out_ref = refs[-1]
-    segment = pl.program_id(0)
+    step = pl.program_id(0)
     lanes = refs[0].shape[-1]
     shape = refs[0].shape[1:]
     lane = lax.broadcasted_iota(jnp.int32, shape, 2)
-    for group in range(groups):
-        for quad in range(per_plane // 2):
-            parts = []
-            for side in range(2):
-                position = quad * 2 + side
-                index = (segment * per_plane + position) * groups + group
-                piece = refs[position * groups + group][0]
-                turned = pltpu.roll(piece, lanes // 2, 2)
-                keep = half_ref[index] == side
-                parts.append(jnp.where(keep, piece, turned))
-            merged = jnp.where(lane < lanes // 2, parts[0], parts[1])
-            out_ref[:, group, :, quad * lanes : (quad + 1) * lanes] = merged.astype(out_ref.dtype)
+    quads = per_plane // 2
+    for local_segment in range(per_step):
+        for group in range(groups):
+            for quad in range(quads):
+                parts = []
+                for side in range(2):
+                    position = local_segment * per_plane + quad * 2 + side
+                    index = (step * per_step * per_plane + position) * groups + group
+                    piece = refs[position * groups + group][0]
+                    turned = pltpu.roll(piece, lanes // 2, 2)
+                    keep = half_ref[index] == side
+                    parts.append(jnp.where(keep, piece, turned))
+                merged = jnp.where(lane < lanes // 2, parts[0], parts[1])
+                start = (local_segment * quads + quad) * lanes
+                out_ref[:, group, :, start : start + lanes] = merged.astype(out_ref.dtype)
 
 
 def unpack_lhs(landed, row, half, plane_count, per_plane, groups):
     _, fields, sliver, lanes = landed.shape
 
+    per_step = 2
+    per_call = per_step * per_plane
+
     def piece_map(position, group):
         def index_map(s, row_ref, half_ref):
-            return (row_ref[(s * per_plane + position) * groups + group], 0, 0, 0)
+            return (row_ref[(s * per_call + position) * groups + group], 0, 0, 0)
 
         return index_map
 
     in_specs = [
         pl.BlockSpec((1, fields, sliver, lanes), piece_map(position, group))
-        for position in range(per_plane)
+        for position in range(per_call)
         for group in range(groups)
     ]
-    width = per_plane * lanes // 2
+    width = per_call * lanes // 2
     return pl.pallas_call(
-        functools.partial(unpack_kernel, groups, per_plane),
-        out_shape=jax.ShapeDtypeStruct((fields, groups, sliver, plane_count * width), landed.dtype),
+        functools.partial(unpack_kernel, groups, per_plane, per_step),
+        out_shape=jax.ShapeDtypeStruct(
+            (fields, groups, sliver, plane_count * per_plane * lanes // 2), landed.dtype
+        ),
         grid_spec=pltpu.PrefetchScalarGridSpec(
             num_scalar_prefetch=2,
-            grid=(plane_count,),
+            grid=(plane_count // per_step,),
             in_specs=in_specs,
             out_specs=pl.BlockSpec(
                 (fields, groups, sliver, width), lambda s, row_ref, half_ref: (0, 0, 0, s)
             ),
         ),
-    )(row, half, *([landed] * (per_plane * groups)))
+    )(row, half, *([landed] * (per_call * groups)))
 
 
 def local(blocks, levels, block_dest, block_phi, block_group):

time: 212 us -> 208 us (0.981)
  Pallas kernels: 27.6 us -> 23.3 us
    pallas_call x1, Pallas kernels: 15.4 us -> 11.7 us  [pack_outbox(): pl.pallas_call(pack_kernel, out_shape=jax.ShapeDtypeStruct((tile_count, p...]
  transfers between devices with their start and end apart: 2 -> 2, of which waited for: 1 -> 1; matrix products, arithmetic and copies ran while one was open for 12% -> 12% of each run, Pallas kernels for 7% -> 6%
where the time goes in v7:
time: 208 us; the launch traced here: 207 us
  waiting for transfers between devices  113 us (54%)
  other arithmetic  25.7 us (12%)
  Pallas kernels  23.3 us (11%)
  starting transfers between devices  21.3 us (10%)
  matrix products  17.5 us (8%)
  local copies, waits for them, and re-layouts  5.9 us (3%)
    all_to_all x1, waiting for transfers between devices, local(): lax.all_to_all(outbox, ('tile', 'phi'), split_axis=0, concat_axis=0, tile...  113 us
    dot_general x1, matrix products, local(): jnp.dot(lhs.reshape(fields * CG_DEV * sliver, NPHI), basis, preferred_ele...  17.5 us
    pallas_call x1, Pallas kernels, pack_outbox(): pl.pallas_call(pack_kernel, out_shape=jax.ShapeDtypeStruct((tile_count, p...  11.7 us
    pallas_call x1, Pallas kernels, unpack_lhs(): pl.pallas_call(functools.partial(unpack_kernel, groups, per_plane, per_st...  11.6 us
    all_to_all x1, starting transfers between devices, local(): lax.all_to_all(outbox, ('tile', 'phi'), split_axis=0, concat_axis=0, tile...  11.1 us
    convert_element_type x1, other arithmetic, dft_basis(): return values.reshape(length, length).astype(jnp.bfloat16)  10.9 us
    all_to_all x1, starting transfers between devices, local(): lax.all_to_all(code_out, ('tile', 'phi'), split_axis=0, concat_axis=0, ti...  10.2 us
    sub x1, other arithmetic, dft_basis(): values = jnp.where(is_cos, ch * cl - sh * sl, sh * cl + ch * sl)  7.04 us
  transfers between devices with their start and end apart: 2, of which 1 were waited for; matrix products, arithmetic and copies ran while one was open for 12% of the time, Pallas kernels for 6%

profile of v7, /device:TPU:97, one launch (start us, length us, event | category | flops | bytes accessed | tf_op | source)
XLA Modules:
  0.0 206.9 jit_solution(7457583583930007621)
XLA Ops:
  0.0 0.0 copy-start
  0.0 0.7 fusion.18
  0.7 0.1 reduce_window_sum.11
  0.8 0.8 select_reduce_fusion
  1.6 0.7 multiply_add_fusion.1
  2.3 0.1 fusion.17
  2.4 0.6 iota_reduce_fusion.1
  3.0 0.0 copy-done
  3.0 0.8 gather_fusion.1
  3.8 1.4 gather_fusion
  5.2 0.1 select_n.86
  5.3 0.6 broadcast_in_dim.15.clone
  6.0 10.2 %all-to-all-start = ((s32[128,1,4]{2,1,0:T(1,128)}), s32[128,1,4]{2,1,0:T(1,128)S(1)}, u32[]{:S(2)}, u32[]{:S(2)}) async-start(s32[128,1,4]{2,1,0:T(1,128)} %bitcast), calls=%async_computation | async-start | bytes 131072 | tf_op jit(solution)/shard_map/all_to_all | solution.py:173
  16.1 1.4 gather_fusion.2
  17.6 0.5 convert_divide_fusion.scale_ref
  18.1 0.0 copy-done.2
  18.1 11.7 %shard_map.55 = bf16[16,8,2,5,32,128]{5,4,3,2,1,0:T(8,128)(2,1)} custom-call(s32[64]{0:T(128)} %copy-done.2, f32[64]{0:T(128)} %convert_divide_fusion.scale_ref, bf16[32,5,64,256]{3,2,1,0:T(8,128)(2,1)} %refs_7_.1, bf16[32,5,64,256]{3,2,1,0:T(8,128)(2,1)} %refs_7_.1, bf16[32,5,64,256]{3,2,1,0:T(8,128)(2,1)} %refs_7_.1, bf16[32,5,64,256]{3,2,1,0:T(8,128)(2,1)} %refs_7_.1, ...), custom_call_target="tpu_custom_call" | custom-call | tf_op jit(solution)/shard_map/pallas_call | solution.py:68
  29.8 0.0 all-to-all-done
  29.8 11.1 %all-to-all-start.1 = ((bf16[128,320,128]{2,1,0:T(8,128)(2,1)}), bf16[128,320,128]{2,1,0:T(8,128)(2,1)}, u32[]{:S(2)}, u32[]{:S(2)}) async-start(bf16[128,320,128]{2,1,0:T(8,128)(2,1)} %bitcast.22), calls=%async_computation.1 | async-start | bytes 20971520 | tf_op jit(solution)/shard_map/all_to_all | solution.py:172
  40.9 1.1 fusion.16
  42.0 2.0 fusion.14
  44.1 7.0 %multiply_subtract_fusion = (f32[32,64,2048]{2,1,0:T(8,128)S(1)}, f32[32,64,2048]{2,1,0:T(8,128)}) fusion(f32[64,2048]{1,0:T(8,128)S(1)} %get-tuple-element.14, f32[32,2048]{1,0:T(8,128)S(1)} %get-tuple-element.12, f32[64,2048]{1,0:T(8,128)S(1)} %get-tuple-element.13, f32[32,2048]{1,0:T(8,128)S(1)} %get-tuple-element.11), kind=kLoop, calls=%fused_computation.7 | loop fusion | flops 25165824 | bytes 35127296 | tf_op jit(solution)/shard_map/sub | solution.py:30
  51.1 10.9 %fusion.1 = bf16[2048,2048]{1,0:T(8,128)(2,1)} fusion(f32[32,64,2048]{2,1,0:T(8,128)} %get-tuple-element.10, f32[32,64,2048]{2,1,0:T(8,128)S(1)} %get-tuple-element.9, pred[2048]{0:T(1024)(128)(4,1)S(1)} %iota_compare_fusion.3), kind=kLoop, calls=%fused_computation.5 | loop fusion | flops 12582912 | bytes 41945088 | tf_op jit(solution)/shard_map/convert_element_type | solution.py:32
  62.0 0.2 copy.21
  62.2 0.1 copy.22
  62.3 1.0 iota_reduce_fusion
  63.3 0.7 reshape.208.half_ref
  63.9 0.7 reshape.207.row_ref
  64.6 113.1 %all-to-all-done.1 = bf16[128,320,128]{2,1,0:T(8,128)(2,1)} async-done(((bf16[128,320,128]{2,1,0:T(8,128)(2,1)}), bf16[128,320,128]{2,1,0:T(8,128)(2,1)}, u32[]{:S(2)}, u32[]{:S(2)}) %all-to-all-start.1) | async-done | bytes 10485792 | tf_op jit(solution)/shard_map/all_to_all | solution.py:172
  177.7 11.6 %shard_map.56 = bf16[5,8,32,2048]{3,2,1,0:T(8,128)(2,1)} custom-call(s32[256]{0:T(256)} %reshape.207.row_ref, s32[256]{0:T(256)} %reshape.208.half_ref, ...), custom_call_target="tpu_custom_call" | custom-call | tf_op jit(solution)/shard_map/pallas_call | solution.py:127
  189.3 17.5 %fusion.2 = f32[5,8,32,2048]{3,2,1,0:T(8,128)} fusion(bf16[5,8,32,2048]{3,2,1,0:T(8,128)(2,1)} %shard_map.56, bf16[2048,2048]{1,0:T(8,128)(2,1)} %fusion.1), kind=kOutput, calls=%fused_computation.8 | convolution fusion | flops 10737418240 | bytes 24117248 | tf_op jit(solution)/shard_map/dot_general | solution.py:188
  206.9 0.0 copy-done.1
  (9 shorter events, 0.1 us)
Async XLA Ops:
  0.0 3.0 %copy-start = (s32[32]{0:T(128)S(1)}, s32[32]{0:T(128)}, u32[]{:S(2)}) copy-start(s32[32]{0:T(128)} %param.9) | copy-start | bytes 388
  3.0 15.1 %copy-start.2 = (s32[64]{0:T(128)}, s32[64]{0:T(128)S(1)}, u32[]{:S(2)}) copy-start(s32[64]{0:T(128)S(1)} %get-tuple-element.7.source_ref) | copy-start | bytes 772
  6.0 23.8 %all-to-all-start = ((s32[128,1,4]{2,1,0:T(1,128)}), s32[128,1,4]{2,1,0:T(1,128)S(1)}, u32[]{:S(2)}, u32[]{:S(2)}) async-start(s32[128,1,4]{2,1,0:T(1,128)} %bitcast), calls=%async_computation | async-start | bytes 131072 | tf_op jit(solution)/shard_map/all_to_all | solution.py:173
  29.8 147.9 %all-to-all-start.1 = ((bf16[128,320,128]{2,1,0:T(8,128)(2,1)}), bf16[128,320,128]{2,1,0:T(8,128)(2,1)}, u32[]{:S(2)}, u32[]{:S(2)}) async-start(bf16[128,320,128]{2,1,0:T(8,128)(2,1)} %bitcast.22), calls=%async_computation.1 | async-start | bytes 20971520 | tf_op jit(solution)/shard_map/all_to_all | solution.py:172
  177.7 29.2 %copy-start.1 = (s32[32]{0:T(128)S(1)}, s32[32]{0:T(128)}, u32[]{:S(2)}) copy-start(s32[32]{0:T(128)} %param.9) | copy-start | bytes 388

commit v8 on v7

--- a/solution.py
+++ b/solution.py
@@ -83,61 +83,72 @@
     )(source, scale, *([blocks] * per_call))
 
 
-def unpack_kernel(groups, per_plane, per_step, row_ref, half_ref, *refs):
-    out_ref = refs[-1]
-    step = pl.program_id(0)
-    lanes = refs[0].shape[-1]
-    shape = refs[0].shape[1:]
+def spectra_kernel(groups, per_plane, row_ref, half_ref, *refs):
+    pieces = refs[: per_plane * groups]
+    basis_ref, out_ref, lhs_ref = refs[per_plane * groups :]
+    segment = pl.program_id(0)
+    lanes = pieces[0].shape[-1]
+    shape = pieces[0].shape[1:]
     lane = lax.broadcasted_iota(jnp.int32, shape, 2)
-    quads = per_plane // 2
-    for local_segment in range(per_step):
-        for group in range(groups):
-            for quad in range(quads):
-                parts = []
-                for side in range(2):
-                    position = local_segment * per_plane + quad * 2 + side
-                    index = (step * per_step * per_plane + position) * groups + group
-                    piece = refs[position * groups + group][0]
-                    turned = pltpu.roll(piece, lanes // 2, 2)
-                    keep = half_ref[index] == side
-                    parts.append(jnp.where(keep, piece, turned))
-                merged = jnp.where(lane < lanes // 2, parts[0], parts[1])
-                start = (local_segment * quads + quad) * lanes
-                out_ref[:, group, :, start : start + lanes] = merged.astype(out_ref.dtype)
-
-
-def unpack_lhs(landed, row, half, plane_count, per_plane, groups):
+    for group in range(groups):
+        for quad in range(per_plane // 2):
+            parts = []
+            for side in range(2):
+                position = quad * 2 + side
+                index = (segment * per_plane + position) * groups + group
+                piece = pieces[position * groups + group][0]
+                turned = pltpu.roll(piece, lanes // 2, 2)
+                keep = half_ref[index] == side
+                parts.append(jnp.where(keep, piece, turned))
+            merged = jnp.where(lane < lanes // 2, parts[0], parts[1])
+            lhs_ref[:, group, :, quad * lanes : (quad + 1) * lanes] = merged
+
+    @pl.when(segment == 0)
+    def _():
+        out_ref[...] = jnp.zeros_like(out_ref)
+
+    rows = out_ref.shape[0]
+    lhs = lhs_ref[...].reshape(rows, lhs_ref.shape[-1])
+    width = 512
+    for chunk in range(out_ref.shape[1] // width):
+        columns = slice(chunk * width, (chunk + 1) * width)
+        out_ref[:, columns] += jnp.dot(
+            lhs, basis_ref[:, columns], preferred_element_type=jnp.float32
+        )
+
+
+def spectra_from(landed, row, half, basis, plane_count, per_plane, groups):
     _, fields, sliver, lanes = landed.shape
-
-    per_step = 2
-    per_call = per_step * per_plane
+    depth = per_plane * lanes // 2
+    length = basis.shape[1]
 
     def piece_map(position, group):
         def index_map(s, row_ref, half_ref):
-            return (row_ref[(s * per_call + position) * groups + group], 0, 0, 0)
+            return (row_ref[(s * per_plane + position) * groups + group], 0, 0, 0)
 
         return index_map
 
     in_specs = [
         pl.BlockSpec((1, fields, sliver, lanes), piece_map(position, group))
-        for position in range(per_call)
+        for position in range(per_plane)
         for group in range(groups)
     ]
-    width = per_call * lanes // 2
+    in_specs.append(pl.BlockSpec((depth, length), lambda s, row_ref, half_ref: (s, 0)))
+    rows = fields * groups * sliver
     return pl.pallas_call(
-        functools.partial(unpack_kernel, groups, per_plane, per_step),
-        out_shape=jax.ShapeDtypeStruct(
-            (fields, groups, sliver, plane_count * per_plane * lanes // 2), landed.dtype
-        ),
+        functools.partial(spectra_kernel, groups, per_plane),
+        out_shape=jax.ShapeDtypeStruct((rows, length), jnp.float32),
         grid_spec=pltpu.PrefetchScalarGridSpec(
             num_scalar_prefetch=2,
-            grid=(plane_count // per_step,),
+            grid=(plane_count,),
             in_specs=in_specs,
-            out_specs=pl.BlockSpec(
-                (fields, groups, sliver, width), lambda s, row_ref, half_ref: (0, 0, 0, s)
-            ),
-        ),
-    )(row, half, *([landed] * (per_call * groups)))
+            out_specs=pl.BlockSpec((rows, length), lambda s, row_ref, half_ref: (0, 0)),
+            scratch_shapes=[pltpu.VMEM((fields, groups, sliver, depth), landed.dtype)],
+        ),
+        compiler_params=pltpu.CompilerParams(
+            dimension_semantics=("arbitrary",), vmem_limit_bytes=60 * 1024 * 1024
+        ),
+    )(row, half, *([landed] * (per_plane * groups)), basis)
 
 
 def local(blocks, levels, block_dest, block_phi, block_group):
@@ -183,11 +194,8 @@
     row = ((origin * plane_count + segment) * pairs + (pick % capacity) // 2).reshape(-1)
     half = (pick % 2).reshape(-1)
     landed = arrived.reshape(device_count * pairs, fields, sliver, 2 * BPHI)
-    lhs = unpack_lhs(landed, row, half, plane_count, per_plane, CG_DEV)
     basis = dft_basis(NPHI)
-    spectra = jnp.dot(
-        lhs.reshape(fields * CG_DEV * sliver, NPHI), basis, preferred_element_type=jnp.float32
-    )
+    spectra = spectra_from(landed, row, half, basis, plane_count, per_plane, CG_DEV)
     return spectra.reshape(fields, CG_DEV, sliver, NPHI)
 
 

time: 208 us -> 207 us (level)
  matrix products: 17.5 us -> 0 us
  Pallas kernels: 23.3 us -> 39.4 us
    dot_general x1 -> x0, matrix products: 17.5 us -> none  [local(): jnp.dot(lhs.reshape(fields * CG_DEV * sliver, NPHI), basis, preferred_ele...]
    pallas_call x1, Pallas kernels: 11.6 us -> 28.2 us  [spectra_from(): pl.pallas_call(functools.partial(spectra_kernel, groups, per_plane), out_...]
  transfers between devices with their start and end apart: 2 -> 2, of which waited for: 1 -> 1; matrix products, arithmetic and copies ran while one was open for 12% -> 12% of each run, Pallas kernels for 6% -> 5%
where the time goes in v8:
time: 207 us
  waiting for transfers between devices  114 us (55%)
  Pallas kernels  39.4 us (19%)
  other arithmetic  25.7 us (12%)
  starting transfers between devices  21.8 us (11%)
  local copies, waits for them, and re-layouts  5.91 us (3%)
    all_to_all x1, waiting for transfers between devices, local(): lax.all_to_all(outbox, ('tile', 'phi'), split_axis=0, concat_axis=0, tile...  114 us
    pallas_call x1, Pallas kernels, spectra_from(): pl.pallas_call(functools.partial(spectra_kernel, groups, per_plane), out_...  28.2 us
    all_to_all x1, starting transfers between devices, local(): lax.all_to_all(outbox, ('tile', 'phi'), split_axis=0, concat_axis=0, tile...  11.7 us
    pallas_call x1, Pallas kernels, pack_outbox(): pl.pallas_call(pack_kernel, out_shape=jax.ShapeDtypeStruct((tile_count, p...  11.2 us
    convert_element_type x1, other arithmetic, dft_basis(): return values.reshape(length, length).astype(jnp.bfloat16)  10.9 us
    all_to_all x1, starting transfers between devices, local(): lax.all_to_all(code_out, ('tile', 'phi'), split_axis=0, concat_axis=0, ti...  10.2 us
    sub x1, other arithmetic, dft_basis(): values = jnp.where(is_cos, ch * cl - sh * sl, sh * cl + ch * sl)  7.04 us
  transfers between devices with their start and end apart: 2, of which 1 were waited for; matrix products, arithmetic and copies ran while one was open for 12% of the time, Pallas kernels for 5%

profile of v8, /device:TPU:97, one launch (start us, length us, event | category | flops | bytes accessed | tf_op | source)
XLA Modules:
  0.0 206.9 jit_solution(12211882185173686567)
XLA Ops:
  0.0 0.0 copy-start
  0.0 0.7 fusion.16
  0.7 0.1 reduce_window_sum.11
  0.8 0.8 select_reduce_fusion
  1.6 0.7 multiply_add_fusion.1
  2.3 0.6 iota_reduce_fusion.1
  2.9 0.0 copy-start.2
  2.9 0.1 fusion.15
  3.0 0.0 copy-done
  3.0 0.8 gather_fusion
  3.8 1.4 gather_fusion.1
  5.2 0.1 select_n.84
  5.3 0.6 broadcast_in_dim.15.clone
  6.0 10.2 %all-to-all-start = ((s32[128,1,4]{2,1,0:T(1,128)}), s32[128,1,4]{2,1,0:T(1,128)S(1)}, u32[]{:S(2)}, u32[]{:S(2)}) async-start(s32[128,1,4]{2,1,0:T(1,128)} %bitcast), calls=%async_computation | async-start | bytes 131072 | tf_op jit(solution)/shard_map/all_to_all | solution.py:184
  16.1 1.4 gather_fusion.2
  17.6 0.5 convert_divide_fusion.scale_ref
  18.1 0.0 copy-done.2
  18.1 11.2 %shard_map.55 = bf16[16,8,2,5,32,128]{5,4,3,2,1,0:T(8,128)(2,1)} custom-call(s32[64]{0:T(128)} %copy-done.2, f32[64]{0:T(128)} %convert_divide_fusion.scale_ref, bf16[32,5,64,256]{3,2,1,0:T(8,128)(2,1)} %refs_7_.1, bf16[32,5,64,256]{3,2,1,0:T(8,128)(2,1)} %refs_7_.1, bf16[32,5,64,256]{3,2,1,0:T(8,128)(2,1)} %refs_7_.1, bf16[32,5,64,256]{3,2,1,0:T(8,128)(2,1)} %refs_7_.1, ...), custom_call_target="tpu_custom_call" | custom-call | tf_op jit(solution)/shard_map/pallas_call | solution.py:68
  29.3 0.0 all-to-all-done
  29.3 11.7 %all-to-all-start.1 = ((bf16[128,320,128]{2,1,0:T(8,128)(2,1)}), bf16[128,320,128]{2,1,0:T(8,128)(2,1)}, u32[]{:S(2)}, u32[]{:S(2)}) async-start(bf16[128,320,128]{2,1,0:T(8,128)(2,1)} %bitcast.17), calls=%async_computation.1 | async-start | bytes 20971520 | tf_op jit(solution)/shard_map/all_to_all | solution.py:183
  41.1 1.1 fusion.14
  42.2 2.0 fusion.12
  44.2 7.0 %multiply_subtract_fusion = (f32[32,64,2048]{2,1,0:T(8,128)S(1)}, f32[32,64,2048]{2,1,0:T(8,128)}) fusion(f32[64,2048]{1,0:T(8,128)S(1)} %get-tuple-element.14, f32[32,2048]{1,0:T(8,128)S(1)} %get-tuple-element.12, f32[64,2048]{1,0:T(8,128)S(1)} %get-tuple-element.13, f32[32,2048]{1,0:T(8,128)S(1)} %get-tuple-element.11), kind=kLoop, calls=%fused_computation.7 | loop fusion | flops 25165824 | bytes 35127296 | tf_op jit(solution)/shard_map/sub | solution.py:30
  51.2 10.9 %fusion.1.refs_32_ = bf16[2048,2048]{1,0:T(8,128)(2,1)} fusion(f32[32,64,2048]{2,1,0:T(8,128)} %get-tuple-element.10, f32[32,64,2048]{2,1,0:T(8,128)S(1)} %get-tuple-element.9, pred[2048]{0:T(1024)(128)(4,1)S(1)} %iota_compare_fusion.3), kind=kLoop, calls=%fused_computation.5 | loop fusion | flops 12582912 | bytes 41945088 | tf_op jit(solution)/shard_map/convert_element_type | solution.py:32
  62.2 0.2 copy.21
  62.4 0.1 copy.22
  62.4 1.0 iota_reduce_fusion
  63.4 0.7 reshape.192.row_ref
  64.1 0.6 reshape.193.half_ref
  64.7 113.8 %all-to-all-done.1 = bf16[128,320,128]{2,1,0:T(8,128)(2,1)} async-done(((bf16[128,320,128]{2,1,0:T(8,128)(2,1)}), bf16[128,320,128]{2,1,0:T(8,128)(2,1)}, u32[]{:S(2)}, u32[]{:S(2)}) %all-to-all-start.1) | async-done | bytes 10485792 | tf_op jit(solution)/shard_map/all_to_all | solution.py:183
  178.5 28.2 %shard_map.56 = f32[1280,2048]{1,0:T(8,128)} custom-call(s32[256]{0:T(256)} %reshape.192.row_ref, s32[256]{0:T(256)} %reshape.193.half_ref, ...), custom_call_target="tpu_custom_call" | custom-call | tf_op jit(solution)/shard_map/pallas_call | solution.py:138
  206.7 0.0 copy-done.1
  (8 shorter events, 0.1 us)
Async XLA Ops:
  0.0 3.0 %copy-start = (s32[32]{0:T(128)S(1)}, s32[32]{0:T(128)}, u32[]{:S(2)}) copy-start(s32[32]{0:T(128)} %param.8) | copy-start | bytes 388
  2.9 15.2 %copy-start.2 = (s32[64]{0:T(128)}, s32[64]{0:T(128)S(1)}, u32[]{:S(2)}) copy-start(s32[64]{0:T(128)S(1)} %get-tuple-element.7.source_ref) | copy-start | bytes 772
  6.0 23.4 %all-to-all-start = ((s32[128,1,4]{2,1,0:T(1,128)}), s32[128,1,4]{2,1,0:T(1,128)S(1)}, u32[]{:S(2)}, u32[]{:S(2)}) async-start(s32[128,1,4]{2,1,0:T(1,128)} %bitcast), calls=%async_computation | async-start | bytes 131072 | tf_op jit(solution)/shard_map/all_to_all | solution.py:184
  29.3 149.2 %all-to-all-start.1 = ((bf16[128,320,128]{2,1,0:T(8,128)(2,1)}), bf16[128,320,128]{2,1,0:T(8,128)(2,1)}, u32[]{:S(2)}, u32[]{:S(2)}) async-start(bf16[128,320,128]{2,1,0:T(8,128)(2,1)} %bitcast.17), calls=%async_computation.1 | async-start | bytes 20971520 | tf_op jit(solution)/shard_map/all_to_all | solution.py:183
  178.5 28.2 %copy-start.1 = (s32[32]{0:T(128)S(1)}, s32[32]{0:T(128)}, u32[]{:S(2)}) copy-start(s32[32]{0:T(128)} %param.8) | copy-start | bytes 388

commit v9 on v8

--- a/solution.py
+++ b/solution.py
@@ -54,8 +54,8 @@
                 out_ref[local_tile, :, pair, field] = flipped.astype(out_ref.dtype)
 
 
-def pack_outbox(blocks, source, scale, tile_count, capacity, plane_count):
-    slot_count, fields, bphi, cols = blocks.shape
+def pack_outbox(blocks, source, scale, tile_count, capacity, plane_count, first, fields):
+    slot_count, _, bphi, cols = blocks.shape
     pairs = capacity // 2
     sliver = cols // plane_count
 
@@ -63,7 +63,7 @@
     per_call = per_step * capacity
 
     def block_map(slot):
-        return lambda t, src_ref: (src_ref[t * per_call + slot], 0, 0, 0)
+        return lambda t, src_ref: (src_ref[t * per_call + slot], first // fields, 0, 0)
 
     return pl.pallas_call(
         pack_kernel,
@@ -85,7 +85,7 @@
 
 def spectra_kernel(groups, per_plane, row_ref, half_ref, *refs):
     pieces = refs[: per_plane * groups]
-    basis_ref, out_ref, lhs_ref = refs[per_plane * groups :]
+    basis_ref, out_ref, lhs_ref = refs[per_plane * groups :][0], refs[-2], refs[-1]
     segment = pl.program_id(0)
     lanes = pieces[0].shape[-1]
     shape = pieces[0].shape[1:]
@@ -117,7 +117,7 @@
         )
 
 
-def spectra_from(landed, row, half, basis, plane_count, per_plane, groups):
+def spectra_from(landed, row, half, basis, plane_count, per_plane, groups, rows, first, previous):
     _, fields, sliver, lanes = landed.shape
     depth = per_plane * lanes // 2
     length = basis.shape[1]
@@ -134,21 +134,30 @@
         for group in range(groups)
     ]
     in_specs.append(pl.BlockSpec((depth, length), lambda s, row_ref, half_ref: (s, 0)))
-    rows = fields * groups * sliver
+    block_rows = fields * groups * sliver
+    operands = [row, half] + [landed] * (per_plane * groups) + [basis]
+    aliases = {}
+    if previous is not None:
+        in_specs.append(pl.BlockSpec(memory_space=pl.ANY))
+        aliases = {len(operands): 0}
+        operands.append(previous)
     return pl.pallas_call(
         functools.partial(spectra_kernel, groups, per_plane),
         out_shape=jax.ShapeDtypeStruct((rows, length), jnp.float32),
+        input_output_aliases=aliases,
         grid_spec=pltpu.PrefetchScalarGridSpec(
             num_scalar_prefetch=2,
             grid=(plane_count,),
             in_specs=in_specs,
-            out_specs=pl.BlockSpec((rows, length), lambda s, row_ref, half_ref: (0, 0)),
+            out_specs=pl.BlockSpec(
+                (block_rows, length), lambda s, row_ref, half_ref: (first // fields, 0)
+            ),
             scratch_shapes=[pltpu.VMEM((fields, groups, sliver, depth), landed.dtype)],
         ),
         compiler_params=pltpu.CompilerParams(
             dimension_semantics=("arbitrary",), vmem_limit_bytes=60 * 1024 * 1024
         ),
-    )(row, half, *([landed] * (per_plane * groups)), basis)
+    )(*operands)
 
 
 def local(blocks, levels, block_dest, block_phi, block_group):
@@ -175,12 +184,9 @@
     device_count = tile_count * plane_count
     pairs = capacity // 2
 
-    outbox = pack_outbox(blocks, source, scale, tile_count, capacity, plane_count)
-    outbox = outbox.reshape(device_count, pairs * fields * sliver, 2 * BPHI)
     code_out = jnp.broadcast_to(
         code.reshape(tile_count, 1, capacity), (tile_count, plane_count, capacity)
     ).reshape(device_count, capacity)
-    arrived = lax.all_to_all(outbox, ("tile", "phi"), split_axis=0, concat_axis=0, tiled=True)
     arrived_code = lax.all_to_all(code_out, ("tile", "phi"), split_axis=0, concat_axis=0, tiled=True)
 
     by_segment = jnp.transpose(
@@ -193,9 +199,18 @@
     segment = jnp.arange(plane_count, dtype=jnp.int32)[:, None]
     row = ((origin * plane_count + segment) * pairs + (pick % capacity) // 2).reshape(-1)
     half = (pick % 2).reshape(-1)
-    landed = arrived.reshape(device_count * pairs, fields, sliver, 2 * BPHI)
     basis = dft_basis(NPHI)
-    spectra = spectra_from(landed, row, half, basis, plane_count, per_plane, CG_DEV)
+
+    rows = fields * CG_DEV * sliver
+    spectra = None
+    for first, count in ((0, fields - 1), (fields - 1, 1)):
+        outbox = pack_outbox(blocks, source, scale, tile_count, capacity, plane_count, first, count)
+        outbox = outbox.reshape(device_count, pairs * count * sliver, 2 * BPHI)
+        arrived = lax.all_to_all(outbox, ("tile", "phi"), split_axis=0, concat_axis=0, tiled=True)
+        landed = arrived.reshape(device_count * pairs, count, sliver, 2 * BPHI)
+        spectra = spectra_from(
+            landed, row, half, basis, plane_count, per_plane, CG_DEV, rows, first, spectra
+        )
     return spectra.reshape(fields, CG_DEV, sliver, NPHI)
 
 

time: 207 us -> 211 us (1.019); the launches traced: 207 us -> 209 us
  waiting for transfers between devices: 114 us -> 84.6 us
  Pallas kernels: 39.4 us -> 54.5 us
  other arithmetic: 25.7 us -> 35 us
  starting transfers between devices: 21.8 us -> 26.9 us
    all_to_all x1 -> x2, waiting for transfers between devices: 114 us -> 84.6 us  [local(): lax.all_to_all(outbox, ('tile', 'phi'), split_axis=0, concat_axis=0, tile...]
    pallas_call x1 -> x2, Pallas kernels: 28.2 us -> 37.4 us  [spectra_from(): pl.pallas_call(functools.partial(spectra_kernel, groups, per_plane), out_...]
    pallas_call x1 -> x2, Pallas kernels: 11.2 us -> 17.1 us  [pack_outbox(): pl.pallas_call(pack_kernel, out_shape=jax.ShapeDtypeStruct((tile_count, p...]
    all_to_all x1 -> x2, starting transfers between devices: 11.7 us -> 16.7 us  [local(): lax.all_to_all(outbox, ('tile', 'phi'), split_axis=0, concat_axis=0, tile...]
    sub x1, other arithmetic: 7.04 us -> 12 us  [dft_basis(): values = jnp.where(is_cos, ch * cl - sh * sl, sh * cl + ch * sl)]
    convert_element_type x1, other arithmetic: 10.9 us -> 15.3 us  [dft_basis(): return values.reshape(length, length).astype(jnp.bfloat16)]
  transfers between devices with their start and end apart: 2 -> 3, of which waited for: 1 -> 1; matrix products, arithmetic and copies ran while one was open for 12% -> 17% of each run, Pallas kernels for 5% -> 20%
where the time goes in v9:
time: 211 us; the launch traced here: 209 us
  waiting for transfers between devices  84.6 us (40%)
  Pallas kernels  54.5 us (26%)
  other arithmetic  35 us (17%)
  starting transfers between devices  26.9 us (13%)
  local copies, waits for them, and re-layouts  7.26 us (3%)
    all_to_all x2, waiting for transfers between devices, local(): lax.all_to_all(outbox, ('tile', 'phi'), split_axis=0, concat_axis=0, tile...  84.6 us
    pallas_call x2, Pallas kernels, spectra_from(): pl.pallas_call(functools.partial(spectra_kernel, groups, per_plane), out_...  37.4 us
    pallas_call x2, Pallas kernels, pack_outbox(): pl.pallas_call(pack_kernel, out_shape=jax.ShapeDtypeStruct((tile_count, p...  17.1 us
    all_to_all x2, starting transfers between devices, local(): lax.all_to_all(outbox, ('tile', 'phi'), split_axis=0, concat_axis=0, tile...  16.7 us
    convert_element_type x1, other arithmetic, dft_basis(): return values.reshape(length, length).astype(jnp.bfloat16)  15.3 us
    sub x1, other arithmetic, dft_basis(): values = jnp.where(is_cos, ch * cl - sh * sl, sh * cl + ch * sl)  12 us
    all_to_all x1, starting transfers between devices, local(): lax.all_to_all(code_out, ('tile', 'phi'), split_axis=0, concat_axis=0, ti...  10.2 us
  transfers between devices with their start and end apart: 3, of which 1 were waited for; matrix products, arithmetic and copies ran while one was open for 17% of the time, Pallas kernels for 20%

profile of v9, /device:TPU:97, one launch (start us, length us, event | category | flops | bytes accessed | tf_op | source)
XLA Modules:
  0.0 208.5 jit_solution(734655991425217195)
XLA Ops:
  0.0 0.7 fusion.16
  0.7 0.1 reduce_window_sum.11
  0.8 0.8 select_reduce_fusion
  1.6 0.7 multiply_add_fusion.1
  2.3 0.6 iota_reduce_fusion.1
  2.9 0.1 fusion.15
  3.0 0.8 gather_fusion
  3.8 1.4 gather_fusion.1
  5.2 0.1 select_n.92
  5.3 0.6 broadcast_in_dim.17.clone
  6.0 10.2 %all-to-all-start = ((s32[128,1,4]{2,1,0:T(1,128)}), s32[128,1,4]{2,1,0:T(1,128)S(1)}, u32[]{:S(2)}, u32[]{:S(2)}) async-start(s32[128,1,4]{2,1,0:T(1,128)} %bitcast), calls=%async_computation | async-start | bytes 131072 | tf_op jit(solution)/shard_map/all_to_all | solution.py:190
  16.1 1.4 gather_fusion.2
  17.6 0.6 convert_divide_fusion.scale_ref
  18.2 10.7 %shard_map.56 = bf16[16,8,2,4,32,128]{5,4,3,2,1,0:T(8,128)(2,1)} custom-call(s32[64]{0:T(128)} %copy-done.3, f32[64]{0:T(128)} %convert_divide_fusion.scale_ref, bf16[32,5,64,256]{3,2,1,0:T(8,128)(2,1)} %refs_7_.3, bf16[32,5,64,256]{3,2,1,0:T(8,128)(2,1)} %refs_7_.3, bf16[32,5,64,256]{3,2,1,0:T(8,128)(2,1)} %refs_7_.3, bf16[32,5,64,256]{3,2,1,0:T(8,128)(2,1)} %refs_7_.3, ...), custom_call_target="tpu_custom_call" | custom-call | tf_op jit(solution)/shard_map/pallas_call | solution.py:68
  28.9 0.0 all-to-all-done
  28.9 10.7 %all-to-all-start.2 = ((bf16[128,256,128]{2,1,0:T(8,128)(2,1)}), bf16[128,256,128]{2,1,0:T(8,128)(2,1)}, u32[]{:S(2)}, u32[]{:S(2)}) async-start(bf16[128,256,128]{2,1,0:T(8,128)(2,1)} %bitcast.51), calls=%async_computation.2 | async-start | bytes 16777216 | tf_op jit(solution)/shard_map/all_to_all | solution.py:209
  39.6 6.4 %shard_map.55 = bf16[16,8,2,1,32,128]{5,4,3,2,1,0:T(8,128)(2,1)} custom-call(s32[64]{0:T(128)} %copy-done.3, f32[64]{0:T(128)} %convert_divide_fusion.scale_ref, bf16[32,5,64,256]{3,2,1,0:T(8,128)(2,1)} %refs_7_.3, bf16[32,5,64,256]{3,2,1,0:T(8,128)(2,1)} %refs_7_.3, bf16[32,5,64,256]{3,2,1,0:T(8,128)(2,1)} %refs_7_.3, bf16[32,5,64,256]{3,2,1,0:T(8,128)(2,1)} %refs_7_.3, ...), custom_call_target="tpu_custom_call" | custom-call | tf_op jit(solution)/shard_map/pallas_call | solution.py:68
  46.1 1.1 fusion.14
  47.2 2.0 fusion.12
  49.2 12.0 %multiply_subtract_fusion = (f32[32,64,2048]{2,1,0:T(8,128)}, f32[32,64,2048]{2,1,0:T(8,128)}) fusion(f32[64,2048]{1,0:T(8,128)S(1)} %get-tuple-element.14, f32[32,2048]{1,0:T(8,128)S(1)} %get-tuple-element.12, f32[64,2048]{1,0:T(8,128)S(1)} %get-tuple-element.13, f32[32,2048]{1,0:T(8,128)S(1)} %get-tuple-element.11), kind=kLoop, calls=%fused_computation.7 | loop fusion | flops 25165824 | bytes 35127296 | tf_op jit(solution)/shard_map/sub | solution.py:30
  61.2 84.6 %all-to-all-done.2 = bf16[128,256,128]{2,1,0:T(8,128)(2,1)} async-done(((bf16[128,256,128]{2,1,0:T(8,128)(2,1)}), bf16[128,256,128]{2,1,0:T(8,128)(2,1)}, u32[]{:S(2)}, u32[]{:S(2)}) %all-to-all-start.2) | async-done | bytes 8388640 | tf_op jit(solution)/shard_map/all_to_all | solution.py:209
  145.8 6.0 %all-to-all-start.1 = ((bf16[128,64,128]{2,1,0:T(8,128)(2,1)}), bf16[128,64,128]{2,1,0:T(8,128)(2,1)S(1)}, u32[]{:S(2)}, u32[]{:S(2)}) async-start(bf16[128,64,128]{2,1,0:T(8,128)(2,1)} %bitcast.52), calls=%async_computation.1 | async-start | bytes 4194304 | tf_op jit(solution)/shard_map/all_to_all | solution.py:209
  151.8 15.3 %fusion.1.refs_32_ = bf16[2048,2048]{1,0:T(8,128)(2,1)} fusion(f32[32,64,2048]{2,1,0:T(8,128)} %get-tuple-element.10, f32[32,64,2048]{2,1,0:T(8,128)} %get-tuple-element.9, pred[2048]{0:T(1024)(128)(4,1)S(1)} %iota_compare_fusion.3), kind=kLoop, calls=%fused_computation.5 | loop fusion | flops 12582912 | bytes 41945088 | tf_op jit(solution)/shard_map/convert_element_type | solution.py:32
  167.1 0.2 copy.22
  167.3 0.1 copy.23
  167.3 0.9 iota_reduce_fusion
  168.3 0.7 reshape.198.row_ref
  169.0 0.7 reshape.199.half_ref
  169.6 24.2 %shard_map.57.refs_33_ = f32[1280,2048]{1,0:T(8,128)} custom-call(s32[256]{0:T(256)} %reshape.198.row_ref, s32[256]{0:T(256)} %reshape.199.half_ref, ...), custom_call_target="tpu_custom_call" | custom-call | tf_op jit(solution)/shard_map/pallas_call | solution.py:144
  193.8 0.0 all-to-all-done.1
  193.8 1.3 copy-done.2
  195.2 13.2 %shard_map.58 = f32[1280,2048]{1,0:T(8,128)} custom-call(s32[256]{0:T(256)} %reshape.198.row_ref, s32[256]{0:T(256)} %reshape.199.half_ref, bf16[256,1,32,128]{3,2,1,0:T(8,128)(2,1)} %bitcast.34, bf16[256,1,32,128]{3,2,1,0:T(8,128)(2,1)} %bitcast.50, bf16[256,1,32,128]{3,2,1,0:T(8,128)(2,1)} %bitcast.21, ...), custom_call_target="tpu_custom_call", output_to_operand_aliasing={{}: (35, {})} | custom-call | tf_op jit(solution)/shard_map/pallas_call | solution.py:144
  (14 shorter events, 0.1 us)
Async XLA Ops:
  0.0 3.0 %copy-start = (s32[32]{0:T(128)S(1)}, s32[32]{0:T(128)}, u32[]{:S(2)}) copy-start(s32[32]{0:T(128)} %param.8) | copy-start | bytes 388
  2.9 15.3 %copy-start.3 = (s32[64]{0:T(128)}, s32[64]{0:T(128)S(1)}, u32[]{:S(2)}) copy-start(s32[64]{0:T(128)S(1)} %get-tuple-element.7.source_ref) | copy-start | bytes 772
  6.0 22.9 %all-to-all-start = ((s32[128,1,4]{2,1,0:T(1,128)}), s32[128,1,4]{2,1,0:T(1,128)S(1)}, u32[]{:S(2)}, u32[]{:S(2)}) async-start(s32[128,1,4]{2,1,0:T(1,128)} %bitcast), calls=%async_computation | async-start | bytes 131072 | tf_op jit(solution)/shard_map/all_to_all | solution.py:190
  28.9 116.9 %all-to-all-start.2 = ((bf16[128,256,128]{2,1,0:T(8,128)(2,1)}), bf16[128,256,128]{2,1,0:T(8,128)(2,1)}, u32[]{:S(2)}, u32[]{:S(2)}) async-start(bf16[128,256,128]{2,1,0:T(8,128)(2,1)} %bitcast.51), calls=%async_computation.2 | async-start | bytes 16777216 | tf_op jit(solution)/shard_map/all_to_all | solution.py:209
  145.8 48.0 %all-to-all-start.1 = ((bf16[128,64,128]{2,1,0:T(8,128)(2,1)}), bf16[128,64,128]{2,1,0:T(8,128)(2,1)S(1)}, u32[]{:S(2)}, u32[]{:S(2)}) async-start(bf16[128,64,128]{2,1,0:T(8,128)(2,1)} %bitcast.52), calls=%async_computation.1 | async-start | bytes 4194304 | tf_op jit(solution)/shard_map/all_to_all | solution.py:209
  193.8 1.4 copy-start.2
  195.2 13.2 %copy-start.1 = (s32[32]{0:T(128)S(1)}, s32[32]{0:T(128)}, u32[]{:S(2)}) copy-start(s32[32]{0:T(128)} %param.8) | copy-start | bytes 388

commit v10 on v9

--- a/solution.py
+++ b/solution.py
@@ -160,6 +160,63 @@
     )(*operands)
 
 
+def unpack_kernel(groups, per_plane, per_step, row_ref, half_ref, *refs):
+    out_ref = refs[-1]
+    step = pl.program_id(0)
+    lanes = refs[0].shape[-1]
+    shape = refs[0].shape[1:]
+    lane = lax.broadcasted_iota(jnp.int32, shape, 2)
+    quads = per_plane // 2
+    for local_segment in range(per_step):
+        for group in range(groups):
+            for quad in range(quads):
+                parts = []
+                for side in range(2):
+                    position = local_segment * per_plane + quad * 2 + side
+                    index = (step * per_step * per_plane + position) * groups + group
+                    piece = refs[position * groups + group][0]
+                    turned = pltpu.roll(piece, lanes // 2, 2)
+                    keep = half_ref[index] == side
+                    parts.append(jnp.where(keep, piece, turned))
+                merged = jnp.where(lane < lanes // 2, parts[0], parts[1])
+                start = (local_segment * quads + quad) * lanes
+                out_ref[:, group, :, start : start + lanes] = merged.astype(out_ref.dtype)
+
+
+def unpack_lhs(landed, row, half, plane_count, per_plane, groups):
+    _, fields, sliver, lanes = landed.shape
+
+    per_step = 2
+    per_call = per_step * per_plane
+
+    def piece_map(position, group):
+        def index_map(s, row_ref, half_ref):
+            return (row_ref[(s * per_call + position) * groups + group], 0, 0, 0)
+
+        return index_map
+
+    in_specs = [
+        pl.BlockSpec((1, fields, sliver, lanes), piece_map(position, group))
+        for position in range(per_call)
+        for group in range(groups)
+    ]
+    width = per_call * lanes // 2
+    return pl.pallas_call(
+        functools.partial(unpack_kernel, groups, per_plane, per_step),
+        out_shape=jax.ShapeDtypeStruct(
+            (fields, groups, sliver, plane_count * per_plane * lanes // 2), landed.dtype
+        ),
+        grid_spec=pltpu.PrefetchScalarGridSpec(
+            num_scalar_prefetch=2,
+            grid=(plane_count // per_step,),
+            in_specs=in_specs,
+            out_specs=pl.BlockSpec(
+                (fields, groups, sliver, width), lambda s, row_ref, half_ref: (0, 0, 0, s)
+            ),
+        ),
+    )(row, half, *([landed] * (per_call * groups)))
+
+
 def local(blocks, levels, block_dest, block_phi, block_group):
     tile_count = lax.axis_size("tile")
     plane_count = lax.axis_size("phi")
@@ -199,18 +256,32 @@
     segment = jnp.arange(plane_count, dtype=jnp.int32)[:, None]
     row = ((origin * plane_count + segment) * pairs + (pick % capacity) // 2).reshape(-1)
     half = (pick % 2).reshape(-1)
-    basis = dft_basis(NPHI)
 
     rows = fields * CG_DEV * sliver
     spectra = None
+    basis = None
+    arrived = None
     for first, count in ((0, fields - 1), (fields - 1, 1)):
+        if arrived is not None:
+            scale = scale + jnp.float32(0.0) * (
+                arrived[0, 0, 0].astype(jnp.float32) + basis[0, 0].astype(jnp.float32)
+            )
         outbox = pack_outbox(blocks, source, scale, tile_count, capacity, plane_count, first, count)
         outbox = outbox.reshape(device_count, pairs * count * sliver, 2 * BPHI)
+        if basis is None:
+            basis = dft_basis(NPHI) + (outbox[0, 0, 0] * 0).astype(jnp.bfloat16)
         arrived = lax.all_to_all(outbox, ("tile", "phi"), split_axis=0, concat_axis=0, tiled=True)
         landed = arrived.reshape(device_count * pairs, count, sliver, 2 * BPHI)
-        spectra = spectra_from(
-            landed, row, half, basis, plane_count, per_plane, CG_DEV, rows, first, spectra
-        )
+        if spectra is None:
+            spectra = spectra_from(
+                landed, row, half, basis, plane_count, per_plane, CG_DEV, rows, first, None
+            )
+        else:
+            lhs = unpack_lhs(landed, row, half, plane_count, per_plane, CG_DEV)
+            tail = jnp.dot(
+                lhs.reshape(count * CG_DEV * sliver, NPHI), basis, preferred_element_type=jnp.float32
+            )
+            spectra = lax.dynamic_update_slice(spectra, tail, (first * CG_DEV * sliver, 0))
     return spectra.reshape(fields, CG_DEV, sliver, NPHI)
 
 

time: 211 us -> 212 us (level)
  matrix products: 0 us -> 7.37 us
  Pallas kernels: 54.5 us -> 49.7 us
  local copies, waits for them, and re-layouts: 7.26 us -> 12 us
  waiting for transfers between devices: 84.6 us -> 80.2 us
  other arithmetic: 35 us -> 31.6 us
    add x0 -> x3, other arithmetic: none -> 16.9 us  [the longest x2 16.4 us: local(): basis = dft_basis(NPHI) + (outbox[0, 0, 0] * 0).astype(jnp.bfloat16)]
    convert_element_type x1 -> x0, other arithmetic: 15.3 us -> none  [dft_basis(): return values.reshape(length, length).astype(jnp.bfloat16)]
    pallas_call x2 -> x1, Pallas kernels: 37.4 us -> 23.9 us  [spectra_from(): pl.pallas_call(functools.partial(spectra_kernel, groups, per_plane), out_...]
    pallas_call x0 -> x1, Pallas kernels: none -> 8.28 us  [unpack_lhs(): pl.pallas_call(functools.partial(unpack_kernel, groups, per_plane, per_st...]
    dot_general x0 -> x1, matrix products: none -> 7.37 us  [local(): jnp.dot(lhs.reshape(count * CG_DEV * sliver, NPHI), basis, preferred_elem...]
    sub x1, other arithmetic: 12 us -> 7.04 us  [dft_basis(): values = jnp.where(is_cos, ch * cl - sh * sl, sh * cl + ch * sl)]
    all_to_all x2, waiting for transfers between devices: 84.6 us -> 80.2 us  [local(): lax.all_to_all(outbox, ('tile', 'phi'), split_axis=0, concat_axis=0, tile...]
    all_to_all x1, starting transfers between devices: 10.2 us -> 5.99 us  [local(): lax.all_to_all(code_out, ('tile', 'phi'), split_axis=0, concat_axis=0, ti...]
  transfers between devices with their start and end apart: 3 -> 3, of which waited for: 1 -> 1; matrix products, arithmetic and copies ran while one was open for 17% -> 16% of each run, Pallas kernels for 20% -> 15%
where the time goes in v10:
time: 212 us; the launch traced here: 209 us
  waiting for transfers between devices  80.2 us (38%)
  Pallas kernels  49.7 us (23%)
  other arithmetic  31.6 us (15%)
  starting transfers between devices  26.3 us (12%)
  local copies, waits for them, and re-layouts  12 us (6%)
  matrix products  7.37 us (3%)
    all_to_all x2, waiting for transfers between devices, local(): lax.all_to_all(outbox, ('tile', 'phi'), split_axis=0, concat_axis=0, tile...  80.2 us
    pallas_call x1, Pallas kernels, spectra_from(): pl.pallas_call(functools.partial(spectra_kernel, groups, per_plane), out_...  23.9 us
    all_to_all x2, starting transfers between devices, local(): lax.all_to_all(outbox, ('tile', 'phi'), split_axis=0, concat_axis=0, tile...  20.3 us
    pallas_call x2, Pallas kernels, pack_outbox(): pl.pallas_call(pack_kernel, out_shape=jax.ShapeDtypeStruct((tile_count, p...  17.5 us
    add x2, other arithmetic, local(): basis = dft_basis(NPHI) + (outbox[0, 0, 0] * 0).astype(jnp.bfloat16)  16.4 us
    pallas_call x1, Pallas kernels, unpack_lhs(): pl.pallas_call(functools.partial(unpack_kernel, groups, per_plane, per_st...  8.28 us
    dot_general x1, matrix products, local(): jnp.dot(lhs.reshape(count * CG_DEV * sliver, NPHI), basis, preferred_elem...  7.37 us
    sub x1, other arithmetic, dft_basis(): values = jnp.where(is_cos, ch * cl - sh * sl, sh * cl + ch * sl)  7.04 us
  transfers between devices with their start and end apart: 3, of which 1 were waited for; matrix products, arithmetic and copies ran while one was open for 16% of the time, Pallas kernels for 15%

profile of v10, /device:TPU:97, one launch (start us, length us, event | category | flops | bytes accessed | tf_op | source)
XLA Modules:
  0.0 209.3 jit_solution(648862889508371843)
XLA Ops:
  0.0 0.7 fusion.18
  0.8 0.8 select_reduce_fusion
  1.6 0.7 multiply_add_fusion.1
  2.3 0.6 iota_reduce_fusion.1
  2.9 0.8 gather_fusion.2
  3.7 0.6 convert_divide_fusion.scale_ref
  4.3 10.9 %shard_map.55 = bf16[16,8,2,4,32,128]{5,4,3,2,1,0:T(8,128)(2,1)} custom-call(s32[64]{0:T(128)} %copy-done.7, f32[64]{0:T(128)} %convert_divide_fusion.scale_ref, bf16[32,5,64,256]{3,2,1,0:T(8,128)(2,1)} %refs_7_.3, bf16[32,5,64,256]{3,2,1,0:T(8,128)(2,1)} %refs_7_.3, bf16[32,5,64,256]{3,2,1,0:T(8,128)(2,1)} %refs_7_.3, bf16[32,5,64,256]{3,2,1,0:T(8,128)(2,1)} %refs_7_.3, ...), custom_call_target="tpu_custom_call" | custom-call | tf_op jit(solution)/shard_map/pallas_call | solution.py:68
  15.2 10.6 %all-to-all-start.1 = ((bf16[128,256,128]{2,1,0:T(8,128)(2,1)}), bf16[128,256,128]{2,1,0:T(8,128)(2,1)}, u32[]{:S(2)}, u32[]{:S(2)}) async-start(bf16[128,256,128]{2,1,0:T(8,128)(2,1)} %bitcast.96), calls=%async_computation.1 | async-start | bytes 16777216 | tf_op jit(solution)/shard_map/all_to_all | solution.py:273
  25.8 1.2 slice.18
  27.1 0.8 gather_fusion.1
  27.8 0.8 gather_fusion
  29.5 1.1 fusion.16
  30.6 2.0 fusion.14
  32.7 7.0 %multiply_subtract_fusion = (f32[32,64,2048]{2,1,0:T(8,128)S(1)}, f32[32,64,2048]{2,1,0:T(8,128)}) fusion(f32[64,2048]{1,0:T(8,128)S(1)} %get-tuple-element.14, f32[32,2048]{1,0:T(8,128)S(1)} %get-tuple-element.12, f32[64,2048]{1,0:T(8,128)S(1)} %get-tuple-element.13, f32[32,2048]{1,0:T(8,128)S(1)} %get-tuple-element.11), kind=kLoop, calls=%fused_computation.8 | loop fusion | flops 25165824 | bytes 35127296 | tf_op jit(solution)/shard_map/sub | solution.py:30
  39.7 8.3 %fusion.3.refs_32_ = bf16[2048,2048]{1,0:T(8,128)(2,1)S(1)} fusion(f32[32,64,2048]{2,1,0:T(8,128)} %get-tuple-element.10, f32[32,64,2048]{2,1,0:T(8,128)S(1)} %get-tuple-element.9, pred[2048]{0:T(1024)(128)(4,1)S(1)} %iota_compare_fusion.3, bf16[]{:T(256)} %bitcast.9), kind=kLoop, calls=%fused_computation.10 | loop fusion | flops 16777216 | bytes 41945088 | tf_op jit(solution)/shard_map/add | solution.py:272
  48.1 3.2 %copy-done.5 = bf16[2048,2048]{1,0:T(8,128)(2,1)} copy-done((bf16[2048,2048]{1,0:T(8,128)(2,1)}, bf16[2048,2048]{1,0:T(8,128)(2,1)S(1)}, u32[]{:S(2)}) %copy-start.5) | copy-done | bytes 8388632
  51.3 0.5 slice.20
  51.8 80.2 %all-to-all-done.1 = bf16[128,256,128]{2,1,0:T(8,128)(2,1)} async-done(((bf16[128,256,128]{2,1,0:T(8,128)(2,1)}), bf16[128,256,128]{2,1,0:T(8,128)(2,1)}, u32[]{:S(2)}, u32[]{:S(2)}) %all-to-all-start.1) | async-done | bytes 8388640 | tf_op jit(solution)/shard_map/all_to_all | solution.py:273
  132.0 0.6 broadcast_in_dim.17.clone
  132.6 6.0 %all-to-all-start = ((s32[128,1,4]{2,1,0:T(1,128)}), s32[128,1,4]{2,1,0:T(1,128)S(1)}, u32[]{:S(2)}, u32[]{:S(2)}) async-start(s32[128,1,4]{2,1,0:T(1,128)} %bitcast), calls=%async_computation | async-start | bytes 131072 | tf_op jit(solution)/shard_map/all_to_all | solution.py:247
  138.6 1.2 slice.19
  141.0 0.5 broadcast_add_fusion.scale_ref
  141.5 6.6 %shard_map.57 = bf16[16,8,2,1,32,128]{5,4,3,2,1,0:T(8,128)(2,1)} custom-call(s32[64]{0:T(128)} %copy-done.7, f32[64]{0:T(128)} %broadcast_add_fusion.scale_ref, bf16[32,5,64,256]{3,2,1,0:T(8,128)(2,1)} %refs_7_.3, bf16[32,5,64,256]{3,2,1,0:T(8,128)(2,1)} %refs_7_.3, bf16[32,5,64,256]{3,2,1,0:T(8,128)(2,1)} %refs_7_.3, bf16[32,5,64,256]{3,2,1,0:T(8,128)(2,1)} %refs_7_.3, ...), custom_call_target="tpu_custom_call" | custom-call | tf_op jit(solution)/shard_map/pallas_call | solution.py:68
  148.1 9.7 %all-to-all-start.2 = ((bf16[128,64,128]{2,1,0:T(8,128)(2,1)}), bf16[128,64,128]{2,1,0:T(8,128)(2,1)S(1)}, u32[]{:S(2)}, u32[]{:S(2)}) async-start(bf16[128,64,128]{2,1,0:T(8,128)(2,1)} %bitcast.98), calls=%async_computation.2 | async-start | bytes 4194304 | tf_op jit(solution)/shard_map/all_to_all | solution.py:273
  157.8 8.0 %fusion.2 = bf16[32,64,2048]{2,1,0:T(8,128)(2,1)} fusion(pred[2048]{0:T(1024)(128)(4,1)S(1)} %iota_compare_fusion.3, bf16[]{:T(256)} %bitcast.9, f32[64,2048]{1,0:T(8,128)S(1)} %get-tuple-element.14, f32[32,2048]{1,0:T(8,128)} %copy-done.6, f32[64,2048]{1,0:T(8,128)S(1)} %get-tuple-element.13, f32[32,2048]{1,0:T(8,128)S(1)} %get-tuple-element.11), kind=kLoop, calls=%fused_computation.9 | loop fusion | flops 41943040 | bytes 9963522 | tf_op jit(solution)/shard_map/add | solution.py:272
  166.1 0.9 iota_reduce_fusion
  167.1 0.6 reshape.252.row_ref
  167.6 0.6 reshape.253.half_ref
  168.3 23.9 %shard_map.56 = f32[1280,2048]{1,0:T(8,128)} custom-call(s32[256]{0:T(256)} %reshape.252.row_ref, s32[256]{0:T(256)} %reshape.253.half_ref, ...), custom_call_target="tpu_custom_call" | custom-call | tf_op jit(solution)/shard_map/pallas_call | solution.py:144
  192.3 1.3 copy-done.2
  193.6 8.3 %shard_map.58 = bf16[1,8,32,2048]{3,2,1,0:T(8,128)(2,1)} custom-call(s32[256]{0:T(256)} %reshape.252.row_ref, s32[256]{0:T(256)} %reshape.253.half_ref, bf16[256,1,32,128]{3,2,1,0:T(8,128)(2,1)} %bitcast.63, bf16[256,1,32,128]{3,2,1,0:T(8,128)(2,1)} %bitcast.95, bf16[256,1,32,128]{3,2,1,0:T(8,128)(2,1)} %bitcast.34, bf16[256,1,32,128]{3,2,1,0:T(8,128)(2,1)} %bitcast.35, ...), custom_call_target="tpu_custom_call" | custom-call | tf_op jit(solution)/shard_map/pallas_call | solution.py:204
  201.9 7.4 %convolution_dynamic-update-slice_fusion = f32[1280,2048]{1,0:T(8,128)} fusion(f32[1280,2048]{1,0:T(8,128)} %shard_map.56, bf16[256,2048]{1,0:T(8,128)(2,1)} %bitcast.100, bf16[2048,2048]{1,0:T(8,128)(2,1)} %bitcast.99), kind=kOutput, calls=%fused_computation.11 | convolution fusion | flops 2147483648 | bytes 11534336 | tf_op jit(solution)/shard_map/dot_general | solution.py:281
  (28 shorter events, 0.5 us)
Async XLA Ops:
  0.0 2.9 %copy-start = (s32[32]{0:T(128)S(1)}, s32[32]{0:T(128)}, u32[]{:S(2)}) copy-start(s32[32]{0:T(128)} %param.6) | copy-start | bytes 388
  2.9 1.4 copy-start.7
  15.2 11.9 %copy-start.3 = (s32[32]{0:T(128)S(1)}, s32[32]{0:T(128)}, u32[]{:S(2)}) copy-start(s32[32]{0:T(128)} %param.9) | copy-start | bytes 388
  15.2 12.6 %copy-start.4 = (s32[32]{0:T(128)S(1)}, s32[32]{0:T(128)}, u32[]{:S(2)}) copy-start(s32[32]{0:T(128)} %param.8) | copy-start | bytes 388
  15.2 116.8 %all-to-all-start.1 = ((bf16[128,256,128]{2,1,0:T(8,128)(2,1)}), bf16[128,256,128]{2,1,0:T(8,128)(2,1)}, u32[]{:S(2)}, u32[]{:S(2)}) async-start(bf16[128,256,128]{2,1,0:T(8,128)(2,1)} %bitcast.96), calls=%async_computation.1 | async-start | bytes 16777216 | tf_op jit(solution)/shard_map/all_to_all | solution.py:273
  30.6 9.1 %copy-start.6 = (f32[32,2048]{1,0:T(8,128)}, f32[32,2048]{1,0:T(8,128)S(1)}, u32[]{:S(2)}) copy-start(f32[32,2048]{1,0:T(8,128)S(1)} %get-tuple-element.12) | copy-start | bytes 786436
  48.0 3.2 %copy-start.5 = (bf16[2048,2048]{1,0:T(8,128)(2,1)}, bf16[2048,2048]{1,0:T(8,128)(2,1)S(1)}, u32[]{:S(2)}) copy-start(bf16[2048,2048]{1,0:T(8,128)(2,1)S(1)} %fusion.3.refs_32_) | copy-start | bytes 25165828
  132.6 15.5 %all-to-all-start = ((s32[128,1,4]{2,1,0:T(1,128)}), s32[128,1,4]{2,1,0:T(1,128)S(1)}, u32[]{:S(2)}, u32[]{:S(2)}) async-start(s32[128,1,4]{2,1,0:T(1,128)} %bitcast), calls=%async_computation | async-start | bytes 131072 | tf_op jit(solution)/shard_map/all_to_all | solution.py:247
  148.1 44.2 %all-to-all-start.2 = ((bf16[128,64,128]{2,1,0:T(8,128)(2,1)}), bf16[128,64,128]{2,1,0:T(8,128)(2,1)S(1)}, u32[]{:S(2)}, u32[]{:S(2)}) async-start(bf16[128,64,128]{2,1,0:T(8,128)(2,1)} %bitcast.98), calls=%async_computation.2 | async-start | bytes 4194304 | tf_op jit(solution)/shard_map/all_to_all | solution.py:273
  192.3 1.4 copy-start.2
  193.6 15.7 %copy-start.1 = (s32[32]{0:T(128)S(1)}, s32[32]{0:T(128)}, u32[]{:S(2)}) copy-start(s32[32]{0:T(128)} %param.6) | copy-start | bytes 388

commit v11 on v8

--- a/solution.py
+++ b/solution.py
@@ -101,20 +101,18 @@
                 keep = half_ref[index] == side
                 parts.append(jnp.where(keep, piece, turned))
             merged = jnp.where(lane < lanes // 2, parts[0], parts[1])
-            lhs_ref[:, group, :, quad * lanes : (quad + 1) * lanes] = merged
-
-    @pl.when(segment == 0)
+            start = pl.multiple_of(segment * (lanes * per_plane // 2) + quad * lanes, lanes)
+            lhs_ref[:, group, :, pl.ds(start, lanes)] = merged
+
+    @pl.when(segment == pl.num_programs(0) - 1)
     def _():
-        out_ref[...] = jnp.zeros_like(out_ref)
-
-    rows = out_ref.shape[0]
-    lhs = lhs_ref[...].reshape(rows, lhs_ref.shape[-1])
-    width = 512
-    for chunk in range(out_ref.shape[1] // width):
-        columns = slice(chunk * width, (chunk + 1) * width)
-        out_ref[:, columns] += jnp.dot(
-            lhs, basis_ref[:, columns], preferred_element_type=jnp.float32
-        )
+        lhs = lhs_ref[...].reshape(out_ref.shape[0], lhs_ref.shape[-1])
+        width = 512
+        for chunk in range(out_ref.shape[1] // width):
+            columns = slice(chunk * width, (chunk + 1) * width)
+            out_ref[:, columns] = jnp.dot(
+                lhs, basis_ref[:, columns], preferred_element_type=jnp.float32
+            )
 
 
 def spectra_from(landed, row, half, basis, plane_count, per_plane, groups):
@@ -133,7 +131,7 @@
         for position in range(per_plane)
         for group in range(groups)
     ]
-    in_specs.append(pl.BlockSpec((depth, length), lambda s, row_ref, half_ref: (s, 0)))
+    in_specs.append(pl.BlockSpec((length, length), lambda s, row_ref, half_ref: (0, 0)))
     rows = fields * groups * sliver
     return pl.pallas_call(
         functools.partial(spectra_kernel, groups, per_plane),
@@ -143,10 +141,12 @@
             grid=(plane_count,),
             in_specs=in_specs,
             out_specs=pl.BlockSpec((rows, length), lambda s, row_ref, half_ref: (0, 0)),
-            scratch_shapes=[pltpu.VMEM((fields, groups, sliver, depth), landed.dtype)],
+            scratch_shapes=[
+                pltpu.VMEM((fields, groups, sliver, plane_count * depth), landed.dtype)
+            ],
         ),
         compiler_params=pltpu.CompilerParams(
-            dimension_semantics=("arbitrary",), vmem_limit_bytes=60 * 1024 * 1024
+            dimension_semantics=("arbitrary",), vmem_limit_bytes=63 * 1024 * 1024
         ),
     )(row, half, *([landed] * (per_plane * groups)), basis)
 

time: 207 us -> 208 us (level)
  Pallas kernels: 39.4 us -> 41.5 us
  transfers between devices with their start and end apart: 2 -> 2, of which waited for: 1 -> 1; matrix products, arithmetic and copies ran while one was open for 12% -> 12% of each run, Pallas kernels for 5% -> 6%
where the time goes in v11:
time: 208 us; the launch traced here: 207 us
  waiting for transfers between devices  113 us (54%)
  Pallas kernels  41.5 us (20%)
  other arithmetic  25.7 us (12%)
  starting transfers between devices  20.6 us (10%)
  local copies, waits for them, and re-layouts  5.91 us (3%)
    all_to_all x1, waiting for transfers between devices, local(): lax.all_to_all(outbox, ('tile', 'phi'), split_axis=0, concat_axis=0, tile...  113 us
    pallas_call x1, Pallas kernels, spectra_from(): pl.pallas_call(functools.partial(spectra_kernel, groups, per_plane), out_...  28.9 us
    pallas_call x1, Pallas kernels, pack_outbox(): pl.pallas_call(pack_kernel, out_shape=jax.ShapeDtypeStruct((tile_count, p...  12.6 us
    convert_element_type x1, other arithmetic, dft_basis(): return values.reshape(length, length).astype(jnp.bfloat16)  10.9 us
    all_to_all x1, starting transfers between devices, local(): lax.all_to_all(outbox, ('tile', 'phi'), split_axis=0, concat_axis=0, tile...  10.4 us
    all_to_all x1, starting transfers between devices, local(): lax.all_to_all(code_out, ('tile', 'phi'), split_axis=0, concat_axis=0, ti...  10.2 us
    sub x1, other arithmetic, dft_basis(): values = jnp.where(is_cos, ch * cl - sh * sl, sh * cl + ch * sl)  7.04 us
  transfers between devices with their start and end apart: 2, of which 1 were waited for; matrix products, arithmetic and copies ran while one was open for 12% of the time, Pallas kernels for 6%

profile of v11, /device:TPU:97, one launch (start us, length us, event | category | flops | bytes accessed | tf_op | source)
XLA Modules:
  0.0 207.0 jit_solution(8336096711290126124)
XLA Ops:
  0.0 0.0 copy-start
  0.0 0.7 fusion.16
  0.7 0.1 reduce_window_sum.11
  0.8 0.8 select_reduce_fusion
  1.6 0.7 multiply_add_fusion.1
  2.3 0.6 iota_reduce_fusion.1
  2.9 0.0 copy-start.2
  2.9 0.1 fusion.15
  3.0 0.0 copy-done
  3.0 0.8 gather_fusion
  3.8 1.4 gather_fusion.1
  5.2 0.1 select_n.84
  5.3 0.6 broadcast_in_dim.15.clone
  6.0 10.2 %all-to-all-start = ((s32[128,1,4]{2,1,0:T(1,128)}), s32[128,1,4]{2,1,0:T(1,128)S(1)}, u32[]{:S(2)}, u32[]{:S(2)}) async-start(s32[128,1,4]{2,1,0:T(1,128)} %bitcast), calls=%async_computation | async-start | bytes 131072 | tf_op jit(solution)/shard_map/all_to_all | solution.py:184
  16.1 1.4 gather_fusion.2
  17.6 0.5 convert_divide_fusion.scale_ref
  18.1 0.0 copy-done.2
  18.1 12.6 %shard_map.55 = bf16[16,8,2,5,32,128]{5,4,3,2,1,0:T(8,128)(2,1)} custom-call(s32[64]{0:T(128)} %copy-done.2, f32[64]{0:T(128)} %convert_divide_fusion.scale_ref, bf16[32,5,64,256]{3,2,1,0:T(8,128)(2,1)} %refs_7_.1, bf16[32,5,64,256]{3,2,1,0:T(8,128)(2,1)} %refs_7_.1, bf16[32,5,64,256]{3,2,1,0:T(8,128)(2,1)} %refs_7_.1, bf16[32,5,64,256]{3,2,1,0:T(8,128)(2,1)} %refs_7_.1, ...), custom_call_target="tpu_custom_call" | custom-call | tf_op jit(solution)/shard_map/pallas_call | solution.py:68
  30.7 0.0 all-to-all-done
  30.7 10.4 %all-to-all-start.1 = ((bf16[128,320,128]{2,1,0:T(8,128)(2,1)}), bf16[128,320,128]{2,1,0:T(8,128)(2,1)}, u32[]{:S(2)}, u32[]{:S(2)}) async-start(bf16[128,320,128]{2,1,0:T(8,128)(2,1)} %bitcast.17), calls=%async_computation.1 | async-start | bytes 20971520 | tf_op jit(solution)/shard_map/all_to_all | solution.py:183
  41.1 1.1 fusion.14
  42.2 2.0 fusion.12
  44.3 7.0 %multiply_subtract_fusion = (f32[32,64,2048]{2,1,0:T(8,128)S(1)}, f32[32,64,2048]{2,1,0:T(8,128)}) fusion(f32[64,2048]{1,0:T(8,128)S(1)} %get-tuple-element.14, f32[32,2048]{1,0:T(8,128)S(1)} %get-tuple-element.12, f32[64,2048]{1,0:T(8,128)S(1)} %get-tuple-element.13, f32[32,2048]{1,0:T(8,128)S(1)} %get-tuple-element.11), kind=kLoop, calls=%fused_computation.7 | loop fusion | flops 25165824 | bytes 35127296 | tf_op jit(solution)/shard_map/sub | solution.py:30
  51.3 10.9 %fusion.1.refs_32_ = bf16[2048,2048]{1,0:T(8,128)(2,1)} fusion(f32[32,64,2048]{2,1,0:T(8,128)} %get-tuple-element.10, f32[32,64,2048]{2,1,0:T(8,128)S(1)} %get-tuple-element.9, pred[2048]{0:T(1024)(128)(4,1)S(1)} %iota_compare_fusion.3), kind=kLoop, calls=%fused_computation.5 | loop fusion | flops 12582912 | bytes 41945088 | tf_op jit(solution)/shard_map/convert_element_type | solution.py:32
  62.3 0.2 copy.21
  62.4 0.1 copy.22
  62.5 1.0 iota_reduce_fusion
  63.5 0.7 reshape.192.row_ref
  64.2 0.6 reshape.193.half_ref
  64.8 113.1 %all-to-all-done.1 = bf16[128,320,128]{2,1,0:T(8,128)(2,1)} async-done(((bf16[128,320,128]{2,1,0:T(8,128)(2,1)}), bf16[128,320,128]{2,1,0:T(8,128)(2,1)}, u32[]{:S(2)}, u32[]{:S(2)}) %all-to-all-start.1) | async-done | bytes 10485792 | tf_op jit(solution)/shard_map/all_to_all | solution.py:183
  177.9 28.9 %shard_map.56 = f32[1280,2048]{1,0:T(8,128)} custom-call(s32[256]{0:T(256)} %reshape.192.row_ref, s32[256]{0:T(256)} %reshape.193.half_ref, ...), custom_call_target="tpu_custom_call" | custom-call | tf_op jit(solution)/shard_map/pallas_call | solution.py:136
  206.8 0.0 copy-done.1
  (8 shorter events, 0.1 us)
Async XLA Ops:
  0.0 3.0 %copy-start = (s32[32]{0:T(128)S(1)}, s32[32]{0:T(128)}, u32[]{:S(2)}) copy-start(s32[32]{0:T(128)} %param.8) | copy-start | bytes 388
  2.9 15.2 %copy-start.2 = (s32[64]{0:T(128)}, s32[64]{0:T(128)S(1)}, u32[]{:S(2)}) copy-start(s32[64]{0:T(128)S(1)} %get-tuple-element.7.source_ref) | copy-start | bytes 772
  6.0 24.7 %all-to-all-start = ((s32[128,1,4]{2,1,0:T(1,128)}), s32[128,1,4]{2,1,0:T(1,128)S(1)}, u32[]{:S(2)}, u32[]{:S(2)}) async-start(s32[128,1,4]{2,1,0:T(1,128)} %bitcast), calls=%async_computation | async-start | bytes 131072 | tf_op jit(solution)/shard_map/all_to_all | solution.py:184
  30.7 147.2 %all-to-all-start.1 = ((bf16[128,320,128]{2,1,0:T(8,128)(2,1)}), bf16[128,320,128]{2,1,0:T(8,128)(2,1)}, u32[]{:S(2)}, u32[]{:S(2)}) async-start(bf16[128,320,128]{2,1,0:T(8,128)(2,1)} %bitcast.17), calls=%async_computation.1 | async-start | bytes 20971520 | tf_op jit(solution)/shard_map/all_to_all | solution.py:183
  177.9 28.9 %copy-start.1 = (s32[32]{0:T(128)S(1)}, s32[32]{0:T(128)}, u32[]{:S(2)}) copy-start(s32[32]{0:T(128)} %param.8) | copy-start | bytes 388

commit v12 on v11

--- a/solution.py
+++ b/solution.py
@@ -86,67 +86,72 @@
 def spectra_kernel(groups, per_plane, row_ref, half_ref, *refs):
     pieces = refs[: per_plane * groups]
     basis_ref, out_ref, lhs_ref = refs[per_plane * groups :]
-    segment = pl.program_id(0)
-    lanes = pieces[0].shape[-1]
-    shape = pieces[0].shape[1:]
-    lane = lax.broadcasted_iota(jnp.int32, shape, 2)
-    for group in range(groups):
-        for quad in range(per_plane // 2):
-            parts = []
-            for side in range(2):
-                position = quad * 2 + side
-                index = (segment * per_plane + position) * groups + group
-                piece = pieces[position * groups + group][0]
-                turned = pltpu.roll(piece, lanes // 2, 2)
-                keep = half_ref[index] == side
-                parts.append(jnp.where(keep, piece, turned))
-            merged = jnp.where(lane < lanes // 2, parts[0], parts[1])
-            start = pl.multiple_of(segment * (lanes * per_plane // 2) + quad * lanes, lanes)
-            lhs_ref[:, group, :, pl.ds(start, lanes)] = merged
-
-    @pl.when(segment == pl.num_programs(0) - 1)
+    step = pl.program_id(0)
+    segments = lhs_ref.shape[-1] // (pieces[0].shape[-1] * per_plane // 2)
+
+    @pl.when(step < segments)
+    def _():
+        lanes = pieces[0].shape[-1]
+        shape = pieces[0].shape[1:]
+        lane = lax.broadcasted_iota(jnp.int32, shape, 2)
+        for group in range(groups):
+            for quad in range(per_plane // 2):
+                parts = []
+                for side in range(2):
+                    position = quad * 2 + side
+                    index = (step * per_plane + position) * groups + group
+                    piece = pieces[position * groups + group][0]
+                    turned = pltpu.roll(piece, lanes // 2, 2)
+                    keep = half_ref[index] == side
+                    parts.append(jnp.where(keep, piece, turned))
+                merged = jnp.where(lane < lanes // 2, parts[0], parts[1])
+                start = pl.multiple_of(step * (lanes * per_plane // 2) + quad * lanes, lanes)
+                lhs_ref[:, group, :, pl.ds(start, lanes)] = merged
+
+    @pl.when(step >= segments)
     def _():
         lhs = lhs_ref[...].reshape(out_ref.shape[0], lhs_ref.shape[-1])
-        width = 512
-        for chunk in range(out_ref.shape[1] // width):
-            columns = slice(chunk * width, (chunk + 1) * width)
-            out_ref[:, columns] = jnp.dot(
-                lhs, basis_ref[:, columns], preferred_element_type=jnp.float32
-            )
+        out_ref[...] = jnp.dot(lhs, basis_ref[...], preferred_element_type=jnp.float32)
 
 
 def spectra_from(landed, row, half, basis, plane_count, per_plane, groups):
     _, fields, sliver, lanes = landed.shape
     depth = per_plane * lanes // 2
     length = basis.shape[1]
+    width = 512
+    chunks = length // width
 
     def piece_map(position, group):
         def index_map(s, row_ref, half_ref):
-            return (row_ref[(s * per_plane + position) * groups + group], 0, 0, 0)
+            segment = jnp.minimum(s, plane_count - 1)
+            return (row_ref[(segment * per_plane + position) * groups + group], 0, 0, 0)
 
         return index_map
+
+    def column_map(s, row_ref, half_ref):
+        return (0, jnp.maximum(s - plane_count, 0))
 
     in_specs = [
         pl.BlockSpec((1, fields, sliver, lanes), piece_map(position, group))
         for position in range(per_plane)
         for group in range(groups)
     ]
-    in_specs.append(pl.BlockSpec((length, length), lambda s, row_ref, half_ref: (0, 0)))
+    in_specs.append(pl.BlockSpec((basis.shape[0], width), column_map))
     rows = fields * groups * sliver
     return pl.pallas_call(
         functools.partial(spectra_kernel, groups, per_plane),
         out_shape=jax.ShapeDtypeStruct((rows, length), jnp.float32),
         grid_spec=pltpu.PrefetchScalarGridSpec(
             num_scalar_prefetch=2,
-            grid=(plane_count,),
+            grid=(plane_count + chunks,),
             in_specs=in_specs,
-            out_specs=pl.BlockSpec((rows, length), lambda s, row_ref, half_ref: (0, 0)),
+            out_specs=pl.BlockSpec((rows, width), column_map),
             scratch_shapes=[
                 pltpu.VMEM((fields, groups, sliver, plane_count * depth), landed.dtype)
             ],
         ),
         compiler_params=pltpu.CompilerParams(
-            dimension_semantics=("arbitrary",), vmem_limit_bytes=63 * 1024 * 1024
+            dimension_semantics=("arbitrary",), vmem_limit_bytes=48 * 1024 * 1024
         ),
     )(row, half, *([landed] * (per_plane * groups)), basis)
 

time: 208 us -> 206 us (level)
  Pallas kernels: 41.5 us -> 39.2 us
where the time goes in v12:
time: 206 us; the launch traced here: 205 us
  waiting for transfers between devices  114 us (55%)
  Pallas kernels  39.2 us (19%)
  other arithmetic  25.7 us (12%)
  starting transfers between devices  20.7 us (10%)
  local copies, waits for them, and re-layouts  4.75 us (2%)
    all_to_all x1, waiting for transfers between devices, local(): lax.all_to_all(outbox, ('tile', 'phi'), split_axis=0, concat_axis=0, tile...  114 us
    pallas_call x1, Pallas kernels, spectra_from(): pl.pallas_call(functools.partial(spectra_kernel, groups, per_plane), out_...  27.2 us
    pallas_call x1, Pallas kernels, pack_outbox(): pl.pallas_call(pack_kernel, out_shape=jax.ShapeDtypeStruct((tile_count, p...  12 us
    convert_element_type x1, other arithmetic, dft_basis(): return values.reshape(length, length).astype(jnp.bfloat16)  10.9 us
    all_to_all x1, starting transfers between devices, local(): lax.all_to_all(outbox, ('tile', 'phi'), split_axis=0, concat_axis=0, tile...  10.6 us
    all_to_all x1, starting transfers between devices, local(): lax.all_to_all(code_out, ('tile', 'phi'), split_axis=0, concat_axis=0, ti...  10.2 us
    sub x1, other arithmetic, dft_basis(): values = jnp.where(is_cos, ch * cl - sh * sl, sh * cl + ch * sl)  7.04 us
  transfers between devices with their start and end apart: 2, of which 1 were waited for; matrix products, arithmetic and copies ran while one was open for 12% of the time, Pallas kernels for 6%

profile of v12, /device:TPU:97, one launch (start us, length us, event | category | flops | bytes accessed | tf_op | source)
XLA Modules:
  0.0 204.7 jit_solution(15211404823769413394)
XLA Ops:
  0.0 0.0 copy-start
  0.0 0.7 fusion.16
  0.7 0.1 reduce_window_sum.11
  0.8 0.8 select_reduce_fusion
  1.6 0.7 multiply_add_fusion.1
  2.3 0.6 iota_reduce_fusion.1
  2.9 0.0 copy-start.2
  2.9 0.1 fusion.15
  3.0 0.0 copy-done
  3.0 0.8 gather_fusion
  3.8 1.4 gather_fusion.1
  5.2 0.1 select_n.84
  5.3 0.6 broadcast_in_dim.15.clone
  6.0 10.2 %all-to-all-start = ((s32[128,1,4]{2,1,0:T(1,128)}), s32[128,1,4]{2,1,0:T(1,128)S(1)}, u32[]{:S(2)}, u32[]{:S(2)}) async-start(s32[128,1,4]{2,1,0:T(1,128)} %bitcast), calls=%async_computation | async-start | bytes 131072 | tf_op jit(solution)/shard_map/all_to_all | solution.py:189
  16.1 1.4 gather_fusion.2
  17.6 0.5 convert_divide_fusion.scale_ref
  18.1 0.0 copy-done.2
  18.1 12.0 %shard_map.55 = bf16[16,8,2,5,32,128]{5,4,3,2,1,0:T(8,128)(2,1)} custom-call(s32[64]{0:T(128)} %copy-done.2, f32[64]{0:T(128)} %convert_divide_fusion.scale_ref, bf16[32,5,64,256]{3,2,1,0:T(8,128)(2,1)} %refs_7_.1, bf16[32,5,64,256]{3,2,1,0:T(8,128)(2,1)} %refs_7_.1, bf16[32,5,64,256]{3,2,1,0:T(8,128)(2,1)} %refs_7_.1, bf16[32,5,64,256]{3,2,1,0:T(8,128)(2,1)} %refs_7_.1, ...), custom_call_target="tpu_custom_call" | custom-call | tf_op jit(solution)/shard_map/pallas_call | solution.py:68
  30.1 0.0 all-to-all-done
  30.1 10.6 %all-to-all-start.1 = ((bf16[128,320,128]{2,1,0:T(8,128)(2,1)}), bf16[128,320,128]{2,1,0:T(8,128)(2,1)}, u32[]{:S(2)}, u32[]{:S(2)}) async-start(bf16[128,320,128]{2,1,0:T(8,128)(2,1)} %bitcast.17), calls=%async_computation.1 | async-start | bytes 20971520 | tf_op jit(solution)/shard_map/all_to_all | solution.py:188
  40.7 1.1 fusion.14
  41.8 2.0 fusion.12
  43.9 7.0 %multiply_subtract_fusion = (f32[32,64,2048]{2,1,0:T(8,128)S(1)}, f32[32,64,2048]{2,1,0:T(8,128)}) fusion(f32[64,2048]{1,0:T(8,128)S(1)} %get-tuple-element.14, f32[32,2048]{1,0:T(8,128)S(1)} %get-tuple-element.12, f32[64,2048]{1,0:T(8,128)S(1)} %get-tuple-element.13, f32[32,2048]{1,0:T(8,128)S(1)} %get-tuple-element.11), kind=kLoop, calls=%fused_computation.7 | loop fusion | flops 25165824 | bytes 35127296 | tf_op jit(solution)/shard_map/sub | solution.py:30
  50.9 10.9 %fusion.1.refs_32_ = bf16[2048,2048]{1,0:T(8,128)(2,1)} fusion(f32[32,64,2048]{2,1,0:T(8,128)} %get-tuple-element.10, f32[32,64,2048]{2,1,0:T(8,128)S(1)} %get-tuple-element.9, pred[2048]{0:T(1024)(128)(4,1)S(1)} %iota_compare_fusion.3), kind=kLoop, calls=%fused_computation.5 | loop fusion | flops 12582912 | bytes 41945088 | tf_op jit(solution)/shard_map/convert_element_type | solution.py:32
  61.8 0.2 copy.21
  62.0 0.1 copy.22
  62.1 1.0 iota_reduce_fusion
  63.0 0.1 reshape.192.row_ref
  63.1 0.1 reshape.193.half_ref
  63.2 114.3 %all-to-all-done.1 = bf16[128,320,128]{2,1,0:T(8,128)(2,1)} async-done(((bf16[128,320,128]{2,1,0:T(8,128)(2,1)}), bf16[128,320,128]{2,1,0:T(8,128)(2,1)}, u32[]{:S(2)}, u32[]{:S(2)}) %all-to-all-start.1) | async-done | bytes 10485792 | tf_op jit(solution)/shard_map/all_to_all | solution.py:188
  177.5 27.2 %shard_map.56 = f32[1280,2048]{1,0:T(8,128)} custom-call(s32[256]{0:T(256)S(1)} %reshape.192.row_ref, s32[256]{0:T(256)S(1)} %reshape.193.half_ref, ...), custom_call_target="tpu_custom_call" | custom-call | tf_op jit(solution)/shard_map/pallas_call | solution.py:141
  204.7 0.0 copy-done.1
  (8 shorter events, 0.1 us)
Async XLA Ops:
  0.0 3.0 %copy-start = (s32[32]{0:T(128)S(1)}, s32[32]{0:T(128)}, u32[]{:S(2)}) copy-start(s32[32]{0:T(128)} %param.8) | copy-start | bytes 388
  2.9 15.2 %copy-start.2 = (s32[64]{0:T(128)}, s32[64]{0:T(128)S(1)}, u32[]{:S(2)}) copy-start(s32[64]{0:T(128)S(1)} %get-tuple-element.7.source_ref) | copy-start | bytes 772
  6.0 24.1 %all-to-all-start = ((s32[128,1,4]{2,1,0:T(1,128)}), s32[128,1,4]{2,1,0:T(1,128)S(1)}, u32[]{:S(2)}, u32[]{:S(2)}) async-start(s32[128,1,4]{2,1,0:T(1,128)} %bitcast), calls=%async_computation | async-start | bytes 131072 | tf_op jit(solution)/shard_map/all_to_all | solution.py:189
  30.1 147.4 %all-to-all-start.1 = ((bf16[128,320,128]{2,1,0:T(8,128)(2,1)}), bf16[128,320,128]{2,1,0:T(8,128)(2,1)}, u32[]{:S(2)}, u32[]{:S(2)}) async-start(bf16[128,320,128]{2,1,0:T(8,128)(2,1)} %bitcast.17), calls=%async_computation.1 | async-start | bytes 20971520 | tf_op jit(solution)/shard_map/all_to_all | solution.py:188
  177.5 27.2 %copy-start.1 = (s32[32]{0:T(128)S(1)}, s32[32]{0:T(128)}, u32[]{:S(2)}) copy-start(s32[32]{0:T(128)} %param.8) | copy-start | bytes 388

commit v13 on v12

--- a/solution.py
+++ b/solution.py
@@ -32,7 +32,14 @@
     return values.reshape(length, length).astype(jnp.bfloat16)
 
 
-def pack_kernel(source_ref, scale_ref, *refs):
+def level_scale(level, dtype):
+    value = jnp.where(
+        level == 0, 1.0, jnp.where(level == 1, 0.5, jnp.where(level == 2, 0.25, 0.125))
+    )
+    return value.astype(jnp.float32).astype(dtype)
+
+
+def pack_kernel(source_ref, level_ref, *refs):
     out_ref = refs[-1]
     per_step, planes, pairs, fields, sliver = out_ref.shape[:5]
     step = pl.program_id(0)
@@ -40,8 +47,8 @@
         for pair in range(pairs):
             slot = (local_tile * pairs + pair) * 2
             first = step * (len(refs) - 1) + slot
-            first_scale = scale_ref[first].astype(out_ref.dtype)
-            second_scale = scale_ref[first + 1].astype(out_ref.dtype)
+            first_scale = level_scale(level_ref[source_ref[first]], out_ref.dtype)
+            second_scale = level_scale(level_ref[source_ref[first + 1]], out_ref.dtype)
             for field in range(fields):
                 both = jnp.concatenate(
                     [
@@ -54,16 +61,16 @@
                 out_ref[local_tile, :, pair, field] = flipped.astype(out_ref.dtype)
 
 
-def pack_outbox(blocks, source, scale, tile_count, capacity, plane_count):
+def pack_outbox(blocks, source, levels, tile_count, capacity, plane_count):
     slot_count, fields, bphi, cols = blocks.shape
     pairs = capacity // 2
     sliver = cols // plane_count
 
-    per_step = 2
+    per_step = 4
     per_call = per_step * capacity
 
     def block_map(slot):
-        return lambda t, src_ref: (src_ref[t * per_call + slot], 0, 0, 0)
+        return lambda t, src_ref, level_ref: (src_ref[t * per_call + slot], 0, 0, 0)
 
     return pl.pallas_call(
         pack_kernel,
@@ -71,16 +78,15 @@
             (tile_count, plane_count, pairs, fields, sliver, 2 * bphi), blocks.dtype
         ),
         grid_spec=pltpu.PrefetchScalarGridSpec(
-            num_scalar_prefetch=1,
+            num_scalar_prefetch=2,
             grid=(tile_count // per_step,),
-            in_specs=[pl.BlockSpec(memory_space=pltpu.SMEM)]
-            + [pl.BlockSpec((1, fields, bphi, cols), block_map(slot)) for slot in range(per_call)],
+            in_specs=[pl.BlockSpec((1, fields, bphi, cols), block_map(slot)) for slot in range(per_call)],
             out_specs=pl.BlockSpec(
                 (per_step, plane_count, pairs, fields, sliver, 2 * bphi),
-                lambda t, src_ref: (t, 0, 0, 0, 0, 0),
+                lambda t, src_ref, level_ref: (t, 0, 0, 0, 0, 0),
             ),
         ),
-    )(source, scale, *([blocks] * per_call))
+    )(source, levels, *([blocks] * per_call))
 
 
 def spectra_kernel(groups, per_plane, row_ref, half_ref, *refs):
@@ -176,11 +182,10 @@
     source = jnp.argmax(match, axis=1).astype(jnp.int32)
     place = block_phi[source] * CG_DEV + block_group[source]
     code = jnp.where(filled, place, -1)
-    scale = 1.0 / jnp.left_shift(1, levels[source]).astype(jnp.float32)
     device_count = tile_count * plane_count
     pairs = capacity // 2
 
-    outbox = pack_outbox(blocks, source, scale, tile_count, capacity, plane_count)
+    outbox = pack_outbox(blocks, source, levels, tile_count, capacity, plane_count)
     outbox = outbox.reshape(device_count, pairs * fields * sliver, 2 * BPHI)
     code_out = jnp.broadcast_to(
         code.reshape(tile_count, 1, capacity), (tile_count, plane_count, capacity)

time: 206 us -> 203 us (0.985)
  transfers between devices with their start and end apart: 2 -> 2, of which waited for: 1 -> 1; matrix products, arithmetic and copies ran while one was open for 12% -> 11% of each run, Pallas kernels for 6% -> 5%
where the time goes in v13:
time: 203 us
  waiting for transfers between devices  115 us (57%)
  Pallas kernels  37.8 us (19%)
  other arithmetic  25.1 us (12%)
  starting transfers between devices  21.2 us (10%)
  local copies, waits for them, and re-layouts  3.32 us (2%)
    all_to_all x1, waiting for transfers between devices, local(): lax.all_to_all(outbox, ('tile', 'phi'), split_axis=0, concat_axis=0, tile...  115 us
    pallas_call x1, Pallas kernels, spectra_from(): pl.pallas_call(functools.partial(spectra_kernel, groups, per_plane), out_...  27.2 us
    all_to_all x1, starting transfers between devices, local(): lax.all_to_all(outbox, ('tile', 'phi'), split_axis=0, concat_axis=0, tile...  11 us
    convert_element_type x1, other arithmetic, dft_basis(): return values.reshape(length, length).astype(jnp.bfloat16)  10.9 us
    pallas_call x1, Pallas kernels, pack_outbox(): pl.pallas_call(pack_kernel, out_shape=jax.ShapeDtypeStruct((tile_count, p...  10.6 us
    all_to_all x1, starting transfers between devices, local(): lax.all_to_all(code_out, ('tile', 'phi'), split_axis=0, concat_axis=0, ti...  10.2 us
    sub x1, other arithmetic, dft_basis(): values = jnp.where(is_cos, ch * cl - sh * sl, sh * cl + ch * sl)  7.04 us
  transfers between devices with their start and end apart: 2, of which 1 were waited for; matrix products, arithmetic and copies ran while one was open for 11% of the time, Pallas kernels for 5%

profile of v13, /device:TPU:97, one launch (start us, length us, event | category | flops | bytes accessed | tf_op | source)
XLA Modules:
  0.0 202.7 jit_solution(15803122459686195597)
XLA Ops:
  0.0 0.0 copy-start
  0.0 0.7 fusion.16
  0.7 0.1 reduce_window_sum.11
  0.8 0.8 select_reduce_fusion
  1.6 0.7 multiply_add_fusion.1
  2.3 0.6 iota_reduce_fusion.1
  2.9 0.0 copy-start.2
  2.9 0.1 fusion.15
  3.0 0.0 copy-done
  3.0 0.8 gather_fusion
  3.8 1.4 gather_fusion.1
  5.2 0.1 select_n.83
  5.3 0.6 broadcast_in_dim.15.clone
  6.0 10.2 %all-to-all-start = ((s32[128,1,4]{2,1,0:T(1,128)}), s32[128,1,4]{2,1,0:T(1,128)S(1)}, u32[]{:S(2)}, u32[]{:S(2)}) async-start(s32[128,1,4]{2,1,0:T(1,128)} %bitcast), calls=%async_computation | async-start | bytes 131072 | tf_op jit(solution)/shard_map/all_to_all | solution.py:194
  16.1 0.0 copy-done.2
  16.2 10.6 %shard_map.55 = bf16[16,8,2,5,32,128]{5,4,3,2,1,0:T(8,128)(2,1)} custom-call(s32[64]{0:T(128)} %copy-done.2, s32[32]{0:T(128)} %level_ref.1, bf16[32,5,64,256]{3,2,1,0:T(8,128)(2,1)} %refs_15_.1, bf16[32,5,64,256]{3,2,1,0:T(8,128)(2,1)} %refs_15_.1, bf16[32,5,64,256]{3,2,1,0:T(8,128)(2,1)} %refs_15_.1, bf16[32,5,64,256]{3,2,1,0:T(8,128)(2,1)} %refs_15_.1, ...), custom_call_target="tpu_custom_call" | custom-call | tf_op jit(solution)/shard_map/pallas_call | solution.py:75
  26.8 0.0 all-to-all-done
  26.8 11.0 %all-to-all-start.1 = ((bf16[128,320,128]{2,1,0:T(8,128)(2,1)}), bf16[128,320,128]{2,1,0:T(8,128)(2,1)}, u32[]{:S(2)}, u32[]{:S(2)}) async-start(bf16[128,320,128]{2,1,0:T(8,128)(2,1)} %bitcast.17), calls=%async_computation.1 | async-start | bytes 20971520 | tf_op jit(solution)/shard_map/all_to_all | solution.py:193
  37.8 1.1 fusion.14
  38.9 2.0 %fusion.12 = (f32[64,2048]{1,0:T(8,128)S(1)}, f32[64,2048]{1,0:T(8,128)S(1)}) fusion(s32[2048]{0:T(1024)S(1)} %add_select_fusion.2), kind=kLoop, calls=%fused_computation.25 | loop fusion | flops 1835008 | bytes 1056768 | tf_op jit(solution)/shard_map/cos | solution.py:28
  41.0 7.0 %multiply_subtract_fusion = (f32[32,64,2048]{2,1,0:T(8,128)S(1)}, f32[32,64,2048]{2,1,0:T(8,128)}) fusion(f32[64,2048]{1,0:T(8,128)S(1)} %get-tuple-element.14, f32[32,2048]{1,0:T(8,128)S(1)} %get-tuple-element.12, f32[64,2048]{1,0:T(8,128)S(1)} %get-tuple-element.13, f32[32,2048]{1,0:T(8,128)S(1)} %get-tuple-element.11), kind=kLoop, calls=%fused_computation.6 | loop fusion | flops 25165824 | bytes 35127296 | tf_op jit(solution)/shard_map/sub | solution.py:30
  48.0 10.9 %fusion.1.refs_32_ = bf16[2048,2048]{1,0:T(8,128)(2,1)} fusion(f32[32,64,2048]{2,1,0:T(8,128)} %get-tuple-element.10, f32[32,64,2048]{2,1,0:T(8,128)S(1)} %get-tuple-element.9, pred[2048]{0:T(1024)(128)(4,1)S(1)} %iota_compare_fusion.3), kind=kLoop, calls=%fused_computation.4 | loop fusion | flops 12582912 | bytes 41945088 | tf_op jit(solution)/shard_map/convert_element_type | solution.py:32
  59.0 0.2 copy.21
  59.1 0.1 copy.22
  59.2 1.0 iota_reduce_fusion
  60.2 0.1 reshape.192.row_ref
  60.3 0.1 reshape.193.half_ref
  60.3 115.0 %all-to-all-done.1 = bf16[128,320,128]{2,1,0:T(8,128)(2,1)} async-done(((bf16[128,320,128]{2,1,0:T(8,128)(2,1)}), bf16[128,320,128]{2,1,0:T(8,128)(2,1)}, u32[]{:S(2)}, u32[]{:S(2)}) %all-to-all-start.1) | async-done | bytes 10485792 | tf_op jit(solution)/shard_map/all_to_all | solution.py:193
  175.3 0.0 copy-start.1
  175.3 27.2 %shard_map.56 = f32[1280,2048]{1,0:T(8,128)} custom-call(s32[256]{0:T(256)S(1)} %reshape.192.row_ref, s32[256]{0:T(256)S(1)} %reshape.193.half_ref, ...), custom_call_target="tpu_custom_call" | custom-call | tf_op jit(solution)/shard_map/pallas_call | solution.py:147
  202.5 0.0 copy-done.1
  (7 shorter events, 0.1 us)
Async XLA Ops:
  0.0 3.0 %copy-start = (s32[32]{0:T(128)S(1)}, s32[32]{0:T(128)}, u32[]{:S(2)}) copy-start(s32[32]{0:T(128)} %param.8) | copy-start | bytes 388
  2.9 13.2 %copy-start.2 = (s32[64]{0:T(128)}, s32[64]{0:T(128)S(1)}, u32[]{:S(2)}) copy-start(s32[64]{0:T(128)S(1)} %get-tuple-element.7.source_ref) | copy-start | bytes 772
  6.0 20.8 %all-to-all-start = ((s32[128,1,4]{2,1,0:T(1,128)}), s32[128,1,4]{2,1,0:T(1,128)S(1)}, u32[]{:S(2)}, u32[]{:S(2)}) async-start(s32[128,1,4]{2,1,0:T(1,128)} %bitcast), calls=%async_computation | async-start | bytes 131072 | tf_op jit(solution)/shard_map/all_to_all | solution.py:194
  26.8 148.5 %all-to-all-start.1 = ((bf16[128,320,128]{2,1,0:T(8,128)(2,1)}), bf16[128,320,128]{2,1,0:T(8,128)(2,1)}, u32[]{:S(2)}, u32[]{:S(2)}) async-start(bf16[128,320,128]{2,1,0:T(8,128)(2,1)} %bitcast.17), calls=%async_computation.1 | async-start | bytes 20971520 | tf_op jit(solution)/shard_map/all_to_all | solution.py:193
  175.3 27.2 %copy-start.1 = (s32[32]{0:T(128)S(1)}, s32[32]{0:T(128)}, u32[]{:S(2)}) copy-start(s32[32]{0:T(128)} %param.8) | copy-start | bytes 388

commit v14 on v13

--- a/solution.py
+++ b/solution.py
@@ -187,15 +187,14 @@
 
     outbox = pack_outbox(blocks, source, levels, tile_count, capacity, plane_count)
     outbox = outbox.reshape(device_count, pairs * fields * sliver, 2 * BPHI)
-    code_out = jnp.broadcast_to(
-        code.reshape(tile_count, 1, capacity), (tile_count, plane_count, capacity)
-    ).reshape(device_count, capacity)
     arrived = lax.all_to_all(outbox, ("tile", "phi"), split_axis=0, concat_axis=0, tiled=True)
-    arrived_code = lax.all_to_all(code_out, ("tile", "phi"), split_axis=0, concat_axis=0, tiled=True)
-
-    by_segment = jnp.transpose(
-        arrived_code.reshape(tile_count, plane_count, capacity), (1, 0, 2)
-    ).reshape(plane_count, tile_count * capacity)
+    code_tile = lax.all_to_all(
+        code.reshape(tile_count, capacity), "tile", split_axis=0, concat_axis=0, tiled=True
+    )
+    code_rep = jnp.broadcast_to(code_tile[None], (plane_count, tile_count, capacity))
+    code_all = lax.all_to_all(code_rep, "phi", split_axis=0, concat_axis=0, tiled=True)
+
+    by_segment = code_all.reshape(plane_count, tile_count * capacity)
     want = jnp.arange(slot_count, dtype=jnp.int32)
     hit = by_segment[:, None, :] == want[None, :, None]
     pick = jnp.argmax(hit, axis=2).astype(jnp.int32)

time: 203 us -> 209 us (1.030)
  blocking collectives: 0 us -> 13 us
  starting transfers between devices: 21.2 us -> 13.3 us
    all_to_all x0 -> x1, blocking collectives: none -> 13 us  [local(): lax.all_to_all(code.reshape(tile_count, capacity), 'tile', split_axis=0,...]
    all_to_all x1, starting transfers between devices: 11 us -> 7.05 us  [local(): lax.all_to_all(outbox, ('tile', 'phi'), split_axis=0, concat_axis=0, tile...]
    all_to_all x1, starting transfers between devices: 10.2 us -> 6.25 us  [local(): lax.all_to_all(code_rep, 'phi', split_axis=0, concat_axis=0, tiled=True)]
  transfers between devices with their start and end apart: 2 -> 2, of which waited for: 1 -> 1; matrix products, arithmetic and copies ran while one was open for 11% -> 11% of each run, Pallas kernels for 5% -> 6%
where the time goes in v14:
time: 209 us; the launch traced here: 208 us
  waiting for transfers between devices  114 us (55%)
  Pallas kernels  38.7 us (19%)
  other arithmetic  25.1 us (12%)
  starting transfers between devices  13.3 us (6%)
  blocking collectives  13 us (6%)
  local copies, waits for them, and re-layouts  3.28 us (2%)
    all_to_all x1, waiting for transfers between devices, local(): lax.all_to_all(outbox, ('tile', 'phi'), split_axis=0, concat_axis=0, tile...  114 us
    pallas_call x1, Pallas kernels, spectra_from(): pl.pallas_call(functools.partial(spectra_kernel, groups, per_plane), out_...  27.1 us
    all_to_all x1, blocking collectives, local(): lax.all_to_all(code.reshape(tile_count, capacity), 'tile', split_axis=0,...  13 us
    pallas_call x1, Pallas kernels, pack_outbox(): pl.pallas_call(pack_kernel, out_shape=jax.ShapeDtypeStruct((tile_count, p...  11.6 us
    convert_element_type x1, other arithmetic, dft_basis(): return values.reshape(length, length).astype(jnp.bfloat16)  10.9 us
    all_to_all x1, starting transfers between devices, local(): lax.all_to_all(outbox, ('tile', 'phi'), split_axis=0, concat_axis=0, tile...  7.05 us
    sub x1, other arithmetic, dft_basis(): values = jnp.where(is_cos, ch * cl - sh * sl, sh * cl + ch * sl)  7.04 us
    all_to_all x1, starting transfers between devices, local(): lax.all_to_all(code_rep, 'phi', split_axis=0, concat_axis=0, tiled=True)  6.25 us
  transfers between devices with their start and end apart: 2, of which 1 were waited for; matrix products, arithmetic and copies ran while one was open for 11% of the time, Pallas kernels for 6%

profile of v14, /device:TPU:97, one launch (start us, length us, event | category | flops | bytes accessed | tf_op | source)
XLA Modules:
  0.0 207.9 jit_solution(16774652828435613988)
XLA Ops:
  0.0 0.0 copy-start
  0.0 0.7 fusion.16
  0.7 0.1 reduce_window_sum.11
  0.8 0.8 select_reduce_fusion
  1.6 0.7 multiply_add_fusion.1
  2.3 0.6 iota_reduce_fusion.1
  2.9 0.0 copy-start.2
  2.9 0.1 fusion.15
  3.0 0.0 copy-done
  3.0 0.8 gather_fusion
  3.8 1.4 gather_fusion.1
  5.2 0.1 select_n.87
  5.3 13.0 %all_to_all.16 = s32[16,1,4]{2,1,0:T(1,128)S(1)} all-to-all(s32[16,1,4]{2,1,0:T(1,128)S(1)} %bitcast.16), channel_id=1, replica_groups=mesh['tile'=16,'phi'=8] {'tile'}, dimensions={0} | all-to-all | bytes 512 | tf_op jit(solution)/shard_map/all_to_all | solution.py:191
  18.3 0.1 copy.16
  18.4 0.6 broadcast_in_dim.18
  19.0 6.3 %all-to-all-start.1 = ((s32[8,16,4]{1,2,0:T(4,128)}), s32[8,16,4]{1,2,0:T(4,128)S(1)}, u32[]{:S(2)}, u32[]{:S(2)}) async-start(s32[8,16,4]{1,2,0:T(4,128)} %broadcast_in_dim.18), calls=%async_computation.1 | async-start | bytes 32768 | tf_op jit(solution)/shard_map/all_to_all | solution.py:195
  25.2 0.0 copy-done.2
  25.2 11.6 %shard_map.55 = bf16[16,8,2,5,32,128]{5,4,3,2,1,0:T(8,128)(2,1)} custom-call(s32[64]{0:T(128)} %copy-done.2, s32[32]{0:T(128)} %level_ref.1, bf16[32,5,64,256]{3,2,1,0:T(8,128)(2,1)} %refs_15_.1, bf16[32,5,64,256]{3,2,1,0:T(8,128)(2,1)} %refs_15_.1, bf16[32,5,64,256]{3,2,1,0:T(8,128)(2,1)} %refs_15_.1, bf16[32,5,64,256]{3,2,1,0:T(8,128)(2,1)} %refs_15_.1, ...), custom_call_target="tpu_custom_call" | custom-call | tf_op jit(solution)/shard_map/pallas_call | solution.py:75
  36.8 0.0 all-to-all-done.1
  36.8 7.1 %all-to-all-start.2 = ((bf16[128,320,128]{2,1,0:T(8,128)(2,1)}), bf16[128,320,128]{2,1,0:T(8,128)(2,1)}, u32[]{:S(2)}, u32[]{:S(2)}) async-start(bf16[128,320,128]{2,1,0:T(8,128)(2,1)} %bitcast.14), calls=%async_computation.2 | async-start | bytes 20971520 | tf_op jit(solution)/shard_map/all_to_all | solution.py:190
  43.9 1.1 fusion.14
  45.0 2.0 fusion.12
  47.1 7.0 %multiply_subtract_fusion = (f32[32,64,2048]{2,1,0:T(8,128)S(1)}, f32[32,64,2048]{2,1,0:T(8,128)}) fusion(f32[64,2048]{1,0:T(8,128)S(1)} %get-tuple-element.14, f32[32,2048]{1,0:T(8,128)S(1)} %get-tuple-element.12, f32[64,2048]{1,0:T(8,128)S(1)} %get-tuple-element.13, f32[32,2048]{1,0:T(8,128)S(1)} %get-tuple-element.11), kind=kLoop, calls=%fused_computation.6 | loop fusion | flops 25165824 | bytes 35127296 | tf_op jit(solution)/shard_map/sub | solution.py:30
  54.1 10.9 %fusion.1.refs_32_ = bf16[2048,2048]{1,0:T(8,128)(2,1)} fusion(f32[32,64,2048]{2,1,0:T(8,128)} %get-tuple-element.10, f32[32,64,2048]{2,1,0:T(8,128)S(1)} %get-tuple-element.9, pred[2048]{0:T(1024)(128)(4,1)S(1)} %iota_compare_fusion.3), kind=kLoop, calls=%fused_computation.4 | loop fusion | flops 12582912 | bytes 41945088 | tf_op jit(solution)/shard_map/convert_element_type | solution.py:32
  65.1 0.1 copy.17
  65.2 0.1 copy.18
  65.2 1.0 iota_reduce_fusion
  66.2 0.1 reshape.205.row_ref
  66.3 0.1 reshape.206.half_ref
  66.4 114.4 %all-to-all-done.2 = bf16[128,320,128]{2,1,0:T(8,128)(2,1)} async-done(((bf16[128,320,128]{2,1,0:T(8,128)(2,1)}), bf16[128,320,128]{2,1,0:T(8,128)(2,1)}, u32[]{:S(2)}, u32[]{:S(2)}) %all-to-all-start.2) | async-done | bytes 10485792 | tf_op jit(solution)/shard_map/all_to_all | solution.py:190
  180.7 27.1 %shard_map.56 = f32[1280,2048]{1,0:T(8,128)} custom-call(s32[256]{0:T(256)S(1)} %reshape.205.row_ref, s32[256]{0:T(256)S(1)} %reshape.206.half_ref, ...), custom_call_target="tpu_custom_call" | custom-call | tf_op jit(solution)/shard_map/pallas_call | solution.py:147
  207.9 0.0 copy-done.1
  (8 shorter events, 0.1 us)
Async XLA Ops:
  0.0 3.0 %copy-start = (s32[32]{0:T(128)S(1)}, s32[32]{0:T(128)}, u32[]{:S(2)}) copy-start(s32[32]{0:T(128)} %param.8) | copy-start | bytes 388
  2.9 22.3 %copy-start.2 = (s32[64]{0:T(128)}, s32[64]{0:T(128)S(1)}, u32[]{:S(2)}) copy-start(s32[64]{0:T(128)S(1)} %get-tuple-element.7.source_ref) | copy-start | bytes 772
  19.0 17.9 %all-to-all-start.1 = ((s32[8,16,4]{1,2,0:T(4,128)}), s32[8,16,4]{1,2,0:T(4,128)S(1)}, u32[]{:S(2)}, u32[]{:S(2)}) async-start(s32[8,16,4]{1,2,0:T(4,128)} %broadcast_in_dim.18), calls=%async_computation.1 | async-start | bytes 32768 | tf_op jit(solution)/shard_map/all_to_all | solution.py:195
  36.8 143.9 %all-to-all-start.2 = ((bf16[128,320,128]{2,1,0:T(8,128)(2,1)}), bf16[128,320,128]{2,1,0:T(8,128)(2,1)}, u32[]{:S(2)}, u32[]{:S(2)}) async-start(bf16[128,320,128]{2,1,0:T(8,128)(2,1)} %bitcast.14), calls=%async_computation.2 | async-start | bytes 20971520 | tf_op jit(solution)/shard_map/all_to_all | solution.py:190
  180.7 27.1 %copy-start.1 = (s32[32]{0:T(128)S(1)}, s32[32]{0:T(128)}, u32[]{:S(2)}) copy-start(s32[32]{0:T(128)} %param.8) | copy-start | bytes 388

commit v15 on v13

--- a/solution.py
+++ b/solution.py
@@ -171,17 +171,15 @@
     capacity = 2 * slot_count // tile_count
     sliver = COLS // plane_count
 
-    onehot_dest = (block_dest[:, None] == jnp.arange(tile_count, dtype=jnp.int32)[None, :]).astype(
-        jnp.int32
-    )
-    slot_rank = jnp.sum((jnp.cumsum(onehot_dest, axis=0) - 1) * onehot_dest, axis=1)
+    block_ids = jnp.arange(slot_count, dtype=jnp.int32)
+    earlier = (block_dest[None, :] == block_dest[:, None]) & (block_ids[None, :] < block_ids[:, None])
+    slot_rank = jnp.sum(earlier.astype(jnp.int32), axis=1)
     send_slot = block_dest * capacity + slot_rank
     slot_ids = jnp.arange(tile_count * capacity, dtype=jnp.int32)
-    match = send_slot[None, :] == slot_ids[:, None]
-    filled = jnp.any(match, axis=1)
-    source = jnp.argmax(match, axis=1).astype(jnp.int32)
-    place = block_phi[source] * CG_DEV + block_group[source]
-    code = jnp.where(filled, place, -1)
+    match = (send_slot[None, :] == slot_ids[:, None]).astype(jnp.int32)
+    source = jnp.sum(match * block_ids[None, :], axis=1)
+    place = block_phi * CG_DEV + block_group
+    code = jnp.sum(match * (place[None, :] + 1), axis=1) - 1
     device_count = tile_count * plane_count
     pairs = capacity // 2
 
@@ -197,8 +195,9 @@
         arrived_code.reshape(tile_count, plane_count, capacity), (1, 0, 2)
     ).reshape(plane_count, tile_count * capacity)
     want = jnp.arange(slot_count, dtype=jnp.int32)
-    hit = by_segment[:, None, :] == want[None, :, None]
-    pick = jnp.argmax(hit, axis=2).astype(jnp.int32)
+    hit = (by_segment[:, None, :] == want[None, :, None]).astype(jnp.int32)
+    arrival = jnp.arange(tile_count * capacity, dtype=jnp.int32)
+    pick = jnp.sum(hit * arrival[None, None, :], axis=2)
     origin = pick // capacity
     segment = jnp.arange(plane_count, dtype=jnp.int32)[:, None]
     row = ((origin * plane_count + segment) * pairs + (pick % capacity) // 2).reshape(-1)

time: 203 us -> 200 us (0.985)
  local copies, waits for them, and re-layouts: 3.32 us -> 1.1 us
    gather x2 -> x0, local copies, waits for them, and re-layouts: 2.21 us -> none  [local(): place = block_phi[source] * CG_DEV + block_group[source]]
where the time goes in v15:
time: 200 us; the launch traced here: 199 us
  waiting for transfers between devices  115 us (58%)
  Pallas kernels  37.9 us (19%)
  other arithmetic  23.6 us (12%)
  starting transfers between devices  21.1 us (11%)
    all_to_all x1, waiting for transfers between devices, local(): lax.all_to_all(outbox, ('tile', 'phi'), split_axis=0, concat_axis=0, tile...  115 us
    pallas_call x1, Pallas kernels, spectra_from(): pl.pallas_call(functools.partial(spectra_kernel, groups, per_plane), out_...  27.4 us
    convert_element_type x1, other arithmetic, dft_basis(): return values.reshape(length, length).astype(jnp.bfloat16)  10.9 us
    all_to_all x1, starting transfers between devices, local(): lax.all_to_all(outbox, ('tile', 'phi'), split_axis=0, concat_axis=0, tile...  10.9 us
    pallas_call x1, Pallas kernels, pack_outbox(): pl.pallas_call(pack_kernel, out_shape=jax.ShapeDtypeStruct((tile_count, p...  10.5 us
    all_to_all x1, starting transfers between devices, local(): lax.all_to_all(code_out, ('tile', 'phi'), split_axis=0, concat_axis=0, ti...  10.2 us
    sub x1, other arithmetic, dft_basis(): values = jnp.where(is_cos, ch * cl - sh * sl, sh * cl + ch * sl)  7.03 us
  transfers between devices with their start and end apart: 2, of which 1 were waited for; matrix products, arithmetic and copies ran while one was open for 11% of the time, Pallas kernels for 5%

profile of v15, /device:TPU:97, one launch (start us, length us, event | category | flops | bytes accessed | tf_op | source)
XLA Modules:
  0.0 198.8 jit_solution(15166390862057674516)
XLA Ops:
  0.0 0.9 convert_reduce_fusion
  0.9 0.7 add_add_fusion
  1.6 0.6 select_reduce_fusion.1
  2.2 0.1 sub.27
  2.3 0.6 broadcast_in_dim.7.clone
  3.0 10.2 %all-to-all-start = ((s32[128,1,4]{2,1,0:T(1,128)}), s32[128,1,4]{2,1,0:T(1,128)S(1)}, u32[]{:S(2)}, u32[]{:S(2)}) async-start(s32[128,1,4]{2,1,0:T(1,128)} %bitcast), calls=%async_computation | async-start | bytes 131072 | tf_op jit(solution)/shard_map/all_to_all | solution.py:192
  13.1 10.5 %shard_map.55 = bf16[16,8,2,5,32,128]{5,4,3,2,1,0:T(8,128)(2,1)} custom-call(s32[64]{0:T(128)} %get-tuple-element.5.source_ref, s32[32]{0:T(128)} %level_ref.1, bf16[32,5,64,256]{3,2,1,0:T(8,128)(2,1)} %refs_15_.1, bf16[32,5,64,256]{3,2,1,0:T(8,128)(2,1)} %refs_15_.1, bf16[32,5,64,256]{3,2,1,0:T(8,128)(2,1)} %refs_15_.1, bf16[32,5,64,256]{3,2,1,0:T(8,128)(2,1)} %refs_15_.1, ...), custom_call_target="tpu_custom_call" | custom-call | tf_op jit(solution)/shard_map/pallas_call | solution.py:75
  23.7 0.0 all-to-all-done
  23.7 10.9 %all-to-all-start.1 = ((bf16[128,320,128]{2,1,0:T(8,128)(2,1)}), bf16[128,320,128]{2,1,0:T(8,128)(2,1)}, u32[]{:S(2)}, u32[]{:S(2)}) async-start(bf16[128,320,128]{2,1,0:T(8,128)(2,1)} %bitcast.17), calls=%async_computation.1 | async-start | bytes 20971520 | tf_op jit(solution)/shard_map/all_to_all | solution.py:191
  34.6 0.1 add.93
  34.7 1.1 fusion.14
  35.8 2.0 %fusion.12 = (f32[64,2048]{1,0:T(8,128)S(1)}, f32[64,2048]{1,0:T(8,128)S(1)}) fusion(s32[2048]{0:T(1024)S(1)} %add_select_fusion.2), kind=kLoop, calls=%fused_computation.23 | loop fusion | flops 1835008 | bytes 1056768 | tf_op jit(solution)/shard_map/cos | solution.py:28
  37.8 7.0 %multiply_subtract_fusion = (f32[32,64,2048]{2,1,0:T(8,128)S(1)}, f32[32,64,2048]{2,1,0:T(8,128)}) fusion(f32[64,2048]{1,0:T(8,128)S(1)} %get-tuple-element.12, f32[32,2048]{1,0:T(8,128)S(1)} %get-tuple-element.10, f32[64,2048]{1,0:T(8,128)S(1)} %get-tuple-element.11, f32[32,2048]{1,0:T(8,128)S(1)} %get-tuple-element.9), kind=kLoop, calls=%fused_computation.4 | loop fusion | flops 25165824 | bytes 35127296 | tf_op jit(solution)/shard_map/sub | solution.py:30
  44.9 10.9 %fusion.1.refs_32_ = bf16[2048,2048]{1,0:T(8,128)(2,1)} fusion(f32[32,64,2048]{2,1,0:T(8,128)} %get-tuple-element.8, f32[32,64,2048]{2,1,0:T(8,128)S(1)} %get-tuple-element.7, pred[2048]{0:T(1024)(128)(4,1)S(1)} %iota_compare_fusion.3), kind=kLoop, calls=%fused_computation.2 | loop fusion | flops 12582912 | bytes 41945088 | tf_op jit(solution)/shard_map/convert_element_type | solution.py:32
  55.8 0.2 copy.21
  56.0 0.1 copy.22
  56.1 0.2 select_reduce_fusion
  56.3 0.1 reduce_sum.41
  56.4 115.0 %all-to-all-done.1 = bf16[128,320,128]{2,1,0:T(8,128)(2,1)} async-done(((bf16[128,320,128]{2,1,0:T(8,128)(2,1)}), bf16[128,320,128]{2,1,0:T(8,128)(2,1)}, u32[]{:S(2)}, u32[]{:S(2)}) %all-to-all-start.1) | async-done | bytes 10485792 | tf_op jit(solution)/shard_map/all_to_all | solution.py:191
  171.4 27.4 %shard_map.56 = f32[1280,2048]{1,0:T(8,128)} custom-call(s32[256]{0:T(256)S(1)} %get-tuple-element.14.row_ref, s32[256]{0:T(256)S(1)} %get-tuple-element.13.half_ref, ...), custom_call_target="tpu_custom_call" | custom-call | tf_op jit(solution)/shard_map/pallas_call | solution.py:147
  (6 shorter events, 0.0 us)
Async XLA Ops:
  3.0 20.7 %all-to-all-start = ((s32[128,1,4]{2,1,0:T(1,128)}), s32[128,1,4]{2,1,0:T(1,128)S(1)}, u32[]{:S(2)}, u32[]{:S(2)}) async-start(s32[128,1,4]{2,1,0:T(1,128)} %bitcast), calls=%async_computation | async-start | bytes 131072 | tf_op jit(solution)/shard_map/all_to_all | solution.py:192
  23.7 147.7 %all-to-all-start.1 = ((bf16[128,320,128]{2,1,0:T(8,128)(2,1)}), bf16[128,320,128]{2,1,0:T(8,128)(2,1)}, u32[]{:S(2)}, u32[]{:S(2)}) async-start(bf16[128,320,128]{2,1,0:T(8,128)(2,1)} %bitcast.17), calls=%async_computation.1 | async-start | bytes 20971520 | tf_op jit(solution)/shard_map/all_to_all | solution.py:191

commit v16 on v15

--- a/solution.py
+++ b/solution.py
@@ -13,6 +13,7 @@
 BPHI = 64
 COLS = 256
 CG_DEV = 8
+CODE_ROWS = 16
 
 
 def dft_basis(length):
@@ -39,11 +40,21 @@
     return value.astype(jnp.float32).astype(dtype)
 
 
-def pack_kernel(source_ref, level_ref, *refs):
+def pack_kernel(pairs, fields, sliver, source_ref, level_ref, code_ref, *refs):
     out_ref = refs[-1]
-    per_step, planes, pairs, fields, sliver = out_ref.shape[:5]
+    per_step, planes, _, lanes = out_ref.shape
     step = pl.program_id(0)
+    slots = 2 * pairs
+    code_rows = out_ref.shape[2] - pairs * fields * sliver
+    lane = lax.broadcasted_iota(jnp.int32, (code_rows, lanes), 1)
     for local_tile in range(per_step):
+        first_slot = (step * per_step + local_tile) * slots
+        codes = jnp.zeros((code_rows, lanes), jnp.float32)
+        for slot in range(slots):
+            codes = jnp.where(lane == slot, code_ref[first_slot + slot].astype(jnp.float32), codes)
+        out_ref[local_tile, :, pl.ds(pairs * fields * sliver, code_rows), :] = jnp.broadcast_to(
+            codes.astype(out_ref.dtype)[None], (planes, code_rows, lanes)
+        )
         for pair in range(pairs):
             slot = (local_tile * pairs + pair) * 2
             first = step * (len(refs) - 1) + slot
@@ -58,10 +69,11 @@
                     axis=0,
                 )
                 flipped = both.T.reshape(planes, sliver, both.shape[0])
-                out_ref[local_tile, :, pair, field] = flipped.astype(out_ref.dtype)
-
-
-def pack_outbox(blocks, source, levels, tile_count, capacity, plane_count):
+                row = (pair * fields + field) * sliver
+                out_ref[local_tile, :, pl.ds(row, sliver), :] = flipped.astype(out_ref.dtype)
+
+
+def pack_outbox(blocks, source, levels, code, tile_count, capacity, plane_count):
     slot_count, fields, bphi, cols = blocks.shape
     pairs = capacity // 2
     sliver = cols // plane_count
@@ -70,23 +82,23 @@
     per_call = per_step * capacity
 
     def block_map(slot):
-        return lambda t, src_ref, level_ref: (src_ref[t * per_call + slot], 0, 0, 0)
+        return lambda t, src_ref, level_ref, code_ref: (src_ref[t * per_call + slot], 0, 0, 0)
 
     return pl.pallas_call(
-        pack_kernel,
+        functools.partial(pack_kernel, pairs, fields, sliver),
         out_shape=jax.ShapeDtypeStruct(
-            (tile_count, plane_count, pairs, fields, sliver, 2 * bphi), blocks.dtype
+            (tile_count, plane_count, pairs * fields * sliver + CODE_ROWS, 2 * bphi), blocks.dtype
         ),
         grid_spec=pltpu.PrefetchScalarGridSpec(
-            num_scalar_prefetch=2,
+            num_scalar_prefetch=3,
             grid=(tile_count // per_step,),
             in_specs=[pl.BlockSpec((1, fields, bphi, cols), block_map(slot)) for slot in range(per_call)],
             out_specs=pl.BlockSpec(
-                (per_step, plane_count, pairs, fields, sliver, 2 * bphi),
-                lambda t, src_ref, level_ref: (t, 0, 0, 0, 0, 0),
+                (per_step, plane_count, pairs * fields * sliver + CODE_ROWS, 2 * bphi),
+                lambda t, src_ref, level_ref, code_ref: (t, 0, 0, 0),
             ),
         ),
-    )(source, levels, *([blocks] * per_call))
+    )(source, levels, code, *([blocks] * per_call))
 
 
 def spectra_kernel(groups, per_plane, row_ref, half_ref, *refs):
@@ -98,7 +110,7 @@
     @pl.when(step < segments)
     def _():
         lanes = pieces[0].shape[-1]
-        shape = pieces[0].shape[1:]
+        shape = lhs_ref.shape[:1] + lhs_ref.shape[2:3] + pieces[0].shape[-1:]
         lane = lax.broadcasted_iota(jnp.int32, shape, 2)
         for group in range(groups):
             for quad in range(per_plane // 2):
@@ -106,7 +118,7 @@
                 for side in range(2):
                     position = quad * 2 + side
                     index = (step * per_plane + position) * groups + group
-                    piece = pieces[position * groups + group][0]
+                    piece = pieces[position * groups + group][0].reshape(shape)
                     turned = pltpu.roll(piece, lanes // 2, 2)
                     keep = half_ref[index] == side
                     parts.append(jnp.where(keep, piece, turned))
@@ -120,8 +132,8 @@
         out_ref[...] = jnp.dot(lhs, basis_ref[...], preferred_element_type=jnp.float32)
 
 
-def spectra_from(landed, row, half, basis, plane_count, per_plane, groups):
-    _, fields, sliver, lanes = landed.shape
+def spectra_from(landed, row, half, basis, plane_count, per_plane, groups, fields, sliver):
+    lanes = landed.shape[-1]
     depth = per_plane * lanes // 2
     length = basis.shape[1]
     width = 512
@@ -130,7 +142,8 @@
     def piece_map(position, group):
         def index_map(s, row_ref, half_ref):
             segment = jnp.minimum(s, plane_count - 1)
-            return (row_ref[(segment * per_plane + position) * groups + group], 0, 0, 0)
+            piece = row_ref[(segment * per_plane + position) * groups + group]
+            return (piece // 2, piece % 2, 0)
 
         return index_map
 
@@ -138,7 +151,7 @@
         return (0, jnp.maximum(s - plane_count, 0))
 
     in_specs = [
-        pl.BlockSpec((1, fields, sliver, lanes), piece_map(position, group))
+        pl.BlockSpec((1, fields * sliver, lanes), piece_map(position, group))
         for position in range(per_plane)
         for group in range(groups)
     ]
@@ -183,13 +196,10 @@
     device_count = tile_count * plane_count
     pairs = capacity // 2
 
-    outbox = pack_outbox(blocks, source, levels, tile_count, capacity, plane_count)
-    outbox = outbox.reshape(device_count, pairs * fields * sliver, 2 * BPHI)
-    code_out = jnp.broadcast_to(
-        code.reshape(tile_count, 1, capacity), (tile_count, plane_count, capacity)
-    ).reshape(device_count, capacity)
+    outbox = pack_outbox(blocks, source, levels, code, tile_count, capacity, plane_count)
+    outbox = outbox.reshape(device_count, pairs * fields * sliver + CODE_ROWS, 2 * BPHI)
     arrived = lax.all_to_all(outbox, ("tile", "phi"), split_axis=0, concat_axis=0, tiled=True)
-    arrived_code = lax.all_to_all(code_out, ("tile", "phi"), split_axis=0, concat_axis=0, tiled=True)
+    arrived_code = arrived[:, pairs * fields * sliver, :capacity].astype(jnp.int32)
 
     by_segment = jnp.transpose(
         arrived_code.reshape(tile_count, plane_count, capacity), (1, 0, 2)
@@ -202,9 +212,10 @@
     segment = jnp.arange(plane_count, dtype=jnp.int32)[:, None]
     row = ((origin * plane_count + segment) * pairs + (pick % capacity) // 2).reshape(-1)
     half = (pick % 2).reshape(-1)
-    landed = arrived.reshape(device_count * pairs, fields, sliver, 2 * BPHI)
     basis = dft_basis(NPHI)
-    spectra = spectra_from(landed, row, half, basis, plane_count, per_plane, CG_DEV)
+    spectra = spectra_from(
+        arrived, row, half, basis, plane_count, per_plane, CG_DEV, fields, sliver
+    )
     return spectra.reshape(fields, CG_DEV, sliver, NPHI)
 
 

time: 200 us -> 207 us (1.035)
  starting transfers between devices: 21.1 us -> 10.7 us
  waiting for transfers between devices: 115 us -> 124 us
  Pallas kernels: 37.9 us -> 46 us
    all_to_all x1 -> x0, starting transfers between devices: 10.2 us -> none  [local(): lax.all_to_all(code_out, ('tile', 'phi'), split_axis=0, concat_axis=0, ti...]
    all_to_all x1, waiting for transfers between devices: 115 us -> 124 us  [local(): lax.all_to_all(outbox, ('tile', 'phi'), split_axis=0, concat_axis=0, tile...]
    pallas_call x1, Pallas kernels: 27.4 us -> 35 us  [spectra_from(): pl.pallas_call(functools.partial(spectra_kernel, groups, per_plane), out_...]
  transfers between devices with their start and end apart: 2 -> 1, of which waited for: 1 -> 1; matrix products, arithmetic and copies ran while one was open for 11% -> 10% of each run, Pallas kernels for 5% -> 0%
where the time goes in v16:
time: 207 us; the launch traced here: 206 us
  waiting for transfers between devices  124 us (60%)
  Pallas kernels  46 us (22%)
  other arithmetic  25.2 us (12%)
  starting transfers between devices  10.7 us (5%)
    all_to_all x1, waiting for transfers between devices, local(): lax.all_to_all(outbox, ('tile', 'phi'), split_axis=0, concat_axis=0, tile...  124 us
    pallas_call x1, Pallas kernels, spectra_from(): pl.pallas_call(functools.partial(spectra_kernel, groups, per_plane), out_...  35 us
    pallas_call x1, Pallas kernels, pack_outbox(): pl.pallas_call(functools.partial(pack_kernel, pairs, fields, sliver), out...  11 us
    convert_element_type x1, other arithmetic, dft_basis(): return values.reshape(length, length).astype(jnp.bfloat16)  10.9 us
    all_to_all x1, starting transfers between devices, local(): lax.all_to_all(outbox, ('tile', 'phi'), split_axis=0, concat_axis=0, tile...  10.7 us
    sub x1, other arithmetic, dft_basis(): values = jnp.where(is_cos, ch * cl - sh * sl, sh * cl + ch * sl)  7.03 us
  transfers between devices with their start and end apart: 1, of which 1 were waited for; matrix products, arithmetic and copies ran while one was open for 10% of the time, Pallas kernels for 0%

profile of v16, /device:TPU:97, one launch (start us, length us, event | category | flops | bytes accessed | tf_op | source)
XLA Modules:
  0.0 205.8 jit_solution(17305113330217716321)
XLA Ops:
  0.0 0.9 convert_reduce_fusion
  0.9 0.7 add_add_fusion
  1.6 0.6 select_reduce_fusion.1
  2.2 0.6 broadcast_add_fusion.code_ref
  2.8 11.0 %shard_map.55 = bf16[16,8,336,128]{3,2,1,0:T(8,128)(2,1)} custom-call(s32[64]{0:T(128)} %get-tuple-element.6.source_ref, s32[32]{0:T(128)} %level_ref.1, s32[64]{0:T(128)} %broadcast_add_fusion.code_ref, bf16[32,5,64,256]{3,2,1,0:T(8,128)(2,1)} %refs_15_.1, bf16[32,5,64,256]{3,2,1,0:T(8,128)(2,1)} %refs_15_.1, bf16[32,5,64,256]{3,2,1,0:T(8,128)(2,1)} %refs_15_.1, ...), custom_call_target="tpu_custom_call" | custom-call | tf_op jit(solution)/shard_map/pallas_call | solution.py:87
  13.8 10.7 %all-to-all-start = ((bf16[128,336,128]{2,1,0:T(8,128)(2,1)}), bf16[128,336,128]{2,1,0:T(8,128)(2,1)}, u32[]{:S(2)}, u32[]{:S(2)}) async-start(bf16[128,336,128]{2,1,0:T(8,128)(2,1)} %bitcast.14), calls=%async_computation | async-start | bytes 22020096 | tf_op jit(solution)/shard_map/all_to_all | solution.py:201
  24.6 0.1 add.88
  24.7 1.1 fusion.14
  25.8 2.0 fusion.12
  27.8 7.0 %multiply_subtract_fusion = (f32[32,64,2048]{2,1,0:T(8,128)S(1)}, f32[32,64,2048]{2,1,0:T(8,128)}) fusion(f32[64,2048]{1,0:T(8,128)S(1)} %get-tuple-element.12, f32[32,2048]{1,0:T(8,128)S(1)} %get-tuple-element.10, f32[64,2048]{1,0:T(8,128)S(1)} %get-tuple-element.11, f32[32,2048]{1,0:T(8,128)S(1)} %get-tuple-element.9), kind=kLoop, calls=%fused_computation.4 | loop fusion | flops 25165824 | bytes 35127296 | tf_op jit(solution)/shard_map/sub | solution.py:31
  34.8 10.9 %fusion.1.refs_32_ = bf16[2048,2048]{1,0:T(8,128)(2,1)} fusion(f32[32,64,2048]{2,1,0:T(8,128)} %get-tuple-element.8, f32[32,64,2048]{2,1,0:T(8,128)S(1)} %get-tuple-element.7, pred[2048]{0:T(1024)(128)(4,1)S(1)} %iota_compare_fusion.3), kind=kLoop, calls=%fused_computation.2 | loop fusion | flops 12582912 | bytes 41945088 | tf_op jit(solution)/shard_map/convert_element_type | solution.py:33
  45.8 123.5 %all-to-all-done.refs_0_.refs_1_.refs_2_.refs_3_.refs_4_.refs_5_.refs_6_.refs_7_.refs_8_.refs_9_.refs_10_.refs_11_.refs_12_.refs_13_.refs_14_.refs_15_.refs_16_.refs_17_.refs_18_.refs_19_.refs_20_.refs_21_.refs_22_.refs_23_.refs_24_.refs_25_.refs_26_.refs_27_.refs_28_.refs_29_.refs_30_.refs_31_ = bf16[128,336,128]{2,1,0:T(8,128)(2,1)} async-done(((bf16[128,336,128]{2,1,0:T(8,128)(2,1)}), ...) | async-done | bytes 11010080 | tf_op jit(solution)/shard_map/all_to_all | solution.py:201
  169.3 1.0 slice_convert_fusion
  170.3 0.2 copy.8
  170.5 0.1 copy.9
  170.5 0.2 select_reduce_fusion
  170.8 0.1 reduce_sum.42
  170.9 35.0 %shard_map.56 = f32[1280,2048]{1,0:T(8,128)} custom-call(s32[256]{0:T(256)S(1)} %get-tuple-element.14.row_ref, s32[256]{0:T(256)S(1)} %get-tuple-element.13.half_ref, ...), custom_call_target="tpu_custom_call" | custom-call | tf_op jit(solution)/shard_map/pallas_call | solution.py:160
  (5 shorter events, 0.0 us)
Async XLA Ops:
  13.8 155.5 %all-to-all-start = ((bf16[128,336,128]{2,1,0:T(8,128)(2,1)}), bf16[128,336,128]{2,1,0:T(8,128)(2,1)}, u32[]{:S(2)}, u32[]{:S(2)}) async-start(bf16[128,336,128]{2,1,0:T(8,128)(2,1)} %bitcast.14), calls=%async_computation | async-start | bytes 22020096 | tf_op jit(solution)/shard_map/all_to_all | solution.py:201

commit v17 on v15

--- a/solution.py
+++ b/solution.py
@@ -89,32 +89,36 @@
     )(source, levels, *([blocks] * per_call))
 
 
-def spectra_kernel(groups, per_plane, row_ref, half_ref, *refs):
-    pieces = refs[: per_plane * groups]
-    basis_ref, out_ref, lhs_ref = refs[per_plane * groups :]
+def spectra_kernel(groups, per_plane, per_step, row_ref, half_ref, *refs):
+    pieces = refs[: per_step * per_plane * groups]
+    basis_ref, out_ref, lhs_ref = refs[per_step * per_plane * groups :]
     step = pl.program_id(0)
     segments = lhs_ref.shape[-1] // (pieces[0].shape[-1] * per_plane // 2)
 
-    @pl.when(step < segments)
+    @pl.when(step < segments // per_step)
     def _():
         lanes = pieces[0].shape[-1]
         shape = pieces[0].shape[1:]
         lane = lax.broadcasted_iota(jnp.int32, shape, 2)
-        for group in range(groups):
-            for quad in range(per_plane // 2):
-                parts = []
-                for side in range(2):
-                    position = quad * 2 + side
-                    index = (step * per_plane + position) * groups + group
-                    piece = pieces[position * groups + group][0]
-                    turned = pltpu.roll(piece, lanes // 2, 2)
-                    keep = half_ref[index] == side
-                    parts.append(jnp.where(keep, piece, turned))
-                merged = jnp.where(lane < lanes // 2, parts[0], parts[1])
-                start = pl.multiple_of(step * (lanes * per_plane // 2) + quad * lanes, lanes)
-                lhs_ref[:, group, :, pl.ds(start, lanes)] = merged
-
-    @pl.when(step >= segments)
+        for local_segment in range(per_step):
+            segment = step * per_step + local_segment
+            for group in range(groups):
+                for quad in range(per_plane // 2):
+                    parts = []
+                    for side in range(2):
+                        position = quad * 2 + side
+                        index = (segment * per_plane + position) * groups + group
+                        piece = pieces[(local_segment * per_plane + position) * groups + group][0]
+                        turned = pltpu.roll(piece, lanes // 2, 2)
+                        keep = half_ref[index] == side
+                        parts.append(jnp.where(keep, piece, turned))
+                    merged = jnp.where(lane < lanes // 2, parts[0], parts[1])
+                    start = pl.multiple_of(
+                        segment * (lanes * per_plane // 2) + quad * lanes, lanes
+                    )
+                    lhs_ref[:, group, :, pl.ds(start, lanes)] = merged
+
+    @pl.when(step >= segments // per_step)
     def _():
         lhs = lhs_ref[...].reshape(out_ref.shape[0], lhs_ref.shape[-1])
         out_ref[...] = jnp.dot(lhs, basis_ref[...], preferred_element_type=jnp.float32)
@@ -126,30 +130,32 @@
     length = basis.shape[1]
     width = 512
     chunks = length // width
+    per_step = 2
+    steps = plane_count // per_step
 
     def piece_map(position, group):
         def index_map(s, row_ref, half_ref):
-            segment = jnp.minimum(s, plane_count - 1)
-            return (row_ref[(segment * per_plane + position) * groups + group], 0, 0, 0)
+            first = jnp.minimum(s, steps - 1) * per_step * per_plane
+            return (row_ref[(first + position) * groups + group], 0, 0, 0)
 
         return index_map
 
     def column_map(s, row_ref, half_ref):
-        return (0, jnp.maximum(s - plane_count, 0))
+        return (0, jnp.maximum(s - steps, 0))
 
     in_specs = [
         pl.BlockSpec((1, fields, sliver, lanes), piece_map(position, group))
-        for position in range(per_plane)
+        for position in range(per_step * per_plane)
         for group in range(groups)
     ]
     in_specs.append(pl.BlockSpec((basis.shape[0], width), column_map))
     rows = fields * groups * sliver
     return pl.pallas_call(
-        functools.partial(spectra_kernel, groups, per_plane),
+        functools.partial(spectra_kernel, groups, per_plane, per_step),
         out_shape=jax.ShapeDtypeStruct((rows, length), jnp.float32),
         grid_spec=pltpu.PrefetchScalarGridSpec(
             num_scalar_prefetch=2,
-            grid=(plane_count + chunks,),
+            grid=(steps + chunks,),
             in_specs=in_specs,
             out_specs=pl.BlockSpec((rows, width), column_map),
             scratch_shapes=[
@@ -159,7 +165,7 @@
         compiler_params=pltpu.CompilerParams(
             dimension_semantics=("arbitrary",), vmem_limit_bytes=48 * 1024 * 1024
         ),
-    )(row, half, *([landed] * (per_plane * groups)), basis)
+    )(row, half, *([landed] * (per_step * per_plane * groups)), basis)
 
 
 def local(blocks, levels, block_dest, block_phi, block_group):

time: 200 us -> 202 us (1.010)
  no operation moved by 1% of the time
where the time goes in v17:
time: 202 us
  waiting for transfers between devices  116 us (57%)
  Pallas kernels  39.6 us (20%)
  other arithmetic  23.6 us (12%)
  starting transfers between devices  21.8 us (11%)
    all_to_all x1, waiting for transfers between devices, local(): lax.all_to_all(outbox, ('tile', 'phi'), split_axis=0, concat_axis=0, tile...  116 us
    pallas_call x1, Pallas kernels, spectra_from(): pl.pallas_call(functools.partial(spectra_kernel, groups, per_plane, per_s...  29.1 us
    all_to_all x1, starting transfers between devices, local(): lax.all_to_all(outbox, ('tile', 'phi'), split_axis=0, concat_axis=0, tile...  11.6 us
    convert_element_type x1, other arithmetic, dft_basis(): return values.reshape(length, length).astype(jnp.bfloat16)  10.9 us
    pallas_call x1, Pallas kernels, pack_outbox(): pl.pallas_call(pack_kernel, out_shape=jax.ShapeDtypeStruct((tile_count, p...  10.4 us
    all_to_all x1, starting transfers between devices, local(): lax.all_to_all(code_out, ('tile', 'phi'), split_axis=0, concat_axis=0, ti...  10.2 us
    sub x1, other arithmetic, dft_basis(): values = jnp.where(is_cos, ch * cl - sh * sl, sh * cl + ch * sl)  7.03 us
  transfers between devices with their start and end apart: 2, of which 1 were waited for; matrix products, arithmetic and copies ran while one was open for 11% of the time, Pallas kernels for 5%

profile of v17, /device:TPU:97, one launch (start us, length us, event | category | flops | bytes accessed | tf_op | source)
XLA Modules:
  0.0 202.0 jit_solution(999949084125956934)
XLA Ops:
  0.0 0.9 convert_reduce_fusion
  0.9 0.7 add_add_fusion
  1.6 0.6 select_reduce_fusion.1
  2.2 0.1 sub.27
  2.3 0.6 broadcast_in_dim.7.clone
  3.0 10.2 %all-to-all-start = ((s32[128,1,4]{2,1,0:T(1,128)}), s32[128,1,4]{2,1,0:T(1,128)S(1)}, u32[]{:S(2)}, u32[]{:S(2)}) async-start(s32[128,1,4]{2,1,0:T(1,128)} %bitcast), calls=%async_computation | async-start | bytes 131072 | tf_op jit(solution)/shard_map/all_to_all | solution.py:198
  13.1 10.4 %shard_map.55 = bf16[16,8,2,5,32,128]{5,4,3,2,1,0:T(8,128)(2,1)} custom-call(s32[64]{0:T(128)} %get-tuple-element.5.source_ref, s32[32]{0:T(128)} %level_ref.1, bf16[32,5,64,256]{3,2,1,0:T(8,128)(2,1)} %refs_15_.1, bf16[32,5,64,256]{3,2,1,0:T(8,128)(2,1)} %refs_15_.1, bf16[32,5,64,256]{3,2,1,0:T(8,128)(2,1)} %refs_15_.1, bf16[32,5,64,256]{3,2,1,0:T(8,128)(2,1)} %refs_15_.1, ...), custom_call_target="tpu_custom_call" | custom-call | tf_op jit(solution)/shard_map/pallas_call | solution.py:75
  23.6 0.0 all-to-all-done
  23.6 11.6 %all-to-all-start.1 = ((bf16[128,320,128]{2,1,0:T(8,128)(2,1)}), bf16[128,320,128]{2,1,0:T(8,128)(2,1)}, u32[]{:S(2)}, u32[]{:S(2)}) async-start(bf16[128,320,128]{2,1,0:T(8,128)(2,1)} %bitcast.17), calls=%async_computation.1 | async-start | bytes 20971520 | tf_op jit(solution)/shard_map/all_to_all | solution.py:197
  35.2 0.1 add.93
  35.3 1.1 fusion.14
  36.4 2.0 %fusion.12 = (f32[64,2048]{1,0:T(8,128)S(1)}, f32[64,2048]{1,0:T(8,128)S(1)}) fusion(s32[2048]{0:T(1024)S(1)} %add_select_fusion.2), kind=kLoop, calls=%fused_computation.23 | loop fusion | flops 1835008 | bytes 1056768 | tf_op jit(solution)/shard_map/cos | solution.py:28
  38.5 7.0 %multiply_subtract_fusion = (f32[32,64,2048]{2,1,0:T(8,128)S(1)}, f32[32,64,2048]{2,1,0:T(8,128)}) fusion(f32[64,2048]{1,0:T(8,128)S(1)} %get-tuple-element.12, f32[32,2048]{1,0:T(8,128)S(1)} %get-tuple-element.10, f32[64,2048]{1,0:T(8,128)S(1)} %get-tuple-element.11, f32[32,2048]{1,0:T(8,128)S(1)} %get-tuple-element.9), kind=kLoop, calls=%fused_computation.4 | loop fusion | flops 25165824 | bytes 35127296 | tf_op jit(solution)/shard_map/sub | solution.py:30
  45.5 10.9 %fusion.1.refs_64_ = bf16[2048,2048]{1,0:T(8,128)(2,1)} fusion(f32[32,64,2048]{2,1,0:T(8,128)} %get-tuple-element.8, f32[32,64,2048]{2,1,0:T(8,128)S(1)} %get-tuple-element.7, pred[2048]{0:T(1024)(128)(4,1)S(1)} %iota_compare_fusion.3), kind=kLoop, calls=%fused_computation.2 | loop fusion | flops 12582912 | bytes 41945088 | tf_op jit(solution)/shard_map/convert_element_type | solution.py:32
  56.5 0.2 copy.21
  56.6 0.1 copy.22
  56.7 0.2 select_reduce_fusion
  56.9 0.1 reduce_sum.41
  57.0 115.7 %all-to-all-done.1 = bf16[128,320,128]{2,1,0:T(8,128)(2,1)} async-done(((bf16[128,320,128]{2,1,0:T(8,128)(2,1)}), bf16[128,320,128]{2,1,0:T(8,128)(2,1)}, u32[]{:S(2)}, u32[]{:S(2)}) %all-to-all-start.1) | async-done | bytes 10485792 | tf_op jit(solution)/shard_map/all_to_all | solution.py:197
  172.7 29.1 %shard_map.56 = f32[1280,2048]{1,0:T(8,128)} custom-call(s32[256]{0:T(256)S(1)} %get-tuple-element.14.row_ref, s32[256]{0:T(256)S(1)} %get-tuple-element.13.half_ref, ...), custom_call_target="tpu_custom_call" | custom-call | tf_op jit(solution)/shard_map/pallas_call | solution.py:153
  (6 shorter events, 0.0 us)
Async XLA Ops:
  3.0 20.6 %all-to-all-start = ((s32[128,1,4]{2,1,0:T(1,128)}), s32[128,1,4]{2,1,0:T(1,128)S(1)}, u32[]{:S(2)}, u32[]{:S(2)}) async-start(s32[128,1,4]{2,1,0:T(1,128)} %bitcast), calls=%async_computation | async-start | bytes 131072 | tf_op jit(solution)/shard_map/all_to_all | solution.py:198
  23.6 149.1 %all-to-all-start.1 = ((bf16[128,320,128]{2,1,0:T(8,128)(2,1)}), bf16[128,320,128]{2,1,0:T(8,128)(2,1)}, u32[]{:S(2)}, u32[]{:S(2)}) async-start(bf16[128,320,128]{2,1,0:T(8,128)(2,1)} %bitcast.17), calls=%async_computation.1 | async-start | bytes 20971520 | tf_op jit(solution)/shard_map/all_to_all | solution.py:197

commit v18 on v15

--- a/solution.py
+++ b/solution.py
@@ -66,7 +66,7 @@
     pairs = capacity // 2
     sliver = cols // plane_count
 
-    per_step = 4
+    per_step = 8
     per_call = per_step * capacity
 
     def block_map(slot):

time: 200 us -> 201 us (level)
  no operation moved by 1% of the time
where the time goes in v18:
time: 201 us; the launch traced here: 200 us
  waiting for transfers between devices  116 us (58%)
  Pallas kernels  38.3 us (19%)
  other arithmetic  23.6 us (12%)
  starting transfers between devices  21.1 us (10%)
    all_to_all x1, waiting for transfers between devices, local(): lax.all_to_all(outbox, ('tile', 'phi'), split_axis=0, concat_axis=0, tile...  116 us
    pallas_call x1, Pallas kernels, spectra_from(): pl.pallas_call(functools.partial(spectra_kernel, groups, per_plane), out_...  27.3 us
    all_to_all x1, starting transfers between devices, local(): lax.all_to_all(outbox, ('tile', 'phi'), split_axis=0, concat_axis=0, tile...  10.9 us
    convert_element_type x1, other arithmetic, dft_basis(): return values.reshape(length, length).astype(jnp.bfloat16)  10.9 us
    pallas_call x1, Pallas kernels, pack_outbox(): pl.pallas_call(pack_kernel, out_shape=jax.ShapeDtypeStruct((tile_count, p...  10.9 us
    all_to_all x1, starting transfers between devices, local(): lax.all_to_all(code_out, ('tile', 'phi'), split_axis=0, concat_axis=0, ti...  10.2 us
    sub x1, other arithmetic, dft_basis(): values = jnp.where(is_cos, ch * cl - sh * sl, sh * cl + ch * sl)  7.03 us
  transfers between devices with their start and end apart: 2, of which 1 were waited for; matrix products, arithmetic and copies ran while one was open for 11% of the time, Pallas kernels for 5%

profile of v18, /device:TPU:97, one launch (start us, length us, event | category | flops | bytes accessed | tf_op | source)
XLA Modules:
  0.0 200.0 jit_solution(8916488430083071751)
XLA Ops:
  0.0 0.9 convert_reduce_fusion
  0.9 0.7 add_add_fusion
  1.6 0.6 select_reduce_fusion.1
  2.2 0.1 sub.27
  2.3 0.6 broadcast_in_dim.7.clone
  3.0 10.2 %all-to-all-start = ((s32[128,1,4]{2,1,0:T(1,128)}), s32[128,1,4]{2,1,0:T(1,128)S(1)}, u32[]{:S(2)}, u32[]{:S(2)}) async-start(s32[128,1,4]{2,1,0:T(1,128)} %bitcast), calls=%async_computation | async-start | bytes 131072 | tf_op jit(solution)/shard_map/all_to_all | solution.py:192
  13.1 10.9 %shard_map.55 = bf16[16,8,2,5,32,128]{5,4,3,2,1,0:T(8,128)(2,1)} custom-call(s32[64]{0:T(128)} %get-tuple-element.5.source_ref, s32[32]{0:T(128)} %level_ref.1, bf16[32,5,64,256]{3,2,1,0:T(8,128)(2,1)} %refs_31_.1, bf16[32,5,64,256]{3,2,1,0:T(8,128)(2,1)} %refs_31_.1, bf16[32,5,64,256]{3,2,1,0:T(8,128)(2,1)} %refs_31_.1, bf16[32,5,64,256]{3,2,1,0:T(8,128)(2,1)} %refs_31_.1, ...), custom_call_target="tpu_custom_call" | custom-call | tf_op jit(solution)/shard_map/pallas_call | solution.py:75
  24.1 0.0 all-to-all-done
  24.1 10.9 %all-to-all-start.1 = ((bf16[128,320,128]{2,1,0:T(8,128)(2,1)}), bf16[128,320,128]{2,1,0:T(8,128)(2,1)}, u32[]{:S(2)}, u32[]{:S(2)}) async-start(bf16[128,320,128]{2,1,0:T(8,128)(2,1)} %bitcast.17), calls=%async_computation.1 | async-start | bytes 20971520 | tf_op jit(solution)/shard_map/all_to_all | solution.py:191
  35.0 0.1 add.93
  35.1 1.1 fusion.14
  36.2 2.0 %fusion.12 = (f32[64,2048]{1,0:T(8,128)S(1)}, f32[64,2048]{1,0:T(8,128)S(1)}) fusion(s32[2048]{0:T(1024)S(1)} %add_select_fusion.2), kind=kLoop, calls=%fused_computation.23 | loop fusion | flops 1835008 | bytes 1056768 | tf_op jit(solution)/shard_map/cos | solution.py:28
  38.3 7.0 %multiply_subtract_fusion = (f32[32,64,2048]{2,1,0:T(8,128)S(1)}, f32[32,64,2048]{2,1,0:T(8,128)}) fusion(f32[64,2048]{1,0:T(8,128)S(1)} %get-tuple-element.12, f32[32,2048]{1,0:T(8,128)S(1)} %get-tuple-element.10, f32[64,2048]{1,0:T(8,128)S(1)} %get-tuple-element.11, f32[32,2048]{1,0:T(8,128)S(1)} %get-tuple-element.9), kind=kLoop, calls=%fused_computation.4 | loop fusion | flops 25165824 | bytes 35127296 | tf_op jit(solution)/shard_map/sub | solution.py:30
  45.3 10.9 %fusion.1.refs_32_ = bf16[2048,2048]{1,0:T(8,128)(2,1)} fusion(f32[32,64,2048]{2,1,0:T(8,128)} %get-tuple-element.8, f32[32,64,2048]{2,1,0:T(8,128)S(1)} %get-tuple-element.7, pred[2048]{0:T(1024)(128)(4,1)S(1)} %iota_compare_fusion.3), kind=kLoop, calls=%fused_computation.2 | loop fusion | flops 12582912 | bytes 41945088 | tf_op jit(solution)/shard_map/convert_element_type | solution.py:32
  56.3 0.2 copy.21
  56.4 0.1 copy.22
  56.5 0.2 select_reduce_fusion
  56.7 0.1 reduce_sum.41
  56.8 115.7 %all-to-all-done.1 = bf16[128,320,128]{2,1,0:T(8,128)(2,1)} async-done(((bf16[128,320,128]{2,1,0:T(8,128)(2,1)}), bf16[128,320,128]{2,1,0:T(8,128)(2,1)}, u32[]{:S(2)}, u32[]{:S(2)}) %all-to-all-start.1) | async-done | bytes 10485792 | tf_op jit(solution)/shard_map/all_to_all | solution.py:191
  172.5 27.3 %shard_map.56 = f32[1280,2048]{1,0:T(8,128)} custom-call(s32[256]{0:T(256)S(1)} %get-tuple-element.14.row_ref, s32[256]{0:T(256)S(1)} %get-tuple-element.13.half_ref, ...), custom_call_target="tpu_custom_call" | custom-call | tf_op jit(solution)/shard_map/pallas_call | solution.py:147
  (6 shorter events, 0.0 us)
Async XLA Ops:
  3.0 21.1 %all-to-all-start = ((s32[128,1,4]{2,1,0:T(1,128)}), s32[128,1,4]{2,1,0:T(1,128)S(1)}, u32[]{:S(2)}, u32[]{:S(2)}) async-start(s32[128,1,4]{2,1,0:T(1,128)} %bitcast), calls=%async_computation | async-start | bytes 131072 | tf_op jit(solution)/shard_map/all_to_all | solution.py:192
  24.1 148.5 %all-to-all-start.1 = ((bf16[128,320,128]{2,1,0:T(8,128)(2,1)}), bf16[128,320,128]{2,1,0:T(8,128)(2,1)}, u32[]{:S(2)}, u32[]{:S(2)}) async-start(bf16[128,320,128]{2,1,0:T(8,128)(2,1)} %bitcast.17), calls=%async_computation.1 | async-start | bytes 20971520 | tf_op jit(solution)/shard_map/all_to_all | solution.py:191

commit v19 on v15

--- a/solution.py
+++ b/solution.py
@@ -124,7 +124,7 @@
     _, fields, sliver, lanes = landed.shape
     depth = per_plane * lanes // 2
     length = basis.shape[1]
-    width = 512
+    width = 256
     chunks = length // width
 
     def piece_map(position, group):

time: 200 us -> 203 us (1.015)
  Pallas kernels: 37.9 us -> 40 us
    pallas_call x1, Pallas kernels: 27.4 us -> 30.1 us  [spectra_from(): pl.pallas_call(functools.partial(spectra_kernel, groups, per_plane), out_...]
where the time goes in v19:
time: 203 us; the launch traced here: 202 us
  waiting for transfers between devices  115 us (57%)
  Pallas kernels  40 us (20%)
  other arithmetic  23.6 us (12%)
  starting transfers between devices  22 us (11%)
    all_to_all x1, waiting for transfers between devices, local(): lax.all_to_all(outbox, ('tile', 'phi'), split_axis=0, concat_axis=0, tile...  115 us
    pallas_call x1, Pallas kernels, spectra_from(): pl.pallas_call(functools.partial(spectra_kernel, groups, per_plane), out_...  30.1 us
    all_to_all x1, starting transfers between devices, local(): lax.all_to_all(outbox, ('tile', 'phi'), split_axis=0, concat_axis=0, tile...  11.8 us
    convert_element_type x1, other arithmetic, dft_basis(): return values.reshape(length, length).astype(jnp.bfloat16)  10.9 us
    all_to_all x1, starting transfers between devices, local(): lax.all_to_all(code_out, ('tile', 'phi'), split_axis=0, concat_axis=0, ti...  10.2 us
    pallas_call x1, Pallas kernels, pack_outbox(): pl.pallas_call(pack_kernel, out_shape=jax.ShapeDtypeStruct((tile_count, p...  9.96 us
    sub x1, other arithmetic, dft_basis(): values = jnp.where(is_cos, ch * cl - sh * sl, sh * cl + ch * sl)  7.03 us
  transfers between devices with their start and end apart: 2, of which 1 were waited for; matrix products, arithmetic and copies ran while one was open for 11% of the time, Pallas kernels for 5%

profile of v19, /device:TPU:97, one launch (start us, length us, event | category | flops | bytes accessed | tf_op | source)
XLA Modules:
  0.0 201.8 jit_solution(1354661336083065965)
XLA Ops:
  0.0 0.9 convert_reduce_fusion
  0.9 0.7 add_add_fusion
  1.6 0.6 select_reduce_fusion.1
  2.2 0.1 sub.27
  2.3 0.6 broadcast_in_dim.7.clone
  3.0 10.2 %all-to-all-start = ((s32[128,1,4]{2,1,0:T(1,128)}), s32[128,1,4]{2,1,0:T(1,128)S(1)}, u32[]{:S(2)}, u32[]{:S(2)}) async-start(s32[128,1,4]{2,1,0:T(1,128)} %bitcast), calls=%async_computation | async-start | bytes 131072 | tf_op jit(solution)/shard_map/all_to_all | solution.py:192
  13.1 10.0 %shard_map.55 = bf16[16,8,2,5,32,128]{5,4,3,2,1,0:T(8,128)(2,1)} custom-call(s32[64]{0:T(128)} %get-tuple-element.5.source_ref, s32[32]{0:T(128)} %level_ref.1, bf16[32,5,64,256]{3,2,1,0:T(8,128)(2,1)} %refs_15_.1, bf16[32,5,64,256]{3,2,1,0:T(8,128)(2,1)} %refs_15_.1, bf16[32,5,64,256]{3,2,1,0:T(8,128)(2,1)} %refs_15_.1, bf16[32,5,64,256]{3,2,1,0:T(8,128)(2,1)} %refs_15_.1, ...), custom_call_target="tpu_custom_call" | custom-call | tf_op jit(solution)/shard_map/pallas_call | solution.py:75
  23.1 0.0 all-to-all-done
  23.1 11.8 %all-to-all-start.1 = ((bf16[128,320,128]{2,1,0:T(8,128)(2,1)}), bf16[128,320,128]{2,1,0:T(8,128)(2,1)}, u32[]{:S(2)}, u32[]{:S(2)}) async-start(bf16[128,320,128]{2,1,0:T(8,128)(2,1)} %bitcast.17), calls=%async_computation.1 | async-start | bytes 20971520 | tf_op jit(solution)/shard_map/all_to_all | solution.py:191
  34.9 0.1 add.93
  35.0 1.1 fusion.14
  36.1 2.0 %fusion.12 = (f32[64,2048]{1,0:T(8,128)S(1)}, f32[64,2048]{1,0:T(8,128)S(1)}) fusion(s32[2048]{0:T(1024)S(1)} %add_select_fusion.2), kind=kLoop, calls=%fused_computation.23 | loop fusion | flops 1835008 | bytes 1056768 | tf_op jit(solution)/shard_map/cos | solution.py:28
  38.2 7.0 %multiply_subtract_fusion = (f32[32,64,2048]{2,1,0:T(8,128)S(1)}, f32[32,64,2048]{2,1,0:T(8,128)}) fusion(f32[64,2048]{1,0:T(8,128)S(1)} %get-tuple-element.12, f32[32,2048]{1,0:T(8,128)S(1)} %get-tuple-element.10, f32[64,2048]{1,0:T(8,128)S(1)} %get-tuple-element.11, f32[32,2048]{1,0:T(8,128)S(1)} %get-tuple-element.9), kind=kLoop, calls=%fused_computation.4 | loop fusion | flops 25165824 | bytes 35127296 | tf_op jit(solution)/shard_map/sub | solution.py:30
  45.2 10.9 %fusion.1.refs_32_ = bf16[2048,2048]{1,0:T(8,128)(2,1)} fusion(f32[32,64,2048]{2,1,0:T(8,128)} %get-tuple-element.8, f32[32,64,2048]{2,1,0:T(8,128)S(1)} %get-tuple-element.7, pred[2048]{0:T(1024)(128)(4,1)S(1)} %iota_compare_fusion.3), kind=kLoop, calls=%fused_computation.2 | loop fusion | flops 12582912 | bytes 41945088 | tf_op jit(solution)/shard_map/convert_element_type | solution.py:32
  56.2 0.2 copy.21
  56.3 0.1 copy.22
  56.4 0.2 select_reduce_fusion
  56.6 0.1 reduce_sum.41
  56.7 115.0 %all-to-all-done.1 = bf16[128,320,128]{2,1,0:T(8,128)(2,1)} async-done(((bf16[128,320,128]{2,1,0:T(8,128)(2,1)}), bf16[128,320,128]{2,1,0:T(8,128)(2,1)}, u32[]{:S(2)}, u32[]{:S(2)}) %all-to-all-start.1) | async-done | bytes 10485792 | tf_op jit(solution)/shard_map/all_to_all | solution.py:191
  171.7 30.1 %shard_map.56 = f32[1280,2048]{1,0:T(8,128)} custom-call(s32[256]{0:T(256)S(1)} %get-tuple-element.14.row_ref, s32[256]{0:T(256)S(1)} %get-tuple-element.13.half_ref, ...), custom_call_target="tpu_custom_call" | custom-call | tf_op jit(solution)/shard_map/pallas_call | solution.py:147
  (6 shorter events, 0.0 us)
Async XLA Ops:
  3.0 20.1 %all-to-all-start = ((s32[128,1,4]{2,1,0:T(1,128)}), s32[128,1,4]{2,1,0:T(1,128)S(1)}, u32[]{:S(2)}, u32[]{:S(2)}) async-start(s32[128,1,4]{2,1,0:T(1,128)} %bitcast), calls=%async_computation | async-start | bytes 131072 | tf_op jit(solution)/shard_map/all_to_all | solution.py:192
  23.1 148.6 %all-to-all-start.1 = ((bf16[128,320,128]{2,1,0:T(8,128)(2,1)}), bf16[128,320,128]{2,1,0:T(8,128)(2,1)}, u32[]{:S(2)}, u32[]{:S(2)}) async-start(bf16[128,320,128]{2,1,0:T(8,128)(2,1)} %bitcast.17), calls=%async_computation.1 | async-start | bytes 20971520 | tf_op jit(solution)/shard_map/all_to_all | solution.py:191

commit v20 on v19

--- a/solution.py
+++ b/solution.py
@@ -124,7 +124,7 @@
     _, fields, sliver, lanes = landed.shape
     depth = per_plane * lanes // 2
     length = basis.shape[1]
-    width = 256
+    width = 1024
     chunks = length // width
 
     def piece_map(position, group):

time: 203 us -> 200 us (0.985)
    pallas_call x1, Pallas kernels: 30.1 us -> 27.3 us  [spectra_from(): pl.pallas_call(functools.partial(spectra_kernel, groups, per_plane), out_...]
  transfers between devices with their start and end apart: 2 -> 2, of which waited for: 1 -> 1; matrix products, arithmetic and copies ran while one was open for 11% -> 11% of each run, Pallas kernels for 5% -> 6%
where the time goes in v20:
time: 200 us
  waiting for transfers between devices  116 us (58%)
  Pallas kernels  38.4 us (19%)
  other arithmetic  23.6 us (12%)
  starting transfers between devices  20.6 us (10%)
    all_to_all x1, waiting for transfers between devices, local(): lax.all_to_all(outbox, ('tile', 'phi'), split_axis=0, concat_axis=0, tile...  116 us
    pallas_call x1, Pallas kernels, spectra_from(): pl.pallas_call(functools.partial(spectra_kernel, groups, per_plane), out_...  27.3 us
    pallas_call x1, Pallas kernels, pack_outbox(): pl.pallas_call(pack_kernel, out_shape=jax.ShapeDtypeStruct((tile_count, p...  11.1 us
    convert_element_type x1, other arithmetic, dft_basis(): return values.reshape(length, length).astype(jnp.bfloat16)  10.9 us
    all_to_all x1, starting transfers between devices, local(): lax.all_to_all(outbox, ('tile', 'phi'), split_axis=0, concat_axis=0, tile...  10.5 us
    all_to_all x1, starting transfers between devices, local(): lax.all_to_all(code_out, ('tile', 'phi'), split_axis=0, concat_axis=0, ti...  10.2 us
    sub x1, other arithmetic, dft_basis(): values = jnp.where(is_cos, ch * cl - sh * sl, sh * cl + ch * sl)  7.03 us
  transfers between devices with their start and end apart: 2, of which 1 were waited for; matrix products, arithmetic and copies ran while one was open for 11% of the time, Pallas kernels for 6%

profile of v20, /device:TPU:97, one launch (start us, length us, event | category | flops | bytes accessed | tf_op | source)
XLA Modules:
  0.0 199.7 jit_solution(16931621575251466635)
XLA Ops:
  0.0 0.9 convert_reduce_fusion
  0.9 0.7 add_add_fusion
  1.6 0.6 select_reduce_fusion.1
  2.2 0.1 sub.27
  2.3 0.6 broadcast_in_dim.7.clone
  3.0 10.2 %all-to-all-start = ((s32[128,1,4]{2,1,0:T(1,128)}), s32[128,1,4]{2,1,0:T(1,128)S(1)}, u32[]{:S(2)}, u32[]{:S(2)}) async-start(s32[128,1,4]{2,1,0:T(1,128)} %bitcast), calls=%async_computation | async-start | bytes 131072 | tf_op jit(solution)/shard_map/all_to_all | solution.py:192
  13.1 11.1 %shard_map.55 = bf16[16,8,2,5,32,128]{5,4,3,2,1,0:T(8,128)(2,1)} custom-call(s32[64]{0:T(128)} %get-tuple-element.5.source_ref, s32[32]{0:T(128)} %level_ref.1, bf16[32,5,64,256]{3,2,1,0:T(8,128)(2,1)} %refs_15_.1, bf16[32,5,64,256]{3,2,1,0:T(8,128)(2,1)} %refs_15_.1, bf16[32,5,64,256]{3,2,1,0:T(8,128)(2,1)} %refs_15_.1, bf16[32,5,64,256]{3,2,1,0:T(8,128)(2,1)} %refs_15_.1, ...), custom_call_target="tpu_custom_call" | custom-call | tf_op jit(solution)/shard_map/pallas_call | solution.py:75
  24.3 0.0 all-to-all-done
  24.3 10.5 %all-to-all-start.1 = ((bf16[128,320,128]{2,1,0:T(8,128)(2,1)}), bf16[128,320,128]{2,1,0:T(8,128)(2,1)}, u32[]{:S(2)}, u32[]{:S(2)}) async-start(bf16[128,320,128]{2,1,0:T(8,128)(2,1)} %bitcast.17), calls=%async_computation.1 | async-start | bytes 20971520 | tf_op jit(solution)/shard_map/all_to_all | solution.py:191
  34.8 0.1 add.93
  34.9 1.1 fusion.14
  36.0 2.0 %fusion.12 = (f32[64,2048]{1,0:T(8,128)S(1)}, f32[64,2048]{1,0:T(8,128)S(1)}) fusion(s32[2048]{0:T(1024)S(1)} %add_select_fusion.2), kind=kLoop, calls=%fused_computation.23 | loop fusion | flops 1835008 | bytes 1056768 | tf_op jit(solution)/shard_map/cos | solution.py:28
  38.0 7.0 %multiply_subtract_fusion = (f32[32,64,2048]{2,1,0:T(8,128)S(1)}, f32[32,64,2048]{2,1,0:T(8,128)}) fusion(f32[64,2048]{1,0:T(8,128)S(1)} %get-tuple-element.12, f32[32,2048]{1,0:T(8,128)S(1)} %get-tuple-element.10, f32[64,2048]{1,0:T(8,128)S(1)} %get-tuple-element.11, f32[32,2048]{1,0:T(8,128)S(1)} %get-tuple-element.9), kind=kLoop, calls=%fused_computation.4 | loop fusion | flops 25165824 | bytes 35127296 | tf_op jit(solution)/shard_map/sub | solution.py:30
  45.0 10.9 %fusion.1.refs_32_ = bf16[2048,2048]{1,0:T(8,128)(2,1)} fusion(f32[32,64,2048]{2,1,0:T(8,128)} %get-tuple-element.8, f32[32,64,2048]{2,1,0:T(8,128)S(1)} %get-tuple-element.7, pred[2048]{0:T(1024)(128)(4,1)S(1)} %iota_compare_fusion.3), kind=kLoop, calls=%fused_computation.2 | loop fusion | flops 12582912 | bytes 41945088 | tf_op jit(solution)/shard_map/convert_element_type | solution.py:32
  56.0 0.2 copy.21
  56.2 0.1 copy.22
  56.2 0.2 select_reduce_fusion
  56.4 0.1 reduce_sum.41
  56.6 115.7 %all-to-all-done.1 = bf16[128,320,128]{2,1,0:T(8,128)(2,1)} async-done(((bf16[128,320,128]{2,1,0:T(8,128)(2,1)}), bf16[128,320,128]{2,1,0:T(8,128)(2,1)}, u32[]{:S(2)}, u32[]{:S(2)}) %all-to-all-start.1) | async-done | bytes 10485792 | tf_op jit(solution)/shard_map/all_to_all | solution.py:191
  172.3 27.3 %shard_map.56 = f32[1280,2048]{1,0:T(8,128)} custom-call(s32[256]{0:T(256)S(1)} %get-tuple-element.14.row_ref, s32[256]{0:T(256)S(1)} %get-tuple-element.13.half_ref, ...), custom_call_target="tpu_custom_call" | custom-call | tf_op jit(solution)/shard_map/pallas_call | solution.py:147
  (6 shorter events, 0.0 us)
Async XLA Ops:
  3.0 21.3 %all-to-all-start = ((s32[128,1,4]{2,1,0:T(1,128)}), s32[128,1,4]{2,1,0:T(1,128)S(1)}, u32[]{:S(2)}, u32[]{:S(2)}) async-start(s32[128,1,4]{2,1,0:T(1,128)} %bitcast), calls=%async_computation | async-start | bytes 131072 | tf_op jit(solution)/shard_map/all_to_all | solution.py:192
  24.3 148.0 %all-to-all-start.1 = ((bf16[128,320,128]{2,1,0:T(8,128)(2,1)}), bf16[128,320,128]{2,1,0:T(8,128)(2,1)}, u32[]{:S(2)}, u32[]{:S(2)}) async-start(bf16[128,320,128]{2,1,0:T(8,128)(2,1)} %bitcast.17), calls=%async_computation.1 | async-start | bytes 20971520 | tf_op jit(solution)/shard_map/all_to_all | solution.py:191

commit v21 on v15

--- a/solution.py
+++ b/solution.py
@@ -179,16 +179,18 @@
     match = (send_slot[None, :] == slot_ids[:, None]).astype(jnp.int32)
     source = jnp.sum(match * block_ids[None, :], axis=1)
     place = block_phi * CG_DEV + block_group
-    code = jnp.sum(match * (place[None, :] + 1), axis=1) - 1
     device_count = tile_count * plane_count
     pairs = capacity // 2
 
     outbox = pack_outbox(blocks, source, levels, tile_count, capacity, plane_count)
     outbox = outbox.reshape(device_count, pairs * fields * sliver, 2 * BPHI)
-    code_out = jnp.broadcast_to(
-        code.reshape(tile_count, 1, capacity), (tile_count, plane_count, capacity)
-    ).reshape(device_count, capacity)
     arrived = lax.all_to_all(outbox, ("tile", "phi"), split_axis=0, concat_axis=0, tiled=True)
+    dest_slot = (
+        lax.broadcasted_iota(jnp.int32, (tile_count, plane_count, capacity), 0) * capacity
+        + lax.broadcasted_iota(jnp.int32, (tile_count, plane_count, capacity), 2)
+    )
+    match_out = (send_slot == dest_slot[..., None]).astype(jnp.int32)
+    code_out = (jnp.sum(match_out * (place + 1), axis=3) - 1).reshape(device_count, capacity)
     arrived_code = lax.all_to_all(code_out, ("tile", "phi"), split_axis=0, concat_axis=0, tiled=True)
 
     by_segment = jnp.transpose(

time: 200 us -> 202 us (1.010)
  no operation moved by 1% of the time
where the time goes in v21:
time: 202 us; the launch traced here: 201 us
  waiting for transfers between devices  116 us (57%)
  Pallas kernels  37.9 us (19%)
  other arithmetic  25 us (12%)
  starting transfers between devices  20.7 us (10%)
    all_to_all x1, waiting for transfers between devices, local(): lax.all_to_all(outbox, ('tile', 'phi'), split_axis=0, concat_axis=0, tile...  116 us
    pallas_call x1, Pallas kernels, spectra_from(): pl.pallas_call(functools.partial(spectra_kernel, groups, per_plane), out_...  27.2 us
    convert_element_type x1, other arithmetic, dft_basis(): return values.reshape(length, length).astype(jnp.bfloat16)  10.9 us
    pallas_call x1, Pallas kernels, pack_outbox(): pl.pallas_call(pack_kernel, out_shape=jax.ShapeDtypeStruct((tile_count, p...  10.8 us
    all_to_all x1, starting transfers between devices, local(): lax.all_to_all(outbox, ('tile', 'phi'), split_axis=0, concat_axis=0, tile...  10.6 us
    all_to_all x1, starting transfers between devices, local(): lax.all_to_all(code_out, ('tile', 'phi'), split_axis=0, concat_axis=0, ti...  10.2 us
    sub x1, other arithmetic, dft_basis(): values = jnp.where(is_cos, ch * cl - sh * sl, sh * cl + ch * sl)  7.03 us
  transfers between devices with their start and end apart: 2, of which 1 were waited for; matrix products, arithmetic and copies ran while one was open for 11% of the time, Pallas kernels for 5%

profile of v21, /device:TPU:97, one launch (start us, length us, event | category | flops | bytes accessed | tf_op | source)
XLA Modules:
  0.0 200.8 jit_solution(8688061879613505389)
XLA Ops:
  0.0 0.9 convert_reduce_fusion
  0.9 0.1 iota_add_fusion
  1.0 0.7 add_add_fusion
  1.7 1.3 select_reduce_fusion
  3.0 0.1 copy.20
  3.1 0.8 copy.26
  3.8 10.2 %all-to-all-start = ((s32[128,1,4]{2,1,0:T(1,128)}), s32[128,1,4]{2,1,0:T(1,128)S(1)}, u32[]{:S(2)}, u32[]{:S(2)}) async-start(s32[128,1,4]{2,1,0:T(1,128)} %bitcast), calls=%async_computation | async-start | bytes 131072 | tf_op jit(solution)/shard_map/all_to_all | solution.py:194
  14.0 0.6 select_reduce_fusion.2.source_ref
  14.6 10.8 %shard_map.55 = bf16[16,8,2,5,32,128]{5,4,3,2,1,0:T(8,128)(2,1)} custom-call(s32[64]{0:T(128)} %select_reduce_fusion.2.source_ref, s32[32]{0:T(128)} %level_ref.1, bf16[32,5,64,256]{3,2,1,0:T(8,128)(2,1)} %refs_15_.1, bf16[32,5,64,256]{3,2,1,0:T(8,128)(2,1)} %refs_15_.1, bf16[32,5,64,256]{3,2,1,0:T(8,128)(2,1)} %refs_15_.1, ...), custom_call_target="tpu_custom_call" | custom-call | tf_op jit(solution)/shard_map/pallas_call | solution.py:75
  25.4 0.0 all-to-all-done
  25.4 10.6 %all-to-all-start.1 = ((bf16[128,320,128]{2,1,0:T(8,128)(2,1)}), bf16[128,320,128]{2,1,0:T(8,128)(2,1)}, u32[]{:S(2)}, u32[]{:S(2)}) async-start(bf16[128,320,128]{2,1,0:T(8,128)(2,1)} %bitcast.17), calls=%async_computation.1 | async-start | bytes 20971520 | tf_op jit(solution)/shard_map/all_to_all | solution.py:187
  36.0 0.1 add.104
  36.1 1.1 fusion.14
  37.2 2.0 %fusion.12 = (f32[64,2048]{1,0:T(8,128)S(1)}, f32[64,2048]{1,0:T(8,128)S(1)}) fusion(s32[2048]{0:T(1024)S(1)} %add_select_fusion.2), kind=kLoop, calls=%fused_computation.23 | loop fusion | flops 1835008 | bytes 1056768 | tf_op jit(solution)/shard_map/cos | solution.py:28
  39.2 7.0 %multiply_subtract_fusion = (f32[32,64,2048]{2,1,0:T(8,128)S(1)}, f32[32,64,2048]{2,1,0:T(8,128)}) fusion(f32[64,2048]{1,0:T(8,128)S(1)} %get-tuple-element.10, f32[32,2048]{1,0:T(8,128)S(1)} %get-tuple-element.8, f32[64,2048]{1,0:T(8,128)S(1)} %get-tuple-element.9, f32[32,2048]{1,0:T(8,128)S(1)} %get-tuple-element.7), kind=kLoop, calls=%fused_computation.4 | loop fusion | flops 25165824 | bytes 35127296 | tf_op jit(solution)/shard_map/sub | solution.py:30
  46.3 10.9 %fusion.1.refs_32_ = bf16[2048,2048]{1,0:T(8,128)(2,1)} fusion(f32[32,64,2048]{2,1,0:T(8,128)} %get-tuple-element.6, f32[32,64,2048]{2,1,0:T(8,128)S(1)} %get-tuple-element.5, pred[2048]{0:T(1024)(128)(4,1)S(1)} %iota_compare_fusion.3), kind=kLoop, calls=%fused_computation.2 | loop fusion | flops 12582912 | bytes 41945088 | tf_op jit(solution)/shard_map/convert_element_type | solution.py:32
  57.2 0.2 copy.24
  57.4 0.1 copy.25
  57.4 0.2 select_reduce_fusion.1
  57.7 0.1 reduce_sum.41
  57.8 115.7 %all-to-all-done.1 = bf16[128,320,128]{2,1,0:T(8,128)(2,1)} async-done(((bf16[128,320,128]{2,1,0:T(8,128)(2,1)}), bf16[128,320,128]{2,1,0:T(8,128)(2,1)}, u32[]{:S(2)}, u32[]{:S(2)}) %all-to-all-start.1) | async-done | bytes 10485792 | tf_op jit(solution)/shard_map/all_to_all | solution.py:187
  173.5 27.2 %shard_map.56 = f32[1280,2048]{1,0:T(8,128)} custom-call(s32[256]{0:T(256)S(1)} %get-tuple-element.12.row_ref, s32[256]{0:T(256)S(1)} %get-tuple-element.11.half_ref, ...), custom_call_target="tpu_custom_call" | custom-call | tf_op jit(solution)/shard_map/pallas_call | solution.py:147
  (7 shorter events, 0.1 us)
Async XLA Ops:
  3.8 21.6 %all-to-all-start = ((s32[128,1,4]{2,1,0:T(1,128)}), s32[128,1,4]{2,1,0:T(1,128)S(1)}, u32[]{:S(2)}, u32[]{:S(2)}) async-start(s32[128,1,4]{2,1,0:T(1,128)} %bitcast), calls=%async_computation | async-start | bytes 131072 | tf_op jit(solution)/shard_map/all_to_all | solution.py:194
  25.4 148.1 %all-to-all-start.1 = ((bf16[128,320,128]{2,1,0:T(8,128)(2,1)}), bf16[128,320,128]{2,1,0:T(8,128)(2,1)}, u32[]{:S(2)}, u32[]{:S(2)}) async-start(bf16[128,320,128]{2,1,0:T(8,128)(2,1)} %bitcast.17), calls=%async_computation.1 | async-start | bytes 20971520 | tf_op jit(solution)/shard_map/all_to_all | solution.py:187
